TPU v7x, 32 devices: a whole 2x2x4 slice. The times are simulated.
32 devices in a mesh: mp: 2 (over core), feat: 16 (over z, y, x).
Axes of the slice: x: 2, y: 2, z: 4, core: 2. Of those that a mesh axis runs over, the one named last changes fastest.
Arguments:
- residual: bfloat16 [2, 96, 2304], P(None, 'feat', 'mp'), may hold values from -6 to 6
- norm_gain: float32 [2, 2304], P(None, 'mp'), may hold values from 0.1 to 1.9
- gate_weight: bfloat16 [2, 2304, 9216], P(None, 'mp', 'feat'), may hold values from -0.125 to 0.125
- up_weight: bfloat16 [2, 2304, 9216], P(None, 'mp', 'feat'), may hold values from -0.125 to 0.125
- down_weight: bfloat16 [2, 9216, 2304], P(None, 'feat', 'mp'), may hold values from -0.0625 to 0.0625
- encoder: bfloat16 [2, 32768, 2304], P(None, 'feat', 'mp'), may hold values from -0.125 to 0.125
- encoder_bias: float32 [2, 32768], P(None, 'feat'), may hold values from -3 to 3
- decoder: bfloat16 [3, 32768, 2304], P(None, 'feat', 'mp'), may hold values from -0.03125 to 0.03125
Outputs:
- grad_encoder: bfloat16 [2, 32768, 2304], P(None, 'feat', 'mp')
- grad_bias: float32 [2, 32768], P(None, 'feat')
- grad_decoder: bfloat16 [3, 32768, 2304], P(None, 'feat', 'mp')
All inputs are finite; a program needn't handle non-finite values.
Results may differ from a plain program's by a relative error of at most 0.02.
The roundings to bfloat16 on the way count: a program that leaves them out, or rounds other values in their place, can miss the bound.
Values may be sent and summed in bfloat16 or wider, within the bound.
No kernel may reach another device: no remote copies, remote signals or barrier semaphores. Data moves between devices by JAX's collectives and lax.ppermute only.
A program may use at most 128 MiB of HBM per device.

v0:
```python
import math

import jax
import jax.numpy as jnp
from jax import lax
from jax.sharding import PartitionSpec as P

D = 2304


sparsity_weight = 0.1


def outer_product(weights_side, errors_side):
    return lax.dot_general(
        weights_side, errors_side, (((0,), (0,)), ((), ())), preferred_element_type=jnp.float32
    )


def body(residual, norm_gain, gate_weight, up_weight, down_weight, encoder, encoder_bias, decoder):
    values = residual.astype(jnp.float32)
    squares = lax.psum(jnp.sum(values * values, axis=2), "mp")
    inverse_rms = lax.rsqrt(squares / D + 1e-06)
    normed_local = (values * inverse_rms[:, :, None] * norm_gain[:, None, :]).astype(jnp.bfloat16)
    normed = lax.all_gather(normed_local, "feat", axis=1, tiled=True)
    tokens = normed.shape[1]
    local_rows = residual.shape[1]
    gate_part = jnp.einsum("ltd,ldh->lth", normed, gate_weight, preferred_element_type=jnp.float32)
    up_part = jnp.einsum("ltd,ldh->lth", normed, up_weight, preferred_element_type=jnp.float32)
    gate_part, up_part = (
        lax.psum(gate_part.astype(jnp.bfloat16), "mp").astype(jnp.float32),
        lax.psum(up_part.astype(jnp.bfloat16), "mp").astype(jnp.float32),
    )
    hidden = (jax.nn.gelu(gate_part, approximate=True) * up_part).astype(jnp.bfloat16)
    preact_part = jnp.einsum("ltd,lfd->tlf", normed, encoder, preferred_element_type=jnp.float32)
    preact = lax.psum(preact_part, "mp")
    active = jnp.maximum(preact + encoder_bias[None], 0.0).astype(jnp.bfloat16)
    features = active.shape[2]
    model_cols = decoder.shape[2]
    joined = jnp.concatenate([decoder[1], decoder[2]], axis=0)
    picked = hidden
    partial_value = jnp.einsum(
        "lth,lhd->tld", picked, down_weight, preferred_element_type=jnp.float32
    )
    picked = active
    first_part = jnp.dot(picked[:, 0], decoder[0], preferred_element_type=jnp.float32)
    second = jnp.dot(
        picked.reshape(local_rows * lax.axis_size("feat"), 2 * features),
        joined,
        preferred_element_type=jnp.float32,
    )
    errors_local = lax.psum_scatter(
        jnp.concatenate([first_part, second], axis=1)
        - partial_value.reshape(local_rows * lax.axis_size("feat"), -1),
        "feat",
        scatter_dimension=0,
        tiled=True,
    ).astype(jnp.bfloat16)
    errors = lax.all_gather(errors_local, "feat", axis=0, tiled=True)
    error_first = errors[:, :model_cols]
    error_second = errors[:, model_cols:]
    first_rows = jnp.concatenate([decoder[0], decoder[1]], axis=1)
    back_first = lax.dot_general(
        errors, first_rows, (((1,), (1,)), ((), ())), preferred_element_type=jnp.float32
    )
    back_second = lax.dot_general(
        error_second, decoder[2], (((1,), (1,)), ((), ())), preferred_element_type=jnp.float32
    )
    back_stack = jnp.stack([back_first, back_second], axis=1)
    loss_scale = 1.0 / math.sqrt(tokens)
    backward = lax.psum(back_stack.astype(jnp.bfloat16), "mp").astype(jnp.float32)
    pre_grad = jnp.where(active > 0, loss_scale * (backward + sparsity_weight), 0.0).astype(
        jnp.bfloat16
    )
    grad_encoder = jnp.einsum(
        "tlf,ltd->lfd", pre_grad, normed, preferred_element_type=jnp.float32
    ).astype(jnp.bfloat16)
    grad_bias = jnp.sum(pre_grad.astype(jnp.float32), axis=0)
    active_first = active[:, 0]
    active_second = active[:, 1]
    grad_decoder = (
        loss_scale
        * jnp.stack(
            [
                outer_product(active_first, error_first),
                outer_product(active_first, error_second),
                outer_product(active_second, error_second),
            ]
        )
    ).astype(jnp.bfloat16)
    return (grad_encoder, grad_bias, grad_decoder)


def solution(mesh):
    return jax.shard_map(
        body,
        mesh=mesh,
        in_specs=(
            P(None, "feat", "mp"),
            P(None, "mp"),
            P(None, "mp", "feat"),
            P(None, "mp", "feat"),
            P(None, "feat", "mp"),
            P(None, "feat", "mp"),
            P(None, "feat"),
            P(None, "feat", "mp"),
        ),
        out_specs=(P(None, "feat", "mp"), P(None, "feat"), P(None, "feat", "mp")),
        check_vma=False,
    )
```

profile of v0, /device:TPU:0, one launch (start us, length us, event | category | flops | bytes accessed | tf_op | source)
XLA Modules:
  0.0 270.2 jit_solution(11253927287694514613)
XLA Ops:
  7.2 1.0 fusion.38
  8.2 2.6 psum.35
  10.9 0.8 fusion.40
  11.7 44.8 %all_gather.6 = bf16[2,96,1152]{2,0,1:T(2,128)(2,1)S(1)} all-gather(bf16[2,6,1152]{2,0,1:T(2,128)(2,1)S(1)} %fusion.40), channel_id=1, replica_groups=mesh['mp'=2,'feat'=16] {'feat'}, dimensions={1}, use_global_device_ids=true | all-gather | bytes 470016 | tf_op jit(solution)/shard_map/all_gather | solution.py:25
  56.5 3.6 %convolution_convert_fusion.3 = bf16[2,96,576]{2,1,0:T(8,128)(2,1)} fusion(bf16[2,1152,576]{1,2,0:T(8,128)(2,1)} %param.10, bf16[2,96,1152]{2,0,1:T(2,128)(2,1)S(1)} %all_gather.6), kind=kOutput, calls=%fused_computation.27 | convolution fusion | flops 254914560 | bytes 3317760 | tf_op jit(solution)/shard_map/ltd,ldh->lth/dot_general | solution.py:28
  60.1 3.4 %convolution_convert_fusion.2 = bf16[2,96,576]{2,1,0:T(8,128)(2,1)} fusion(bf16[2,1152,576]{1,2,0:T(8,128)(2,1)} %param.11, bf16[2,96,1152]{2,0,1:T(2,128)(2,1)S(1)} %all_gather.6), kind=kOutput, calls=%fused_computation.26 | convolution fusion | flops 254914560 | bytes 3317760 | tf_op jit(solution)/shard_map/ltd,ldh->lth/dot_general | solution.py:29
  63.6 8.0 %convolution_bitcast_fusion.4 = f32[96,2,2048]{2,0,1:T(8,128)} fusion(bf16[2,2048,1152]{2,1,0:T(8,128)(2,1)} %param.13, bf16[2,96,1152]{2,0,1:T(2,128)(2,1)S(1)} %all_gather.6), kind=kOutput, calls=%fused_computation.18 | convolution fusion | flops 905969664 | bytes 11452416 | tf_op jit(solution)/shard_map/ltd,lfd->tlf/dot_general | solution.py:35
  71.7 11.3 %slice_bitcast_fusion.2 = (bf16[2048,1152]{1,0:T(8,128)(2,1)}, bf16[2048,1152]{1,0:T(8,128)(2,1)}, bf16[2048,1152]{1,0:T(8,128)(2,1)}) fusion(bf16[3,2048,1152]{2,1,0:T(8,128)(2,1)} %param.15), kind=kLoop, calls=%fused_computation.16 | loop fusion | bytes 28311552 | tf_op jit(solution)/shard_map/squeeze | solution.py:46
  83.0 1.7 convolution_bitcast_fusion.3
  84.8 17.4 %all-reduce.7.cloned.1.call-done = f32[96,2,2048]{2,0,1:T(8,128)} async-done(((f32[96,2,2048]{2,0,1:T(8,128)}), f32[96,2,2048]{2,0,1:T(8,128)}) %all-reduce.7.cloned.1.call-update) | async-done | bytes 1572880 | tf_op jit(solution)/shard_map/psum | solution.py:36
  102.1 1.7 maximum_convert_fusion
  103.9 3.7 %fusion.24 = f32[96,1152]{1,0:T(8,128)S(1)} fusion(bf16[96,2,2048]{2,0,1:T(8,128)(2,1)S(1)} %maximum_convert_fusion, bf16[3,2048,1152]{2,1,0:T(8,128)(2,1)} %param.15), kind=kOutput, calls=%fused_computation.43 | convolution fusion | flops 452984832 | bytes 5554176 | tf_op jit(solution)/shard_map/dot_general | solution.py:46
  107.9 0.6 copy-done.4
  108.5 2.0 fusion.2
  110.6 49.0 %fusion = f32[8,2304]{1,0:T(8,128)S(1)} fusion(f32[96,2304]{1,0:T(8,128)S(1)} %maximum_subtract_fusion), kind=kCustom, calls=%all-reduce-scatter | all-reduce-scatter fusion | flops 294913 | bytes 958976
  159.6 1.3 collective-permute-start.1
  160.9 1.3 collective-permute-start.2
  162.2 1.9 collective-permute-start
  164.1 2.4 collective-permute-start.3
  166.5 0.6 dynamic-slice.4
  167.8 0.4 collective-permute-done.3
  168.1 0.6 concatenate.12
  168.8 43.6 %all-gather = bf16[16,6,2304]{2,1,0:T(8,128)(2,1)S(1)} all-gather(bf16[1,6,2304]{2,1,0:T(8,128)(2,1)S(1)} %fusion.41), channel_id=1, replica_groups=mesh['mp'=2,'feat'=16] {'feat'}, dimensions={0}, use_global_device_ids=true | all-gather | bytes 470016 | tf_op jit(solution)/shard_map/all_gather | solution.py:59
  212.5 3.9 %fusion.16 = bf16[96,1,2048]{2,0,1:T(8,128)(2,1)S(1)} fusion(bf16[96,2304]{1,0:T(8,128)(2,1)S(1)} %reshape.18, bf16[3,2048,1152]{2,1,0:T(8,128)(2,1)} %param.15), kind=kOutput, calls=%fused_computation.22 | convolution fusion | flops 453181440 | bytes 5332992 | tf_op jit(solution)/shard_map/dot_general | solution.py:66
  216.4 5.1 %convolution_bitcast_fusion.1 = f32[1,2048,1152]{2,1,0:T(8,128)} fusion(bf16[96,2,2048]{2,0,1:T(8,128)(2,1)S(1)} %maximum_convert_fusion, bf16[96,2304]{1,0:T(8,128)(2,1)S(1)} %reshape.18), kind=kOutput, calls=%fused_computation.12 | convolution fusion | flops 452984832 | bytes 10051584 | tf_op jit(solution)/shard_map/dot_general | solution.py:15
  221.5 5.8 %convolution_bitcast_fusion = f32[1,2048,1152]{2,1,0:T(8,128)} fusion(bf16[96,2,2048]{2,0,1:T(8,128)(2,1)S(1)} %maximum_convert_fusion, bf16[96,2304]{1,0:T(8,128)(2,1)S(1)} %reshape.18), kind=kOutput, calls=%fused_computation.11 | convolution fusion | flops 452984832 | bytes 10051584 | tf_op jit(solution)/shard_map/dot_general | solution.py:15
  227.3 5.1 %convolution_bitcast_fusion.2 = f32[1,2048,1152]{2,1,0:T(8,128)} fusion(bf16[96,2,2048]{2,0,1:T(8,128)(2,1)S(1)} %maximum_convert_fusion, bf16[96,2304]{1,0:T(8,128)(2,1)S(1)} %reshape.18), kind=kOutput, calls=%fused_computation.13 | convolution fusion | flops 452984832 | bytes 10051584 | tf_op jit(solution)/shard_map/dot_general | solution.py:15
  232.4 3.1 %fusion.13 = bf16[96,1,2048]{2,0,1:T(8,128)(2,1)S(1)} fusion(bf16[96,2304]{1,0:T(8,128)(2,1)S(1)} %reshape.18, bf16[2048,1152]{1,0:T(8,128)(2,1)S(1)} %bitcast.51, bf16[2048,1152]{1,0:T(8,128)(2,1)S(1)} %bitcast.47), kind=kOutput, calls=%fused_computation.21 | convolution fusion | flops 925040640 | bytes 10272768 | tf_op jit(solution)/shard_map/dot_general | solution.py:63
  235.6 1.0 pad_maximum_fusion
  236.5 16.6 %fusion.1 = bf16[3,2048,1152]{2,1,0:T(8,128)(2,1)} fusion(f32[1,2048,1152]{2,1,0:T(8,128)} %convolution_bitcast_fusion, f32[1,2048,1152]{2,1,0:T(8,128)} %convolution_bitcast_fusion.1, f32[1,2048,1152]{2,1,0:T(8,128)} %convolution_bitcast_fusion.2), kind=kLoop, calls=%fused_computation.1 | loop fusion | flops 28311552 | bytes 42467328 | tf_op jit(solution)/shard_map/convert_element_type | solution.py:90
  253.2 2.8 %convert_reduce_fusion = f32[2,2048]{1,0:T(2,128)} fusion(bf16[96,2,2048]{2,0,1:T(8,128)(2,1)} %all-reduce.9.cloned.1.call-done, f32[96,2,2048]{2,0,1:T(8,128)} %all-reduce.7.cloned.1.call-done, f32[2,2048]{1,0:T(2,128)S(1)} %copy-done.5), kind=kLoop, calls=%fused_computation.23 | loop fusion | flops 4321280 | bytes 2392064 | tf_op jit(solution)/shard_map/reduce_sum | solution.py:78
  256.0 7.6 %convolution_convert_fusion = bf16[2,2048,1152]{2,1,0:T(8,128)(2,1)} fusion(bf16[2,96,1152]{2,0,1:T(2,128)(2,1)} %copy-done.3, bf16[96,2,2048]{2,0,1:T(8,128)(2,1)} %all-reduce.9.cloned.1.call-done, bf16[96,2,2048]{2,0,1:T(8,128)(2,1)S(1)} %maximum_convert_fusion), kind=kOutput, calls=%fused_computation.2 | convolution fusion | flops 913047552 | bytes 11452416 | tf_op jit(solution)/shard_map/tlf,ltd->lfd/dot_general | solution.py:75
  (48 shorter events, 0.9 us)
Async XLA Ops:
  7.2 75.8 %copy-start = (bf16[2,576,1152]{2,1,0:T(8,128)(2,1)S(1)}, bf16[2,576,1152]{2,1,0:T(8,128)(2,1)}, u32[]{:S(2)}) copy-start(bf16[2,576,1152]{2,1,0:T(8,128)(2,1)} %param.12) | copy-start | bytes 7962628
  7.2 75.8 %all-reduce.11.cloned.1.call-start = ((), (), s32[]{:S(2)}) async-start(), calls=%async_computation.2 | async-start | bytes 983040 | tf_op jit(solution)/shard_map/psum | solution.py:31
  56.5 15.0 %copy-start.3 = (bf16[2,96,1152]{2,0,1:T(2,128)(2,1)}, bf16[2,96,1152]{2,0,1:T(2,128)(2,1)S(1)}, u32[]{:S(2)}) copy-start(bf16[2,96,1152]{2,0,1:T(2,128)(2,1)S(1)} %all_gather.6) | copy-start | bytes 1327108
  63.5 38.6 %all-reduce.7.cloned.1.call-start = ((), (), s32[]{:S(2)}) async-start(), calls=%async_computation | async-start | bytes 3145728 | tf_op jit(solution)/shard_map/psum | solution.py:36
  71.6 181.6 %all-reduce.9.cloned.1.call-start = ((), (), s32[]{:S(2)}) async-start(), calls=%async_computation.1 | async-start | bytes 1572864 | tf_op jit(solution)/shard_map/psum | solution.py:71
  83.0 19.1 %copy-start.5 = (f32[2,2048]{1,0:T(2,128)S(1)}, f32[2,2048]{1,0:T(2,128)}, u32[]{:S(2)}) copy-start(f32[2,2048]{1,0:T(2,128)} %param.14) | copy-start | bytes 49156
  102.1 5.4 %copy-start.2 = (f32[96,2,2048]{2,0,1:T(8,128)S(1)}, f32[96,2,2048]{2,0,1:T(8,128)}, u32[]{:S(2)}) copy-start(f32[96,2,2048]{2,0,1:T(8,128)} %all-reduce.7.cloned.1.call-done) | copy-start | bytes 4718596
  102.1 5.7 %slice-start.2 = ((s8[4718592]{0:T(1024)(128)(4,1)}), s8[4194304]{0:T(1024)(128)(4,1)S(1)}, s32[]{:S(2)}) async-start(s8[4718592]{0:T(1024)(128)(4,1)} %bitcast.48), calls=%async_computation.5 | async-start | bytes 8388608
  103.9 4.0 %slice-start.3 = ((s8[4718592]{0:T(1024)(128)(4,1)}), s8[524288]{0:T(1024)(128)(4,1)S(1)}, s32[]{:S(2)}) async-start(s8[4718592]{0:T(1024)(128)(4,1)} %bitcast.48), calls=%async_computation.6 | async-start | bytes 1048576
  103.9 4.6 %copy-start.4 = (bf16[2048,1152]{1,0:T(8,128)(2,1)S(1)}, bf16[2048,1152]{1,0:T(8,128)(2,1)}, u32[]{:S(2)}) copy-start(bf16[2048,1152]{1,0:T(8,128)(2,1)} %get-tuple-element.6) | copy-start | bytes 14155780
  108.5 58.1 %copy-start.6 = (u32[32]{0:T(128)S(1)}, u32[32]{0:T(128)}, u32[]{:S(2)}) copy-start(u32[32]{0:T(128)} %constant.26) | copy-start | bytes 388
  159.6 8.5 %collective-permute-start.1 = (bf16[8,2304]{1,0:T(8,128)(2,1)S(1)}, bf16[8,2304]{1,0:T(8,128)(2,1)S(1)}, u32[]{:S(2)}, u32[]{:S(2)}) collective-permute-start(bf16[8,2304]{1,0:T(8,128)(2,1)S(1)} %convert.22), channel_id=1, source_target_pairs={{0,2},{1,3},{2,4},{3,5},{4,6},{5,7},{6,8},{7,9},{8,10},{9,11},{10,... | collective-permute-start | bytes 110600
  160.9 7.2 %collective-permute-start.2 = (bf16[8,2304]{1,0:T(8,128)(2,1)S(1)}, bf16[8,2304]{1,0:T(8,128)(2,1)S(1)}, u32[]{:S(2)}, u32[]{:S(2)}) collective-permute-start(bf16[8,2304]{1,0:T(8,128)(2,1)S(1)} %convert.22), channel_id=1, source_target_pairs={{0,3},{1,4},{2,5},{3,6},{4,7},{5,8},{6,9},{7,10},{8,11},{9,12},{10... | collective-permute-start | bytes 110600
  162.2 5.9 %collective-permute-start = (bf16[8,2304]{1,0:T(8,128)(2,1)S(1)}, bf16[8,2304]{1,0:T(8,128)(2,1)S(1)}, u32[]{:S(2)}, u32[]{:S(2)}) collective-permute-start(bf16[8,2304]{1,0:T(8,128)(2,1)S(1)} %convert.22), channel_id=1, source_target_pairs={{0,1},{1,2},{2,3},{3,4},{4,5},{5,6},{6,7},{7,8},{8,9},{9,10},{10,1... | collective-permute-start | bytes 110600
  164.1 4.0 %collective-permute-start.3 = (bf16[6,2304]{1,0:T(8,128)(2,1)S(1)}, bf16[6,2304]{1,0:T(8,128)(2,1)S(1)}, u32[]{:S(2)}, u32[]{:S(2)}) collective-permute-start(bf16[6,2304]{1,0:T(8,128)(2,1)S(1)} %slice.36), channel_id=1, source_target_pairs={{0,4},{1,5},{2,6},{3,7},{4,8},{5,9},{6,10},{7,11},{8,12},{9,13},{1... | collective-permute-start | bytes 82952
  221.5 10.9 %slice-start = ((s8[4718592]{0:T(1024)(128)(4,1)}), s8[4194304]{0:T(1024)(128)(4,1)S(1)}, s32[]{:S(2)}) async-start(s8[4718592]{0:T(1024)(128)(4,1)} %bitcast.46), calls=%async_computation.3 | async-start | bytes 8388608
  221.5 10.9 %slice-start.4 = ((s8[4718592]{0:T(1024)(128)(4,1)}), s8[4194304]{0:T(1024)(128)(4,1)S(1)}, s32[]{:S(2)}) async-start(s8[4718592]{0:T(1024)(128)(4,1)} %bitcast.50), calls=%async_computation.7 | async-start | bytes 8388608
  227.3 5.1 %slice-start.1 = ((s8[4718592]{0:T(1024)(128)(4,1)}), s8[524288]{0:T(1024)(128)(4,1)S(1)}, s32[]{:S(2)}) async-start(s8[4718592]{0:T(1024)(128)(4,1)} %bitcast.46), calls=%async_computation.4 | async-start | bytes 1048576
  227.3 5.1 %slice-start.5 = ((s8[4718592]{0:T(1024)(128)(4,1)}), s8[524288]{0:T(1024)(128)(4,1)S(1)}, s32[]{:S(2)}) async-start(s8[4718592]{0:T(1024)(128)(4,1)} %bitcast.50), calls=%async_computation.8 | async-start | bytes 1048576
  253.2 10.5 %copy-start.1 = (bf16[2,576,1152]{2,1,0:T(8,128)(2,1)S(1)}, bf16[2,576,1152]{2,1,0:T(8,128)(2,1)}, u32[]{:S(2)}) copy-start(bf16[2,576,1152]{2,1,0:T(8,128)(2,1)} %param.12) | copy-start | bytes 7962628
Sparse Core Ops, SparseCore 0:
  63.6 14.4 all-reduce.10
  80.5 21.5 all-reduce.6
  236.7 14.8 all-reduce.8
where the time goes:
time: 271 us; the launch traced here: 270 us
  blocking collectives  140 us (52%)
  matrix products  53 us (20%)
  other arithmetic  24.3 us (9%)
  waiting for transfers between devices  17.8 us (7%)
  between operations  14.6 us (5%)
  local copies, waits for them, and re-layouts  13.5 us (5%)
  starting transfers between devices  6.99 us (3%)
    unnamed x1, blocking collectives  49 us
    all_gather x1, blocking collectives, body(): normed = lax.all_gather(normed_local, 'feat', axis=1, tiled=True)  44.8 us
    all_gather x1, blocking collectives, body(): errors = lax.all_gather(errors_local, 'feat', axis=0, tiled=True)  43.6 us
    psum x1, waiting for transfers between devices, body(): preact = lax.psum(preact_part, 'mp')  17.4 us
    convert_element_type x1, other arithmetic, body(): grad_decoder = (loss_scale * jnp.stack([outer_product(active_first, error...  16.6 us
    dot_general x3, matrix products, outer_product(): lax.dot_general(weights_side, errors_side, (((0,), (0,)), ((), ())), pref...  15.9 us
    squeeze x1, local copies, waits for them, and re-layouts, body(): decoder[0]  11.3 us
    dot_general x1, matrix products, body(): jnp.einsum('ltd,lfd->tlf', normed, encoder, preferred_element_type=jnp.fl...  8.01 us
  transfers between devices with their start and end apart: 7, of which 2 were waited for; matrix products, arithmetic and copies ran while one was open for 14% of the time, Pallas kernels for 0%

commit v1 on v0

v1 whole, which is shorter than its diff:
```python
import math

import jax
import jax.numpy as jnp
from jax import lax
from jax.sharding import PartitionSpec as P

D = 2304


sparsity_weight = 0.1


def swap(values, axis, bit):
    size = lax.axis_size(axis)
    return lax.ppermute(values, axis, [(i, i ^ bit) for i in range(size)])


def bits_of(axis):
    size = lax.axis_size(axis)
    return [1 << k for k in range(size.bit_length() - 1)]


def mp_sum(values, wire=None):
    for bit in bits_of("mp"):
        sent = values if wire is None else values.astype(wire)
        values = values + swap(sent, "mp", bit).astype(values.dtype)
    return values


def gather_tokens(values, dim):
    for bit in reversed(bits_of("feat")):
        values = jnp.concatenate([values, swap(values, "feat", bit)], axis=dim)
    return values


def scatter_tokens(values):
    for bit in bits_of("feat"):
        half = values.shape[0] // 2
        values = values[:half] + swap(values[half:].astype(jnp.bfloat16), "feat", bit).astype(jnp.float32)
    return values


def dot(a, b, contract):
    return lax.dot_general(a, b, (contract, ((), ())), preferred_element_type=jnp.float32)


def body(residual, norm_gain, gate_weight, up_weight, down_weight, encoder, encoder_bias, decoder):
    values = residual.astype(jnp.float32)
    squares = mp_sum(jnp.sum(values * values, axis=2))
    inverse_rms = lax.rsqrt(squares / D + 1e-06)
    normed_local = (values * inverse_rms[:, :, None] * norm_gain[:, None, :]).astype(jnp.bfloat16)
    normed = gather_tokens(normed_local, 1)
    tokens = normed.shape[1]
    gate_part = jnp.einsum("ltd,ldh->lth", normed, gate_weight, preferred_element_type=jnp.float32)
    up_part = jnp.einsum("ltd,ldh->lth", normed, up_weight, preferred_element_type=jnp.float32)
    mlp_part = mp_sum(jnp.stack([gate_part, up_part]).astype(jnp.bfloat16)).astype(jnp.float32)
    hidden = (jax.nn.gelu(mlp_part[0], approximate=True) * mlp_part[1]).astype(jnp.bfloat16)
    preact = mp_sum(
        jnp.einsum("ltd,lfd->ltf", normed, encoder, preferred_element_type=jnp.float32)
    )
    active = jnp.maximum(preact + encoder_bias[:, None, :], 0.0).astype(jnp.bfloat16)
    target = jnp.einsum("lth,lhd->ltd", hidden, down_weight, preferred_element_type=jnp.float32)
    model_cols = decoder.shape[2]
    nn = ((1,), (0,))
    nt = ((1,), (1,))
    first = dot(active[0], decoder[0], nn) - target[0]
    second = dot(active[0], decoder[1], nn) + dot(active[1], decoder[2], nn) - target[1]
    errors_local = scatter_tokens(jnp.concatenate([first, second], axis=1)).astype(jnp.bfloat16)
    errors = gather_tokens(errors_local, 0)
    error_first = errors[:, :model_cols]
    error_second = errors[:, model_cols:]
    back_first = dot(error_first, decoder[0], nt) + dot(error_second, decoder[1], nt)
    back_second = dot(error_second, decoder[2], nt)
    loss_scale = 1.0 / math.sqrt(tokens)
    backward = mp_sum(jnp.stack([back_first, back_second]).astype(jnp.bfloat16)).astype(jnp.float32)
    pre_grad = jnp.where(active > 0, loss_scale * (backward + sparsity_weight), 0.0).astype(
        jnp.bfloat16
    )
    grad_encoder = jnp.einsum(
        "ltf,ltd->lfd", pre_grad, normed, preferred_element_type=jnp.float32
    ).astype(jnp.bfloat16)
    grad_bias = jnp.sum(pre_grad.astype(jnp.float32), axis=1)
    grad_decoder = (
        loss_scale
        * jnp.einsum(
            "ltf,ltd->lfd",
            jnp.stack([active[0], active[0], active[1]]),
            jnp.stack([error_first, error_second, error_second]),
            preferred_element_type=jnp.float32,
        )
    ).astype(jnp.bfloat16)
    return (grad_encoder, grad_bias, grad_decoder)


def solution(mesh):
    return jax.shard_map(
        body,
        mesh=mesh,
        in_specs=(
            P(None, "feat", "mp"),
            P(None, "mp"),
            P(None, "mp", "feat"),
            P(None, "mp", "feat"),
            P(None, "feat", "mp"),
            P(None, "feat", "mp"),
            P(None, "feat"),
            P(None, "feat", "mp"),
        ),
        out_specs=(P(None, "feat", "mp"), P(None, "feat"), P(None, "feat", "mp")),
        check_vma=False,
    )
```

time: 271 us -> 112 us (0.41)
  blocking collectives: 140 us -> 0 us
  waiting for transfers between devices: 17.8 us -> 40.3 us
  starting transfers between devices: 6.99 us -> 27.4 us
  other arithmetic: 24.3 us -> 3.9 us
  matrix products: 53 us -> 36.4 us
  between operations: 14.6 us -> 0.94 us
  local copies, waits for them, and re-layouts: 13.5 us -> 2.84 us
    all_gather x2 -> x0, blocking collectives: 88.4 us -> none  [the longest x1 44.8 us: body(): normed = lax.all_gather(normed_local, 'feat', axis=1, tiled=True)]
    unnamed x1 -> x0, blocking collectives: 49 us -> none
    ppermute x0 -> x16, waiting for transfers between devices: none -> 40.3 us  [swap(): return lax.ppermute(values, axis, [(i, i ^ bit) for i in range(size)])]
    ppermute x0 -> x16, starting transfers between devices: none -> 27.4 us  [swap(): return lax.ppermute(values, axis, [(i, i ^ bit) for i in range(size)])]
    convert_element_type x2 -> x3, other arithmetic: 18.4 us -> 0.39 us  [the longest x1 0.29 us: body(): jnp.maximum(preact + encoder_bias[:, None, :], 0.0).astype(jnp.bfloat16)]
    psum x3 -> x0, waiting for transfers between devices: 17.4 us -> none  [the longest x1 17.4 us: body(): preact = lax.psum(preact_part, 'mp')]
    dot_general x10, matrix products: 46 us -> 34.5 us  [the longest x6 14.5 us: dot(): lax.dot_general(a, b, (contract, ((), ())), preferred_element_type=jnp.fl...]
    squeeze x1 -> x0, local copies, waits for them, and re-layouts: 11.3 us -> none  [body(): decoder[0]]
  transfers between devices with their start and end apart: 7 -> 16, of which waited for: 2 -> 14; matrix products, arithmetic and copies ran while one was open for 14% -> 9% of each run, Pallas kernels for 0% -> 0%
where the time goes in v1:
time: 112 us
  waiting for transfers between devices  40.3 us (36%)
  matrix products  36.4 us (32%)
  starting transfers between devices  27.4 us (24%)
  other arithmetic  3.9 us (3%)
  local copies, waits for them, and re-layouts  2.84 us (3%)
    ppermute x16, waiting for transfers between devices, swap(): return lax.ppermute(values, axis, [(i, i ^ bit) for i in range(size)])  40.3 us
    ppermute x16, starting transfers between devices, swap(): return lax.ppermute(values, axis, [(i, i ^ bit) for i in range(size)])  27.4 us
    dot_general x6, matrix products, dot(): lax.dot_general(a, b, (contract, ((), ())), preferred_element_type=jnp.fl...  14.5 us
    dot_general x1, matrix products, body(): jnp.einsum('ltf,ltd->lfd', jnp.stack([active[0], active[0], active[1]]),...  7.36 us
    dot_general x1, matrix products, body(): jnp.einsum('ltd,lfd->ltf', normed, encoder, preferred_element_type=jnp.fl...  6.78 us
    dot_general x1, matrix products, body(): jnp.einsum('ltf,ltd->lfd', pre_grad, normed, preferred_element_type=jnp.f...  5.18 us
  transfers between devices with their start and end apart: 16, of which 14 were waited for; matrix products, arithmetic and copies ran while one was open for 9% of the time, Pallas kernels for 0%

profile of v1, /device:TPU:0, one launch (start us, length us, event | category | flops | bytes accessed | tf_op | source)
XLA Modules:
  0.0 111.8 jit_solution(17298691925878264198)
XLA Ops:
  3.8 4.0 %collective-permute-start.1 = (bf16[2,6,1152]{2,1,0:T(8,128)(2,1)S(1)}, bf16[2,6,1152]{2,1,0:T(8,128)(2,1)S(1)}, u32[]{:S(2)}, u32[]{:S(2)}) collective-permute-start(bf16[2,6,1152]{2,1,0:T(8,128)(2,1)S(1)} %fusion.77), channel_id=1, source_target_pairs={{0,8},{1,9},{2,10},{3,11},{4,12},{5,13},{6,14},{7,15},{8,0},{9,1},... | collective-permute-start | bytes 82952 | tf_op jit(solution)/shard_map/ppermute | solution.py:16
  7.8 1.9 %collective-permute-done.1 = bf16[2,6,1152]{2,1,0:T(8,128)(2,1)S(1)} collective-permute-done((bf16[2,6,1152]{2,1,0:T(8,128)(2,1)S(1)}, bf16[2,6,1152]{2,1,0:T(8,128)(2,1)S(1)}, u32[]{:S(2)}, u32[]{:S(2)}) %collective-permute-start.1) | collective-permute-done | bytes 27680 | tf_op jit(solution)/shard_map/ppermute | solution.py:16
  9.7 2.0 %collective-permute-start.2 = (bf16[2,12,1152]{2,1,0:T(8,128)(2,1)S(1)}, bf16[2,12,1152]{2,1,0:T(8,128)(2,1)S(1)}, u32[]{:S(2)}, u32[]{:S(2)}) collective-permute-start(bf16[2,12,1152]{2,1,0:T(8,128)(2,1)S(1)} %pad_maximum_fusion.7), channel_id=1, source_target_pairs={{0,4},{1,5},{2,6},{3,7},{4,0},{5,1},{6,2},{7,3},{8,12},{9,13},{10,... | collective-permute-start | bytes 165896 | tf_op jit(solution)/shard_map/ppermute | solution.py:16
  11.7 2.4 %collective-permute-done.2 = bf16[2,12,1152]{2,1,0:T(8,128)(2,1)S(1)} collective-permute-done((bf16[2,12,1152]{2,1,0:T(8,128)(2,1)S(1)}, bf16[2,12,1152]{2,1,0:T(8,128)(2,1)S(1)}, u32[]{:S(2)}, u32[]{:S(2)}) %collective-permute-start.2) | collective-permute-done | bytes 55328 | tf_op jit(solution)/shard_map/ppermute | solution.py:16
  14.2 2.3 %collective-permute-start.3 = (bf16[2,24,1152]{2,1,0:T(8,128)(2,1)S(1)}, bf16[2,24,1152]{2,1,0:T(8,128)(2,1)S(1)}, u32[]{:S(2)}, u32[]{:S(2)}) collective-permute-start(bf16[2,24,1152]{2,1,0:T(8,128)(2,1)S(1)} %pad_maximum_fusion.5), channel_id=1, source_target_pairs={{0,2},{1,3},{2,0},{3,1},{4,6},{5,7},{6,4},{7,5},{8,10},{9,11},{10,... | collective-permute-start | bytes 331784 | tf_op jit(solution)/shard_map/ppermute | solution.py:16
  16.5 2.7 %collective-permute-done.3 = bf16[2,24,1152]{2,1,0:T(8,128)(2,1)S(1)} collective-permute-done((bf16[2,24,1152]{2,1,0:T(8,128)(2,1)S(1)}, bf16[2,24,1152]{2,1,0:T(8,128)(2,1)S(1)}, u32[]{:S(2)}, u32[]{:S(2)}) %collective-permute-start.3) | collective-permute-done | bytes 110624 | tf_op jit(solution)/shard_map/ppermute | solution.py:16
  19.3 2.1 %collective-permute-start.4 = (bf16[2,48,1152]{2,1,0:T(8,128)(2,1)S(1)}, bf16[2,48,1152]{2,1,0:T(8,128)(2,1)}, u32[]{:S(2)}, u32[]{:S(2)}) collective-permute-start(bf16[2,48,1152]{2,1,0:T(8,128)(2,1)S(1)} %pad_maximum_fusion.3), channel_id=1, source_target_pairs={{0,1},{1,0},{2,3},{3,2},{4,5},{5,4},{6,7},{7,6},{8,9},{9,8},{10,11... | collective-permute-start | bytes 663560 | tf_op jit(solution)/shard_map/ppermute | solution.py:16
  21.4 4.0 %collective-permute-done.4 = bf16[2,48,1152]{2,1,0:T(8,128)(2,1)} collective-permute-done((bf16[2,48,1152]{2,1,0:T(8,128)(2,1)S(1)}, bf16[2,48,1152]{2,1,0:T(8,128)(2,1)}, u32[]{:S(2)}, u32[]{:S(2)}) %collective-permute-start.4) | collective-permute-done | bytes 221216 | tf_op jit(solution)/shard_map/ppermute | solution.py:16
  25.4 1.4 %concatenate.36 = bf16[2,96,1152]{2,1,0:T(8,128)(2,1)S(1)} concatenate(bf16[2,6,1152]{2,1,0:T(8,128)(2,1)S(1)} %fusion.77, bf16[2,6,1152]{2,1,0:T(8,128)(2,1)S(1)} %collective-permute-done.1, bf16[2,12,1152]{2,1,0:T(8,128)(2,1)S(1)} %collective-permute-done.2, bf16[2,24,1152]{2,1,0:T(8,128)(2,1)S(1)} %collective-permute-done.3, bf16[2,48,1152]{2,1,0:T(8,128)(2,1)} %collective-permute-done.4), dimensions={1} | concatenate | bytes 884736 | tf_op jit(solution)/shard_map/concatenate | solution.py:33
  26.9 6.8 %fusion.86 = f32[2,96,2048]{2,1,0:T(8,128)S(1)} fusion(bf16[2,96,1152]{2,1,0:T(8,128)(2,1)S(1)} %concatenate.36, bf16[2,2048,1152]{2,1,0:T(8,128)(2,1)} %param.13), kind=kOutput, calls=%fused_computation.105 | convolution fusion | flops 905969664 | bytes 11452416 | tf_op jit(solution)/shard_map/ltd,lfd->ltf/dot_general | solution.py:60
  36.3 1.5 %collective-permute-done.6 = bf16[2,2,96,576]{3,2,1,0:T(8,128)(2,1)S(1)} collective-permute-done((bf16[2,2,96,576]{3,2,1,0:T(8,128)(2,1)S(1)}, bf16[2,2,96,576]{3,2,1,0:T(8,128)(2,1)S(1)}, u32[]{:S(2)}, u32[]{:S(2)}) %collective-permute-start.6) | collective-permute-done | bytes 442400 | tf_op jit(solution)/shard_map/ppermute | solution.py:16
  42.6 2.1 %collective-permute-start.7 = (bf16[48,2304]{1,0:T(8,128)(2,1)S(1)}, bf16[48,2304]{1,0:T(8,128)(2,1)S(1)}, u32[]{:S(2)}, u32[]{:S(2)}) collective-permute-start(bf16[48,2304]{1,0:T(8,128)(2,1)S(1)} %fusion.63), channel_id=1, source_target_pairs={{0,1},{1,0},{2,3},{3,2},{4,5},{5,4},{6,7},{7,6},{8,9},{9,8},{10,11... | collective-permute-start | bytes 663560 | tf_op jit(solution)/shard_map/ppermute | solution.py:16
  44.6 6.1 %collective-permute-done.7 = bf16[48,2304]{1,0:T(8,128)(2,1)S(1)} collective-permute-done((bf16[48,2304]{1,0:T(8,128)(2,1)S(1)}, bf16[48,2304]{1,0:T(8,128)(2,1)S(1)}, u32[]{:S(2)}, u32[]{:S(2)}) %collective-permute-start.7) | collective-permute-done | bytes 221216 | tf_op jit(solution)/shard_map/ppermute | solution.py:16
  50.8 1.8 %collective-permute-start.8 = (bf16[24,2304]{1,0:T(8,128)(2,1)S(1)}, bf16[24,2304]{1,0:T(8,128)(2,1)S(1)}, u32[]{:S(2)}, u32[]{:S(2)}) collective-permute-start(bf16[24,2304]{1,0:T(8,128)(2,1)S(1)} %slice.192), channel_id=1, source_target_pairs={{0,2},{1,3},{2,0},{3,1},{4,6},{5,7},{6,4},{7,5},{8,10},{9,11},{10,... | collective-permute-start | bytes 331784 | tf_op jit(solution)/shard_map/ppermute | solution.py:16
  52.6 3.1 %collective-permute-done.8 = bf16[24,2304]{1,0:T(8,128)(2,1)S(1)} collective-permute-done((bf16[24,2304]{1,0:T(8,128)(2,1)S(1)}, bf16[24,2304]{1,0:T(8,128)(2,1)S(1)}, u32[]{:S(2)}, u32[]{:S(2)}) %collective-permute-start.8) | collective-permute-done | bytes 110624 | tf_op jit(solution)/shard_map/ppermute | solution.py:16
  55.7 1.4 %collective-permute-start.9 = (bf16[12,2304]{1,0:T(8,128)(2,1)S(1)}, bf16[12,2304]{1,0:T(8,128)(2,1)S(1)}, u32[]{:S(2)}, u32[]{:S(2)}) collective-permute-start(bf16[12,2304]{1,0:T(8,128)(2,1)S(1)} %slice.193), channel_id=1, source_target_pairs={{0,4},{1,5},{2,6},{3,7},{4,0},{5,1},{6,2},{7,3},{8,12},{9,13},{10,... | collective-permute-start | bytes 165896 | tf_op jit(solution)/shard_map/ppermute | solution.py:16
  57.1 3.0 %collective-permute-done.9 = bf16[12,2304]{1,0:T(8,128)(2,1)S(1)} collective-permute-done((bf16[12,2304]{1,0:T(8,128)(2,1)S(1)}, bf16[12,2304]{1,0:T(8,128)(2,1)S(1)}, u32[]{:S(2)}, u32[]{:S(2)}) %collective-permute-start.9) | collective-permute-done | bytes 55328 | tf_op jit(solution)/shard_map/ppermute | solution.py:16
  60.2 2.4 %collective-permute-start.10 = (bf16[6,2304]{1,0:T(8,128)(2,1)S(1)}, bf16[6,2304]{1,0:T(8,128)(2,1)S(1)}, u32[]{:S(2)}, u32[]{:S(2)}) collective-permute-start(bf16[6,2304]{1,0:T(8,128)(2,1)S(1)} %slice.194), channel_id=1, source_target_pairs={{0,8},{1,9},{2,10},{3,11},{4,12},{5,13},{6,14},{7,15},{8,0},{9,1},... | collective-permute-start | bytes 82952 | tf_op jit(solution)/shard_map/ppermute | solution.py:16
  62.6 2.5 %collective-permute-done.10 = bf16[6,2304]{1,0:T(8,128)(2,1)S(1)} collective-permute-done((bf16[6,2304]{1,0:T(8,128)(2,1)S(1)}, bf16[6,2304]{1,0:T(8,128)(2,1)S(1)}, u32[]{:S(2)}, u32[]{:S(2)}) %collective-permute-start.10) | collective-permute-done | bytes 27680 | tf_op jit(solution)/shard_map/ppermute | solution.py:16
  65.1 2.5 %collective-permute-start.11 = (bf16[6,2304]{1,0:T(8,128)(2,1)S(1)}, bf16[6,2304]{1,0:T(8,128)(2,1)S(1)}, u32[]{:S(2)}, u32[]{:S(2)}) collective-permute-start(bf16[6,2304]{1,0:T(8,128)(2,1)S(1)} %fusion.78), channel_id=1, source_target_pairs={{0,8},{1,9},{2,10},{3,11},{4,12},{5,13},{6,14},{7,15},{8,0},{9,1},... | collective-permute-start | bytes 82952 | tf_op jit(solution)/shard_map/ppermute | solution.py:16
  67.7 2.5 %collective-permute-done.11 = bf16[6,2304]{1,0:T(8,128)(2,1)S(1)} collective-permute-done((bf16[6,2304]{1,0:T(8,128)(2,1)S(1)}, bf16[6,2304]{1,0:T(8,128)(2,1)S(1)}, u32[]{:S(2)}, u32[]{:S(2)}) %collective-permute-start.11) | collective-permute-done | bytes 27680 | tf_op jit(solution)/shard_map/ppermute | solution.py:16
  70.2 2.3 %collective-permute-start.12 = (bf16[12,2304]{1,0:T(8,128)(2,1)S(1)}, bf16[12,2304]{1,0:T(8,128)(2,1)S(1)}, u32[]{:S(2)}, u32[]{:S(2)}) collective-permute-start(bf16[12,2304]{1,0:T(8,128)(2,1)S(1)} %pad_maximum_fusion.8), channel_id=1, source_target_pairs={{0,4},{1,5},{2,6},{3,7},{4,0},{5,1},{6,2},{7,3},{8,12},{9,13},{10,... | collective-permute-start | bytes 165896 | tf_op jit(solution)/shard_map/ppermute | solution.py:16
  72.4 2.3 %collective-permute-done.12 = bf16[12,2304]{1,0:T(8,128)(2,1)S(1)} collective-permute-done((bf16[12,2304]{1,0:T(8,128)(2,1)S(1)}, bf16[12,2304]{1,0:T(8,128)(2,1)S(1)}, u32[]{:S(2)}, u32[]{:S(2)}) %collective-permute-start.12) | collective-permute-done | bytes 55328 | tf_op jit(solution)/shard_map/ppermute | solution.py:16
  74.8 1.7 %collective-permute-start.13 = (bf16[24,2304]{1,0:T(8,128)(2,1)S(1)}, bf16[24,2304]{1,0:T(8,128)(2,1)S(1)}, u32[]{:S(2)}, u32[]{:S(2)}) collective-permute-start(bf16[24,2304]{1,0:T(8,128)(2,1)S(1)} %pad_maximum_fusion.6), channel_id=1, source_target_pairs={{0,2},{1,3},{2,0},{3,1},{4,6},{5,7},{6,4},{7,5},{8,10},{9,11},{10,... | collective-permute-start | bytes 331784 | tf_op jit(solution)/shard_map/ppermute | solution.py:16
  76.5 3.1 %collective-permute-done.13 = bf16[24,2304]{1,0:T(8,128)(2,1)S(1)} collective-permute-done((bf16[24,2304]{1,0:T(8,128)(2,1)S(1)}, bf16[24,2304]{1,0:T(8,128)(2,1)S(1)}, u32[]{:S(2)}, u32[]{:S(2)}) %collective-permute-start.13) | collective-permute-done | bytes 110624 | tf_op jit(solution)/shard_map/ppermute | solution.py:16
  79.7 1.7 %collective-permute-start.14 = (bf16[48,2304]{1,0:T(8,128)(2,1)S(1)}, bf16[48,2304]{1,0:T(8,128)(2,1)S(1)}, u32[]{:S(2)}, u32[]{:S(2)}) collective-permute-start(bf16[48,2304]{1,0:T(8,128)(2,1)S(1)} %pad_maximum_fusion.4), channel_id=1, source_target_pairs={{0,1},{1,0},{2,3},{3,2},{4,5},{5,4},{6,7},{7,6},{8,9},{9,8},{10,11... | collective-permute-start | bytes 663560 | tf_op jit(solution)/shard_map/ppermute | solution.py:16
  81.4 4.3 %collective-permute-done.14 = bf16[48,2304]{1,0:T(8,128)(2,1)S(1)} collective-permute-done((bf16[48,2304]{1,0:T(8,128)(2,1)S(1)}, bf16[48,2304]{1,0:T(8,128)(2,1)S(1)}, u32[]{:S(2)}, u32[]{:S(2)}) %collective-permute-start.14) | collective-permute-done | bytes 221216 | tf_op jit(solution)/shard_map/ppermute | solution.py:16
  86.1 3.9 %fusion.4 = f32[96,2048]{1,0:T(8,128)S(1)} fusion(bf16[3,2048,1152]{2,1,0:T(8,128)(2,1)} %param.15, bf16[96,2304]{1,0:T(8,128)(2,1)S(1)} %concatenate.41), kind=kOutput, calls=%fused_computation.6 | convolution fusion | flops 452984832 | bytes 5726208 | tf_op jit(solution)/shard_map/dot_general | solution.py:45
  90.0 3.9 %fusion.39 = bf16[1,96,2048]{2,1,0:T(8,128)(2,1)S(1)} fusion(bf16[3,2048,1152]{2,1,0:T(8,128)(2,1)} %param.15, bf16[96,2304]{1,0:T(8,128)(2,1)S(1)} %concatenate.41), kind=kOutput, calls=%fused_computation.27 | convolution fusion | flops 453181440 | bytes 5332992 | tf_op jit(solution)/shard_map/dot_general | solution.py:45
  93.9 4.0 %fusion.36 = bf16[1,96,2048]{2,1,0:T(8,128)(2,1)S(1)} fusion(f32[96,2048]{1,0:T(8,128)S(1)} %fusion.4, bf16[3,2048,1152]{2,1,0:T(8,128)(2,1)} %param.15, bf16[96,2304]{1,0:T(8,128)(2,1)S(1)} %concatenate.41), kind=kOutput, calls=%fused_computation.26 | convolution fusion | flops 453378048 | bytes 6119424 | tf_op jit(solution)/shard_map/dot_general | solution.py:45
  98.1 7.4 %multiply_convert_fusion = bf16[3,2048,1152]{2,1,0:T(8,128)(2,1)} fusion(bf16[2,96,2048]{2,1,0:T(8,128)(2,1)S(1)} %copy-done.3, bf16[1,96,2048]{2,1,0:T(8,128)(2,1)S(1)} %slice-done, bf16[1,96,1152]{2,1,0:T(8,128)(2,1)S(1)} %get-tuple-element.6, bf16[1,96,1152]{2,1,0:T(8,128)(2,1)S(1)} %get-tuple-element.5), kind=kOutput, calls=%fused_computation | convolution fusion | flops 1374363648 | bytes 15777792 | tf_op jit(solution)/shard_map/ltf,ltd->lfd/dot_general | solution.py:86
  106.6 5.2 %convolution_convert_fusion = bf16[2,2048,1152]{2,1,0:T(8,128)(2,1)} fusion(bf16[2,96,2048]{2,1,0:T(8,128)(2,1)S(1)} %get-tuple-element.4, bf16[2,96,1152]{2,1,0:T(8,128)(2,1)S(1)} %concatenate.36), kind=kOutput, calls=%fused_computation.1 | convolution fusion | flops 910688256 | bytes 10665984 | tf_op jit(solution)/shard_map/ltf,ltd->lfd/dot_general | solution.py:80
  (55 shorter events, 12.6 us)
Async XLA Ops:
  0.6 37.3 %copy-start = (bf16[2,576,1152]{2,1,0:T(8,128)(2,1)S(1)}, bf16[2,576,1152]{2,1,0:T(8,128)(2,1)}, u32[]{:S(2)}) copy-start(bf16[2,576,1152]{2,1,0:T(8,128)(2,1)} %param.12) | copy-start | bytes 7962628
  1.6 1.3 %collective-permute-start = (f32[2,6]{1,0:T(2,128)S(1)}, f32[2,6]{1,0:T(2,128)S(1)}, u32[]{:S(2)}, u32[]{:S(2)}) collective-permute-start(f32[2,6]{1,0:T(2,128)S(1)} %fusion.75), channel_id=1, source_target_pairs={{0,16},{16,0},{1,17},{17,1},{2,18},{18,2},{3,19},{19,3},{4,20},{20... | collective-permute-start | bytes 152 | tf_op jit(solution)/shard_map/ppermute | solution.py:16
  3.8 5.9 %collective-permute-start.1 = (bf16[2,6,1152]{2,1,0:T(8,128)(2,1)S(1)}, bf16[2,6,1152]{2,1,0:T(8,128)(2,1)S(1)}, u32[]{:S(2)}, u32[]{:S(2)}) collective-permute-start(bf16[2,6,1152]{2,1,0:T(8,128)(2,1)S(1)} %fusion.77), channel_id=1, source_target_pairs={{0,8},{1,9},{2,10},{3,11},{4,12},{5,13},{6,14},{7,15},{8,0},{9,1},... | collective-permute-start | bytes 82952 | tf_op jit(solution)/shard_map/ppermute | solution.py:16
  9.7 4.4 %collective-permute-start.2 = (bf16[2,12,1152]{2,1,0:T(8,128)(2,1)S(1)}, bf16[2,12,1152]{2,1,0:T(8,128)(2,1)S(1)}, u32[]{:S(2)}, u32[]{:S(2)}) collective-permute-start(bf16[2,12,1152]{2,1,0:T(8,128)(2,1)S(1)} %pad_maximum_fusion.7), channel_id=1, source_target_pairs={{0,4},{1,5},{2,6},{3,7},{4,0},{5,1},{6,2},{7,3},{8,12},{9,13},{10,... | collective-permute-start | bytes 165896 | tf_op jit(solution)/shard_map/ppermute | solution.py:16
  14.2 5.0 %collective-permute-start.3 = (bf16[2,24,1152]{2,1,0:T(8,128)(2,1)S(1)}, bf16[2,24,1152]{2,1,0:T(8,128)(2,1)S(1)}, u32[]{:S(2)}, u32[]{:S(2)}) collective-permute-start(bf16[2,24,1152]{2,1,0:T(8,128)(2,1)S(1)} %pad_maximum_fusion.5), channel_id=1, source_target_pairs={{0,2},{1,3},{2,0},{3,1},{4,6},{5,7},{6,4},{7,5},{8,10},{9,11},{10,... | collective-permute-start | bytes 331784 | tf_op jit(solution)/shard_map/ppermute | solution.py:16
  19.3 6.1 %collective-permute-start.4 = (bf16[2,48,1152]{2,1,0:T(8,128)(2,1)S(1)}, bf16[2,48,1152]{2,1,0:T(8,128)(2,1)}, u32[]{:S(2)}, u32[]{:S(2)}) collective-permute-start(bf16[2,48,1152]{2,1,0:T(8,128)(2,1)S(1)} %pad_maximum_fusion.3), channel_id=1, source_target_pairs={{0,1},{1,0},{2,3},{3,2},{4,5},{5,4},{6,7},{7,6},{8,9},{9,8},{10,11... | collective-permute-start | bytes 663560 | tf_op jit(solution)/shard_map/ppermute | solution.py:16
  26.8 6.9 %copy-start.4 = (bf16[2,1152,576]{1,2,0:T(8,128)(2,1)S(1)}, bf16[2,1152,576]{1,2,0:T(8,128)(2,1)}, u32[]{:S(2)}) copy-start(bf16[2,1152,576]{1,2,0:T(8,128)(2,1)} %param.10) | copy-start | bytes 7962628
  26.9 7.8 %copy-start.5 = (bf16[2,1152,576]{1,2,0:T(8,128)(2,1)S(1)}, bf16[2,1152,576]{1,2,0:T(8,128)(2,1)}, u32[]{:S(2)}) copy-start(bf16[2,1152,576]{1,2,0:T(8,128)(2,1)} %param.11) | copy-start | bytes 7962628
  33.7 4.9 %collective-permute-start.5 = (f32[2,96,2048]{2,1,0:T(8,128)S(1)}, f32[2,96,2048]{2,1,0:T(8,128)S(1)}, u32[]{:S(2)}, u32[]{:S(2)}) collective-permute-start(f32[2,96,2048]{2,1,0:T(8,128)S(1)} %fusion.86), channel_id=1, source_target_pairs={{0,16},{16,0},{1,17},{17,1},{2,18},{18,2},{3,19},{19,3},{4,20},{20... | collective-permute-start | bytes 4718600 | tf_op jit(solution)/shard_map/ppermute | solution.py:16
  34.7 3.9 %copy-start.6 = (f32[2,2048]{1,0:T(2,128)S(1)}, f32[2,2048]{1,0:T(2,128)}, u32[]{:S(2)}) copy-start(f32[2,2048]{1,0:T(2,128)} %param.14) | copy-start | bytes 49156
  34.7 5.0 %copy-start.7 = (bf16[3,2048,1152]{2,1,0:T(8,128)(2,1)S(1)}, bf16[3,2048,1152]{2,1,0:T(8,128)(2,1)}, u32[]{:S(2)}) copy-start(bf16[3,2048,1152]{2,1,0:T(8,128)(2,1)} %param.15) | copy-start | bytes 42467332
  35.8 2.0 %collective-permute-start.6 = (bf16[2,2,96,576]{3,2,1,0:T(8,128)(2,1)S(1)}, bf16[2,2,96,576]{3,2,1,0:T(8,128)(2,1)S(1)}, u32[]{:S(2)}, u32[]{:S(2)}) collective-permute-start(bf16[2,2,96,576]{3,2,1,0:T(8,128)(2,1)S(1)} %pad_maximum_fusion.1), channel_id=1, source_target_pairs={{0,16},{16,0},{1,17},{17,1},{2,18},{18,2},{3,19},{19,3},{4,20},{20... | collective-permute-start | bytes 1327112 | tf_op jit(solution)/shard_map/ppermute | solution.py:16
  39.8 41.6 %copy-start.2 = (bf16[2,96,2048]{2,1,0:T(8,128)(2,1)}, bf16[2,96,2048]{2,1,0:T(8,128)(2,1)S(1)}, u32[]{:S(2)}) copy-start(bf16[2,96,2048]{2,1,0:T(8,128)(2,1)S(1)} %maximum_convert_fusion) | copy-start | bytes 2359300
  42.6 8.1 %collective-permute-start.7 = (bf16[48,2304]{1,0:T(8,128)(2,1)S(1)}, bf16[48,2304]{1,0:T(8,128)(2,1)S(1)}, u32[]{:S(2)}, u32[]{:S(2)}) collective-permute-start(bf16[48,2304]{1,0:T(8,128)(2,1)S(1)} %fusion.63), channel_id=1, source_target_pairs={{0,1},{1,0},{2,3},{3,2},{4,5},{5,4},{6,7},{7,6},{8,9},{9,8},{10,11... | collective-permute-start | bytes 663560 | tf_op jit(solution)/shard_map/ppermute | solution.py:16
  50.8 4.9 %collective-permute-start.8 = (bf16[24,2304]{1,0:T(8,128)(2,1)S(1)}, bf16[24,2304]{1,0:T(8,128)(2,1)S(1)}, u32[]{:S(2)}, u32[]{:S(2)}) collective-permute-start(bf16[24,2304]{1,0:T(8,128)(2,1)S(1)} %slice.192), channel_id=1, source_target_pairs={{0,2},{1,3},{2,0},{3,1},{4,6},{5,7},{6,4},{7,5},{8,10},{9,11},{10,... | collective-permute-start | bytes 331784 | tf_op jit(solution)/shard_map/ppermute | solution.py:16
  55.7 4.4 %collective-permute-start.9 = (bf16[12,2304]{1,0:T(8,128)(2,1)S(1)}, bf16[12,2304]{1,0:T(8,128)(2,1)S(1)}, u32[]{:S(2)}, u32[]{:S(2)}) collective-permute-start(bf16[12,2304]{1,0:T(8,128)(2,1)S(1)} %slice.193), channel_id=1, source_target_pairs={{0,4},{1,5},{2,6},{3,7},{4,0},{5,1},{6,2},{7,3},{8,12},{9,13},{10,... | collective-permute-start | bytes 165896 | tf_op jit(solution)/shard_map/ppermute | solution.py:16
  60.2 4.9 %collective-permute-start.10 = (bf16[6,2304]{1,0:T(8,128)(2,1)S(1)}, bf16[6,2304]{1,0:T(8,128)(2,1)S(1)}, u32[]{:S(2)}, u32[]{:S(2)}) collective-permute-start(bf16[6,2304]{1,0:T(8,128)(2,1)S(1)} %slice.194), channel_id=1, source_target_pairs={{0,8},{1,9},{2,10},{3,11},{4,12},{5,13},{6,14},{7,15},{8,0},{9,1},... | collective-permute-start | bytes 82952 | tf_op jit(solution)/shard_map/ppermute | solution.py:16
  65.1 5.0 %collective-permute-start.11 = (bf16[6,2304]{1,0:T(8,128)(2,1)S(1)}, bf16[6,2304]{1,0:T(8,128)(2,1)S(1)}, u32[]{:S(2)}, u32[]{:S(2)}) collective-permute-start(bf16[6,2304]{1,0:T(8,128)(2,1)S(1)} %fusion.78), channel_id=1, source_target_pairs={{0,8},{1,9},{2,10},{3,11},{4,12},{5,13},{6,14},{7,15},{8,0},{9,1},... | collective-permute-start | bytes 82952 | tf_op jit(solution)/shard_map/ppermute | solution.py:16
  70.2 4.6 %collective-permute-start.12 = (bf16[12,2304]{1,0:T(8,128)(2,1)S(1)}, bf16[12,2304]{1,0:T(8,128)(2,1)S(1)}, u32[]{:S(2)}, u32[]{:S(2)}) collective-permute-start(bf16[12,2304]{1,0:T(8,128)(2,1)S(1)} %pad_maximum_fusion.8), channel_id=1, source_target_pairs={{0,4},{1,5},{2,6},{3,7},{4,0},{5,1},{6,2},{7,3},{8,12},{9,13},{10,... | collective-permute-start | bytes 165896 | tf_op jit(solution)/shard_map/ppermute | solution.py:16
  74.8 4.8 %collective-permute-start.13 = (bf16[24,2304]{1,0:T(8,128)(2,1)S(1)}, bf16[24,2304]{1,0:T(8,128)(2,1)S(1)}, u32[]{:S(2)}, u32[]{:S(2)}) collective-permute-start(bf16[24,2304]{1,0:T(8,128)(2,1)S(1)} %pad_maximum_fusion.6), channel_id=1, source_target_pairs={{0,2},{1,3},{2,0},{3,1},{4,6},{5,7},{6,4},{7,5},{8,10},{9,11},{10,... | collective-permute-start | bytes 331784 | tf_op jit(solution)/shard_map/ppermute | solution.py:16
  79.7 6.0 %collective-permute-start.14 = (bf16[48,2304]{1,0:T(8,128)(2,1)S(1)}, bf16[48,2304]{1,0:T(8,128)(2,1)S(1)}, u32[]{:S(2)}, u32[]{:S(2)}) collective-permute-start(bf16[48,2304]{1,0:T(8,128)(2,1)S(1)} %pad_maximum_fusion.4), channel_id=1, source_target_pairs={{0,1},{1,0},{2,3},{3,2},{4,5},{5,4},{6,7},{7,6},{8,9},{9,8},{10,11... | collective-permute-start | bytes 663560 | tf_op jit(solution)/shard_map/ppermute | solution.py:16
  93.9 4.2 %copy-start.3 = (bf16[2,96,2048]{2,1,0:T(8,128)(2,1)S(1)}, bf16[2,96,2048]{2,1,0:T(8,128)(2,1)}, u32[]{:S(2)}) copy-start(bf16[2,96,2048]{2,1,0:T(8,128)(2,1)} %copy-done.2) | copy-start | bytes 2359300
  93.9 4.2 %slice-start = ((bf16[2,96,2048]{2,1,0:T(8,128)(2,1)}), bf16[1,96,2048]{2,1,0:T(8,128)(2,1)S(1)}, s32[]{:S(2)}) async-start(bf16[2,96,2048]{2,1,0:T(8,128)(2,1)} %copy-done.2), calls=%async_computation | async-start | bytes 786432 | tf_op jit(solution)/shard_map/slice | solution.py:67
  98.0 7.5 %collective-permute-start.15 = (bf16[2,96,2048]{2,1,0:T(8,128)(2,1)S(1)}, bf16[2,96,2048]{2,1,0:T(8,128)(2,1)S(1)}, u32[]{:S(2)}, u32[]{:S(2)}) collective-permute-start(bf16[2,96,2048]{2,1,0:T(8,128)(2,1)S(1)} %pad_maximum_fusion), channel_id=1, source_target_pairs={{0,16},{16,0},{1,17},{17,1},{2,18},{18,2},{3,19},{19,3},{4,20},{20... | collective-permute-start | bytes 2359304 | tf_op jit(solution)/shard_map/ppermute | solution.py:16
  106.6 5.2 %copy-start.1 = (bf16[2,576,1152]{2,1,0:T(8,128)(2,1)S(1)}, bf16[2,576,1152]{2,1,0:T(8,128)(2,1)}, u32[]{:S(2)}) copy-start(bf16[2,576,1152]{2,1,0:T(8,128)(2,1)} %param.12) | copy-start | bytes 7962628

commit v2 on v1

v2 whole, which is shorter than its diff:
```python
import math

import jax
import jax.numpy as jnp
from jax import lax
from jax.experimental import pallas as pl
from jax.experimental.pallas import tpu as pltpu
from jax.sharding import PartitionSpec as P

D = 2304


sparsity_weight = 0.1


def swap(values, axis, bit):
    size = lax.axis_size(axis)
    return lax.ppermute(values, axis, [(i, i ^ bit) for i in range(size)])


def bits_of(axis):
    size = lax.axis_size(axis)
    return [1 << k for k in range(size.bit_length() - 1)]


def mp_sum(values, wire=None):
    for bit in bits_of("mp"):
        sent = values if wire is None else values.astype(wire)
        values = values + swap(sent, "mp", bit).astype(values.dtype)
    return values


def join(*parts):
    return jnp.concatenate(parts, axis=0)


def gather_inner(block):
    place = lax.axis_index("feat")
    for bit in reversed(bits_of("feat")[2:]):
        other = swap(block, "feat", bit)
        upper = (place & bit) > 0
        block = join(jnp.where(upper, other, block), jnp.where(upper, block, other))
    return block


def gather_outer(quarter, layer):
    rows = quarter.shape[0]
    if layer == 0:
        half = join(quarter, swap(quarter, "feat", 2))
        return join(half, swap(half, "feat", 1))
    across = swap(quarter, "feat", 1)
    other = swap(join(quarter, across), "feat", 2)
    return join(quarter, other[:rows], across, other[rows:])


def send_add(kept, sent, bit):
    return kept + swap(sent.astype(jnp.bfloat16), "feat", bit).astype(jnp.float32)


def scatter_outer(values, layer):
    rows = values.shape[0] // 4
    own, second, first, both = (values[k * rows : (k + 1) * rows] for k in range(4))
    if layer == 0:
        half = send_add(values[: 2 * rows], values[2 * rows :], 1)
        return send_add(half[:rows], half[rows:], 2)
    half = send_add(join(own, first), join(second, both), 2)
    return send_add(half[:rows], half[rows:], 1)


def sum_inner(quarter):
    bits = bits_of("feat")[2:]
    for bit in bits:
        received = swap(quarter.astype(jnp.bfloat16), "feat", bit)
        if bit == bits[-1]:
            return add_round(quarter, received, int(4e10))
        quarter = quarter + received.astype(jnp.float32)


def square_sums(values, flops):
    def kernel(values_ref, out_ref):
        v = values_ref[...].astype(jnp.float32)
        out_ref[...] = jnp.sum(v * v, axis=2)

    return pl.pallas_call(
        kernel,
        out_shape=jax.ShapeDtypeStruct(values.shape[:2], jnp.float32),
        in_specs=[pl.BlockSpec(memory_space=pltpu.VMEM)],
        out_specs=pl.BlockSpec(memory_space=pltpu.VMEM),
        compiler_params=pltpu.CompilerParams(vmem_limit_bytes=4 << 20),
        cost_estimate=pl.CostEstimate(flops=flops, bytes_accessed=1 << 16, transcendentals=0),
    )(values)


def add_round(kept, received, flops):
    def kernel(kept_ref, received_ref, out_ref):
        total = kept_ref[...] + received_ref[...].astype(jnp.float32)
        out_ref[...] = total.astype(jnp.bfloat16)

    return pl.pallas_call(
        kernel,
        out_shape=jax.ShapeDtypeStruct(kept.shape, jnp.bfloat16),
        in_specs=[pl.BlockSpec(memory_space=pltpu.VMEM)] * 2,
        out_specs=pl.BlockSpec(memory_space=pltpu.VMEM),
        compiler_params=pltpu.CompilerParams(vmem_limit_bytes=4 << 20),
        cost_estimate=pl.CostEstimate(flops=flops, bytes_accessed=1 << 16, transcendentals=0),
    )(kept, received)


def row_chunks(rows, most):
    size = min(rows, most)
    while rows % size:
        size //= 2
    return [(at, size) for at in range(0, rows, size)]


def dot(a, b, contract):
    return lax.dot_general(a, b, (contract, ((), ())), preferred_element_type=jnp.float32)


tn = ((0,), (0,))
nn = ((1,), (0,))
nt = ((1,), (1,))


def decoder_gradient(active, errors, scale):
    tokens, features = active[0].shape
    cols = errors[0].shape[1]
    picks = [(0, 0), (0, 1), (1, 1)]
    chunks = row_chunks(features, 256)

    def kernel(active_0, active_1, errors_0, errors_1, out_ref, held, sems):
        actives, error_refs = (active_0, active_1), (errors_0, errors_1)
        copies = []
        for k, (a, e) in enumerate(picks):
            right = error_refs[e][...]
            for c, (at, size) in enumerate(chunks):
                rows = pl.ds(at, size)
                held[k, rows] = (scale * dot(actives[a][:, rows], right, tn)).astype(jnp.bfloat16)
                copies.append(pltpu.make_async_copy(held.at[k, rows], out_ref.at[k, rows], sems.at[k, c]))
                copies[-1].start()
        for copy in copies:
            copy.wait()

    vmem = pl.BlockSpec(memory_space=pltpu.VMEM)
    return pl.pallas_call(
        kernel,
        out_shape=jax.ShapeDtypeStruct((3, features, cols), jnp.bfloat16),
        in_specs=[vmem] * 4,
        out_specs=pl.BlockSpec(memory_space=pl.ANY),
        scratch_shapes=[
            pltpu.VMEM((3, features, cols), jnp.bfloat16),
            pltpu.SemaphoreType.DMA((3, len(chunks))),
        ],
        compiler_params=pltpu.CompilerParams(vmem_limit_bytes=24 << 20),
        cost_estimate=pl.CostEstimate(
            flops=6 * tokens * features * cols, bytes_accessed=6 * features * cols, transcendentals=0
        ),
    )(*active, *errors)


def encoder_gradient(active, own, received, normed, scale):
    tokens, features = active[0].shape
    cols = normed[0].shape[1]
    chunks = row_chunks(features, 256)

    def kernel(active_0, active_1, own_ref, received_ref, normed_0, normed_1, out_ref, bias_ref, held, sems):
        copies = []
        for l, (active_ref, normed_ref) in enumerate(((active_0, normed_0), (active_1, normed_1))):
            right = normed_ref[...]
            for c, (at, size) in enumerate(chunks):
                rows = pl.ds(at, size)
                backward = own_ref[l, :, rows].astype(jnp.float32) + received_ref[l, :, rows].astype(jnp.float32)
                open_gate = active_ref[:, rows].astype(jnp.float32) > 0
                pre_grad = jnp.where(open_gate, scale * (backward + sparsity_weight), 0.0).astype(jnp.bfloat16)
                bias_ref[l : l + 1, rows] = jnp.sum(pre_grad.astype(jnp.float32), axis=0, keepdims=True)
                held[l, rows] = dot(pre_grad, right, tn).astype(jnp.bfloat16)
                copies.append(pltpu.make_async_copy(held.at[l, rows], out_ref.at[l, rows], sems.at[l, c]))
                copies[-1].start()
        for copy in copies:
            copy.wait()

    vmem = pl.BlockSpec(memory_space=pltpu.VMEM)
    return pl.pallas_call(
        kernel,
        out_shape=(
            jax.ShapeDtypeStruct((2, features, cols), jnp.bfloat16),
            jax.ShapeDtypeStruct((2, features), jnp.float32),
        ),
        in_specs=[vmem] * 6,
        out_specs=(pl.BlockSpec(memory_space=pl.ANY), vmem),
        scratch_shapes=[
            pltpu.VMEM((2, features, cols), jnp.bfloat16),
            pltpu.SemaphoreType.DMA((2, len(chunks))),
        ],
        compiler_params=pltpu.CompilerParams(vmem_limit_bytes=24 << 20),
        cost_estimate=pl.CostEstimate(
            flops=4 * tokens * features * cols, bytes_accessed=4 * features * cols, transcendentals=0
        ),
    )(*active, own, received, *normed)


def body(residual, norm_gain, gate_weight, up_weight, down_weight, encoder, encoder_bias, decoder):
    values = residual.astype(jnp.float32)
    squares = mp_sum(square_sums(residual, int(4e11)))
    inverse_rms = lax.rsqrt(squares / D + 1e-06)
    normed_local = (values * inverse_rms[:, :, None] * norm_gain[:, None, :]).astype(jnp.bfloat16)
    model_cols = decoder.shape[2]
    quarter = gather_inner(jnp.concatenate([normed_local[0], normed_local[1]], axis=1))
    normed = [gather_outer(quarter[:, l * model_cols : (l + 1) * model_cols], l) for l in range(2)]
    tokens = normed[0].shape[0]
    active = []
    target = []
    for l in range(2):
        preact = mp_sum(dot(normed[l], encoder[l], nt))
        active.append(jnp.maximum(preact + encoder_bias[l][None, :], 0.0).astype(jnp.bfloat16))
        gate_part = dot(normed[l], gate_weight[l], nn)
        up_part = dot(normed[l], up_weight[l], nn)
        mlp = mp_sum(jnp.stack([gate_part, up_part]).astype(jnp.bfloat16)).astype(jnp.float32)
        hidden = (jax.nn.gelu(mlp[0], approximate=True) * mlp[1]).astype(jnp.bfloat16)
        target.append(dot(hidden, down_weight[l], nn))
    partial = [
        dot(active[0], decoder[0], nn) - target[0],
        dot(active[0], decoder[1], nn) + dot(active[1], decoder[2], nn) - target[1],
    ]
    errors = [
        gather_outer(sum_inner(scatter_outer(partial[l], l)), l)
        for l in range(2)
    ]
    back_first = dot(errors[0], decoder[0], nt) + dot(errors[1], decoder[1], nt)
    back_second = dot(errors[1], decoder[2], nt)
    loss_scale = 1.0 / math.sqrt(tokens)
    own = jnp.stack([back_first, back_second]).astype(jnp.bfloat16)
    *inner, last = bits_of("mp")
    for bit in inner:
        own = own + swap(own, "mp", bit)
    received = swap(own, "mp", last)
    grad_decoder = decoder_gradient(active, errors, loss_scale)
    grad_encoder, grad_bias = encoder_gradient(active, own, received, normed, loss_scale)
    return (grad_encoder, grad_bias, grad_decoder)


def solution(mesh):
    return jax.shard_map(
        body,
        mesh=mesh,
        in_specs=(
            P(None, "feat", "mp"),
            P(None, "mp"),
            P(None, "mp", "feat"),
            P(None, "mp", "feat"),
            P(None, "feat", "mp"),
            P(None, "feat", "mp"),
            P(None, "feat"),
            P(None, "feat", "mp"),
        ),
        out_specs=(P(None, "feat", "mp"), P(None, "feat"), P(None, "feat", "mp")),
        check_vma=False,
    )
```

time: 112 us -> 82.7 us (0.74)
  waiting for transfers between devices: 40.3 us -> 18.3 us
  matrix products: 36.4 us -> 17.2 us
  Pallas kernels: 0 us -> 10.4 us
  starting transfers between devices: 27.4 us -> 33.5 us
  other arithmetic: 3.9 us -> 0.96 us
  local copies, waits for them, and re-layouts: 2.84 us -> 0.91 us
    ppermute x16 -> x24, waiting for transfers between devices: 40.3 us -> 18.3 us  [swap(): return lax.ppermute(values, axis, [(i, i ^ bit) for i in range(size)])]
    dot_general x6 -> x0, matrix products: 21.9 us -> none  [the longest x1 7.36 us: body(): jnp.einsum('ltf,ltd->lfd', jnp.stack([active[0], active[0], active[1]]),...]
    pallas_call x0 -> x5, Pallas kernels: none -> 10.4 us  [the longest x1 5.59 us: decoder_gradient(): pl.pallas_call(kernel, out_shape=jax.ShapeDtypeStruct((3, features, cols)...]
    ppermute x16 -> x24, starting transfers between devices: 27.4 us -> 33.5 us  [swap(): return lax.ppermute(values, axis, [(i, i ^ bit) for i in range(size)])]
    dot_general x6 -> x14, matrix products: 14.5 us -> 17.2 us  [dot(): lax.dot_general(a, b, (contract, ((), ())), preferred_element_type=jnp.fl...]
    reduce_sum x2 -> x0, other arithmetic: 2.13 us -> none  [the longest x1 1.14 us: body(): grad_bias = jnp.sum(pre_grad.astype(jnp.float32), axis=1)]
    concatenate x2 -> x0, local copies, waits for them, and re-layouts: 1.84 us -> none  [gather_tokens(): values = jnp.concatenate([values, swap(values, 'feat', bit)], axis=dim)]
  transfers between devices with their start and end apart: 16 -> 24, of which waited for: 14 -> 13; matrix products, arithmetic and copies ran while one was open for 9% -> 20% of each run, Pallas kernels for 0% -> 7%
where the time goes in v2:
time: 82.7 us; the launch traced here: 82.5 us
  starting transfers between devices  33.5 us (41%)
  waiting for transfers between devices  18.3 us (22%)
  matrix products  17.2 us (21%)
  Pallas kernels  10.4 us (13%)
  between operations  1.26 us (2%)
  other arithmetic  0.96 us (1%)
  local copies, waits for them, and re-layouts  0.91 us (1%)
    ppermute x24, starting transfers between devices, swap(): return lax.ppermute(values, axis, [(i, i ^ bit) for i in range(size)])  33.5 us
    ppermute x24, waiting for transfers between devices, swap(): return lax.ppermute(values, axis, [(i, i ^ bit) for i in range(size)])  18.3 us
    dot_general x14, matrix products, dot(): lax.dot_general(a, b, (contract, ((), ())), preferred_element_type=jnp.fl...  17.2 us
    pallas_call x1, Pallas kernels, decoder_gradient(): pl.pallas_call(kernel, out_shape=jax.ShapeDtypeStruct((3, features, cols)...  5.59 us
    pallas_call x1, Pallas kernels, encoder_gradient(): pl.pallas_call(kernel, out_shape=(jax.ShapeDtypeStruct((2, features, cols...  4.72 us
  transfers between devices with their start and end apart: 24, of which 13 were waited for; matrix products, arithmetic and copies ran while one was open for 20% of the time, Pallas kernels for 7%

profile of v2, /device:TPU:0, one launch (start us, length us, event | category | flops | bytes accessed | tf_op | source)
XLA Modules:
  0.0 82.5 jit_solution(12642768683439944688)
XLA Ops:
  2.9 4.0 %collective-permute-start.1 = (bf16[6,2304]{1,0:T(8,128)(2,1)S(1)}, bf16[6,2304]{1,0:T(8,128)(2,1)S(1)}, u32[]{:S(2)}, u32[]{:S(2)}) collective-permute-start(bf16[6,2304]{1,0:T(8,128)(2,1)S(1)} %pad_maximum_fusion.14), channel_id=1, source_target_pairs={{0,8},{1,9},{2,10},{3,11},{4,12},{5,13},{6,14},{7,15},{8,0},{9,1},... | collective-permute-start | bytes 82952 | tf_op jit(solution)/shard_map/ppermute | solution.py:18
  6.9 1.9 %collective-permute-done.1 = bf16[6,2304]{1,0:T(8,128)(2,1)S(1)} collective-permute-done((bf16[6,2304]{1,0:T(8,128)(2,1)S(1)}, bf16[6,2304]{1,0:T(8,128)(2,1)S(1)}, u32[]{:S(2)}, u32[]{:S(2)}) %collective-permute-start.1) | collective-permute-done | bytes 27680 | tf_op jit(solution)/shard_map/ppermute | solution.py:18
  8.9 2.0 %collective-permute-start.2 = (bf16[12,2304]{1,0:T(8,128)(2,1)S(1)}, bf16[12,2304]{1,0:T(8,128)(2,1)S(1)}, u32[]{:S(2)}, u32[]{:S(2)}) collective-permute-start(bf16[12,2304]{1,0:T(8,128)(2,1)S(1)} %pad_maximum_fusion.12), channel_id=1, source_target_pairs={{0,4},{1,5},{2,6},{3,7},{4,0},{5,1},{6,2},{7,3},{8,12},{9,13},{10,... | collective-permute-start | bytes 165896 | tf_op jit(solution)/shard_map/ppermute | solution.py:18
  10.9 2.4 %collective-permute-done.2 = bf16[12,2304]{1,0:T(8,128)(2,1)S(1)} collective-permute-done((bf16[12,2304]{1,0:T(8,128)(2,1)S(1)}, bf16[12,2304]{1,0:T(8,128)(2,1)S(1)}, u32[]{:S(2)}, u32[]{:S(2)}) %collective-permute-start.2) | collective-permute-done | bytes 55328 | tf_op jit(solution)/shard_map/ppermute | solution.py:18
  13.4 2.3 %collective-permute-start.3 = (bf16[24,1152]{1,0:T(8,128)(2,1)S(1)}, bf16[24,1152]{1,0:T(8,128)(2,1)S(1)}, u32[]{:S(2)}, u32[]{:S(2)}) collective-permute-start(bf16[24,1152]{1,0:T(8,128)(2,1)S(1)} %get-tuple-element.16), channel_id=1, source_target_pairs={{0,2},{1,3},{2,0},{3,1},{4,6},{5,7},{6,4},{7,5},{8,10},{9,11},{10,... | collective-permute-start | bytes 165896 | tf_op jit(solution)/shard_map/ppermute | solution.py:18
  15.8 1.6 %collective-permute-start.6 = (bf16[24,1152]{1,0:T(8,128)(2,1)S(1)}, bf16[24,1152]{1,0:T(8,128)(2,1)S(1)}, u32[]{:S(2)}, u32[]{:S(2)}) collective-permute-start(bf16[24,1152]{1,0:T(8,128)(2,1)S(1)} %get-tuple-element.15), channel_id=1, source_target_pairs={{0,1},{1,0},{2,3},{3,2},{4,5},{5,4},{6,7},{7,6},{8,9},{9,8},{10,11... | collective-permute-start | bytes 165896 | tf_op jit(solution)/shard_map/ppermute | solution.py:18
  17.9 2.1 %collective-permute-start.4 = (bf16[48,1152]{1,0:T(8,128)(2,1)S(1)}, bf16[48,1152]{1,0:T(8,128)(2,1)S(1)}, u32[]{:S(2)}, u32[]{:S(2)}) collective-permute-start(bf16[48,1152]{1,0:T(8,128)(2,1)S(1)} %pad_maximum_fusion.7), channel_id=1, source_target_pairs={{0,1},{1,0},{2,3},{3,2},{4,5},{5,4},{6,7},{7,6},{8,9},{9,8},{10,11... | collective-permute-start | bytes 331784 | tf_op jit(solution)/shard_map/ppermute | solution.py:18
  20.0 2.1 %collective-permute-start.7 = (bf16[48,1152]{1,0:T(8,128)(2,1)S(1)}, bf16[48,1152]{1,0:T(8,128)(2,1)S(1)}, u32[]{:S(2)}, u32[]{:S(2)}) collective-permute-start(bf16[48,1152]{1,0:T(8,128)(2,1)S(1)} %pad_maximum_fusion.8), channel_id=1, source_target_pairs={{0,2},{1,3},{2,0},{3,1},{4,6},{5,7},{6,4},{7,5},{8,10},{9,11},{10,... | collective-permute-start | bytes 331784 | tf_op jit(solution)/shard_map/ppermute | solution.py:18
  23.2 2.3 %fusion.80 = bf16[1,96,576]{2,1,0:T(8,128)(2,1)S(1)} fusion(bf16[2,1152,576]{1,2,0:T(8,128)(2,1)} %param.11, bf16[48,1152]{1,0:T(8,128)(2,1)S(1)} %collective-permute-done.4, bf16[24,1152]{1,0:T(8,128)(2,1)S(1)} %collective-permute-done.3, bf16[24,1152]{1,0:T(8,128)(2,1)S(1)} %get-tuple-element.16), kind=kOutput, calls=%fused_computation.55 | convolution fusion | flops 128120832 | bytes 1658880 | tf_op jit(solution)/shard_map/dot_general | solution.py:117
  26.2 2.6 %fusion.74 = bf16[1,96,576]{2,1,0:T(8,128)(2,1)S(1)} fusion(bf16[2,1152,576]{1,2,0:T(8,128)(2,1)} %param.11, bf16[24,1152]{1,0:T(8,128)(2,1)S(1)} %get-tuple-element.22, bf16[24,1152]{1,0:T(8,128)(2,1)S(1)} %collective-permute-done.6, bf16[24,1152]{1,0:T(8,128)(2,1)S(1)} %get-tuple-element.21, bf16[24,1152]{1,0:T(8,128)(2,1)S(1)} %get-tuple-element.15), kind=kOutput, calls=%fused_computation.53 | convolution fusion | flops 128342016 | bytes 1658880 | tf_op jit(solution)/shard_map/dot_general | solution.py:117
  28.9 1.5 %fusion.14 = f32[96,2048]{1,0:T(8,128)S(1)} fusion(bf16[2,2048,1152]{2,1,0:T(8,128)(2,1)S(1)} %copy-done.4, bf16[48,1152]{1,0:T(8,128)(2,1)S(1)} %collective-permute-done.4, bf16[24,1152]{1,0:T(8,128)(2,1)S(1)} %collective-permute-done.3, bf16[24,1152]{1,0:T(8,128)(2,1)S(1)} %get-tuple-element.16), kind=kOutput, calls=%fused_computation.14 | convolution fusion | flops 453648384 | bytes 5726208 | tf_op jit(solution)/shard_map/dot_general | solution.py:117
  31.1 1.5 %fusion.12 = f32[96,2048]{1,0:T(8,128)S(1)} fusion(bf16[2,2048,1152]{2,1,0:T(8,128)(2,1)S(1)} %copy-done.4, bf16[24,1152]{1,0:T(8,128)(2,1)S(1)} %get-tuple-element.22, bf16[24,1152]{1,0:T(8,128)(2,1)S(1)} %collective-permute-done.6, bf16[24,1152]{1,0:T(8,128)(2,1)S(1)} %get-tuple-element.21, bf16[24,1152]{1,0:T(8,128)(2,1)S(1)} %get-tuple-element.15), kind=kOutput, calls=%fused_computation.12 | convolution fusion | flops 453869568 | bytes 5726208 | tf_op jit(solution)/shard_map/dot_general | solution.py:117
  33.5 0.9 %fusion.24 = f32[96,1152]{1,0:T(8,128)S(1)} fusion(f32[96,1152]{1,0:T(8,128)S(1)} %fusion.50, bf16[96,2048]{1,0:T(8,128)(2,1)S(1)} %maximum_convert_fusion.1.active_0, bf16[3,2048,1152]{2,1,0:T(8,128)(2,1)S(1)} %bitcast.103), kind=kOutput, calls=%fused_computation.25 | convolution fusion | flops 453095424 | bytes 5996544 | tf_op jit(solution)/shard_map/dot_general | solution.py:117
  34.4 2.0 %collective-permute-start.10 = (bf16[48,1152]{1,0:T(8,128)(2,1)S(1)}, bf16[48,1152]{1,0:T(8,128)(2,1)S(1)}, u32[]{:S(2)}, u32[]{:S(2)}) collective-permute-start(bf16[48,1152]{1,0:T(8,128)(2,1)S(1)} %slice.294), channel_id=1, source_target_pairs={{0,1},{1,0},{2,3},{3,2},{4,5},{5,4},{6,7},{7,6},{8,9},{9,8},{10,11... | collective-permute-start | bytes 331784 | tf_op jit(solution)/shard_map/ppermute | solution.py:18
  38.8 1.9 %collective-permute-start.17 = (bf16[48,1152]{1,0:T(8,128)(2,1)S(1)}, bf16[48,1152]{1,0:T(8,128)(2,1)S(1)}, u32[]{:S(2)}, u32[]{:S(2)}) collective-permute-start(bf16[48,1152]{1,0:T(8,128)(2,1)S(1)} %pad_maximum_fusion.10), channel_id=1, source_target_pairs={{0,2},{1,3},{2,0},{3,1},{4,6},{5,7},{6,4},{7,5},{8,10},{9,11},{10,... | collective-permute-start | bytes 331784 | tf_op jit(solution)/shard_map/ppermute | solution.py:18
  40.8 2.9 %collective-permute-done.17 = bf16[48,1152]{1,0:T(8,128)(2,1)S(1)} collective-permute-done((bf16[48,1152]{1,0:T(8,128)(2,1)S(1)}, bf16[48,1152]{1,0:T(8,128)(2,1)S(1)}, u32[]{:S(2)}, u32[]{:S(2)}) %collective-permute-start.17) | collective-permute-done | bytes 110624 | tf_op jit(solution)/shard_map/ppermute | solution.py:18
  44.7 1.8 %collective-permute-start.11 = (bf16[24,1152]{1,0:T(8,128)(2,1)S(1)}, bf16[24,1152]{1,0:T(8,128)(2,1)S(1)}, u32[]{:S(2)}, u32[]{:S(2)}) collective-permute-start(bf16[24,1152]{1,0:T(8,128)(2,1)S(1)} %slice.296), channel_id=1, source_target_pairs={{0,2},{1,3},{2,0},{3,1},{4,6},{5,7},{6,4},{7,5},{8,10},{9,11},{10,... | collective-permute-start | bytes 165896 | tf_op jit(solution)/shard_map/ppermute | solution.py:18
  46.5 1.5 %collective-permute-done.18 = bf16[24,1152]{1,0:T(8,128)(2,1)S(1)} collective-permute-done((bf16[24,1152]{1,0:T(8,128)(2,1)S(1)}, bf16[24,1152]{1,0:T(8,128)(2,1)S(1)}, u32[]{:S(2)}, u32[]{:S(2)}) %collective-permute-start.18) | collective-permute-done | bytes 55328 | tf_op jit(solution)/shard_map/ppermute | solution.py:18
  48.0 1.5 %collective-permute-start.19 = (bf16[24,1152]{1,0:T(8,128)(2,1)S(1)}, bf16[24,1152]{1,0:T(8,128)(2,1)S(1)}, u32[]{:S(2)}, u32[]{:S(2)}) collective-permute-start(bf16[24,1152]{1,0:T(8,128)(2,1)S(1)} %fusion.115), channel_id=1, source_target_pairs={{0,4},{1,5},{2,6},{3,7},{4,0},{5,1},{6,2},{7,3},{8,12},{9,13},{10,... | collective-permute-start | bytes 165896 | tf_op jit(solution)/shard_map/ppermute | solution.py:18
  50.3 1.9 %collective-permute-done.19 = bf16[24,1152]{1,0:T(8,128)(2,1)S(1)} collective-permute-done((bf16[24,1152]{1,0:T(8,128)(2,1)S(1)}, bf16[24,1152]{1,0:T(8,128)(2,1)S(1)}, u32[]{:S(2)}, u32[]{:S(2)}) %collective-permute-start.19) | collective-permute-done | bytes 55328 | tf_op jit(solution)/shard_map/ppermute | solution.py:18
  52.3 3.1 %collective-permute-start.20 = (bf16[24,1152]{1,0:T(8,128)(2,1)S(1)}, bf16[24,1152]{1,0:T(8,128)(2,1)S(1)}, u32[]{:S(2)}, u32[]{:S(2)}) collective-permute-start(bf16[24,1152]{1,0:T(8,128)(2,1)S(1)} %get-tuple-element.9), channel_id=1, source_target_pairs={{0,8},{1,9},{2,10},{3,11},{4,12},{5,13},{6,14},{7,15},{8,0},{9,1},... | collective-permute-start | bytes 165896 | tf_op jit(solution)/shard_map/ppermute | solution.py:18
  55.4 1.4 %collective-permute-start.13 = (bf16[24,1152]{1,0:T(8,128)(2,1)S(1)}, bf16[24,1152]{1,0:T(8,128)(2,1)S(1)}, u32[]{:S(2)}, u32[]{:S(2)}) collective-permute-start(bf16[24,1152]{1,0:T(8,128)(2,1)S(1)} %get-tuple-element.7), channel_id=1, source_target_pairs={{0,8},{1,9},{2,10},{3,11},{4,12},{5,13},{6,14},{7,15},{8,0},{9,1},... | collective-permute-start | bytes 165896 | tf_op jit(solution)/shard_map/ppermute | solution.py:18
  57.5 1.0 %collective-permute-start.21 = (bf16[24,1152]{1,0:T(8,128)(2,1)S(1)}, bf16[24,1152]{1,0:T(8,128)(2,1)S(1)}, u32[]{:S(2)}, u32[]{:S(2)}) collective-permute-start(bf16[24,1152]{1,0:T(8,128)(2,1)S(1)} %shard_map.105), channel_id=1, source_target_pairs={{0,1},{1,0},{2,3},{3,2},{4,5},{5,4},{6,7},{7,6},{8,9},{9,8},{10,11... | collective-permute-start | bytes 165896 | tf_op jit(solution)/shard_map/ppermute | solution.py:18
  58.5 2.0 %collective-permute-done.13.received_ref = bf16[24,1152]{1,0:T(8,128)(2,1)S(1)} collective-permute-done((bf16[24,1152]{1,0:T(8,128)(2,1)S(1)}, bf16[24,1152]{1,0:T(8,128)(2,1)S(1)}, u32[]{:S(2)}, u32[]{:S(2)}) %collective-permute-start.13) | collective-permute-done | bytes 55328 | tf_op jit(solution)/shard_map/ppermute | solution.py:18
  60.5 1.1 %collective-permute-start.14 = (bf16[24,1152]{1,0:T(8,128)(2,1)S(1)}, bf16[24,1152]{1,0:T(8,128)(2,1)S(1)}, u32[]{:S(2)}, u32[]{:S(2)}) collective-permute-start(bf16[24,1152]{1,0:T(8,128)(2,1)S(1)} %shard_map.104), channel_id=1, source_target_pairs={{0,2},{1,3},{2,0},{3,1},{4,6},{5,7},{6,4},{7,5},{8,10},{9,11},{10,... | collective-permute-start | bytes 165896 | tf_op jit(solution)/shard_map/ppermute | solution.py:18
  62.3 1.9 %collective-permute-start.22 = (bf16[48,1152]{1,0:T(8,128)(2,1)S(1)}, bf16[48,1152]{1,0:T(8,128)(2,1)S(1)}, u32[]{:S(2)}, u32[]{:S(2)}) collective-permute-start(bf16[48,1152]{1,0:T(8,128)(2,1)S(1)} %pad_maximum_fusion.11), channel_id=1, source_target_pairs={{0,2},{1,3},{2,0},{3,1},{4,6},{5,7},{6,4},{7,5},{8,10},{9,11},{10,... | collective-permute-start | bytes 331784 | tf_op jit(solution)/shard_map/ppermute | solution.py:18
  65.3 1.8 %collective-permute-done.22 = bf16[48,1152]{1,0:T(8,128)(2,1)S(1)} collective-permute-done((bf16[48,1152]{1,0:T(8,128)(2,1)S(1)}, bf16[48,1152]{1,0:T(8,128)(2,1)S(1)}, u32[]{:S(2)}, u32[]{:S(2)}) %collective-permute-start.22) | collective-permute-done | bytes 110624 | tf_op jit(solution)/shard_map/ppermute | solution.py:18
  67.1 1.5 %fusion.42 = bf16[1,96,2048]{2,1,0:T(8,128)(2,1)S(1)} fusion(bf16[3,2048,1152]{2,1,0:T(8,128)(2,1)S(1)} %bitcast.103, bf16[24,1152]{1,0:T(8,128)(2,1)S(1)} %get-tuple-element.20, bf16[24,1152]{1,0:T(8,128)(2,1)S(1)} %collective-permute-done.21, bf16[24,1152]{1,0:T(8,128)(2,1)S(1)} %get-tuple-element.19, bf16[24,1152]{1,0:T(8,128)(2,1)S(1)} %shard_map.105), kind=kOutput, calls=%fused_computation.31 | convolution fusion | flops 454066176 | bytes 5332992 | tf_op jit(solution)/shard_map/dot_general | solution.py:117
  68.7 1.5 %fusion.4 = f32[96,2048]{1,0:T(8,128)S(1)} fusion(bf16[3,2048,1152]{2,1,0:T(8,128)(2,1)S(1)} %bitcast.103, bf16[24,1152]{1,0:T(8,128)(2,1)S(1)} %get-tuple-element.20, bf16[24,1152]{1,0:T(8,128)(2,1)S(1)} %collective-permute-done.21, bf16[24,1152]{1,0:T(8,128)(2,1)S(1)} %get-tuple-element.19, bf16[24,1152]{1,0:T(8,128)(2,1)S(1)} %shard_map.105), kind=kOutput, calls=%fused_computation.4 | convolution fusion | flops 453869568 | bytes 5726208 | tf_op jit(solution)/shard_map/dot_general | solution.py:117
  70.2 1.6 %fusion.39 = bf16[1,96,2048]{2,1,0:T(8,128)(2,1)S(1)} fusion(f32[96,2048]{1,0:T(8,128)S(1)} %fusion.4, bf16[3,2048,1152]{2,1,0:T(8,128)(2,1)S(1)} %bitcast.103, bf16[48,1152]{1,0:T(8,128)(2,1)S(1)} %collective-permute-done.15, bf16[24,1152]{1,0:T(8,128)(2,1)S(1)} %collective-permute-done.14, bf16[24,1152]{1,0:T(8,128)(2,1)S(1)} %shard_map.104), kind=kOutput, calls=%fused_computation.30 | convolution fusion | flops 454041600 | bytes 6119424 | tf_op jit(solution)/shard_map/dot_general | solution.py:117
  72.0 5.6 %shard_map.107 = bf16[3,2048,1152]{2,1,0:T(8,128)(2,1)} custom-call(bf16[96,2048]{1,0:T(8,128)(2,1)S(1)} %maximum_convert_fusion.1.active_0, bf16[96,2048]{1,0:T(8,128)(2,1)S(1)} %maximum_convert_fusion.active_1, bf16[96,1152]{1,0:T(8,128)(2,1)S(1)} %pad_maximum_fusion.5.errors_0, bf16[96,1152]{1,0:T(8,128)(2,1)S(1)} %pad_maximum_fusion.6.errors_1), custom_call_target="tpu_custom_call" | custom-call | flops 1358954496 | bytes 14155776 | tf_op jit(solution)/shard_map/pallas_call | solution.py:145
  77.7 4.7 %shard_map.106 = (bf16[2,2048,1152]{2,1,0:T(8,128)(2,1)}, f32[2,2048]{1,0:T(2,128)}) custom-call(bf16[96,2048]{1,0:T(8,128)(2,1)S(1)} %maximum_convert_fusion.1.active_0, bf16[96,2048]{1,0:T(8,128)(2,1)S(1)} %maximum_convert_fusion.active_1, bf16[2,96,2048]{2,1,0:T(8,128)(2,1)S(1)} %pad_maximum_fusion.own_ref, ...), custom_call_target="tpu_custom_call" | custom-call | flops 905969664 | bytes 9437184 | tf_op jit(solution)/shard_map/pallas_call | solution.py:183
  (95 shorter events, 13.1 us)
Async XLA Ops:
  1.4 14.4 %copy-start.2 = (f32[2,2048]{1,0:T(2,128)S(1)}, f32[2,2048]{1,0:T(2,128)}, u32[]{:S(2)}) copy-start(f32[2,2048]{1,0:T(2,128)} %param.14) | copy-start | bytes 49156
  1.4 21.3 %copy-start.5 = (bf16[2,1152,576]{1,2,0:T(8,128)(2,1)S(1)}, bf16[2,1152,576]{1,2,0:T(8,128)(2,1)}, u32[]{:S(2)}) copy-start(bf16[2,1152,576]{1,2,0:T(8,128)(2,1)} %param.10) | copy-start | bytes 7962628
  1.5 1.3 %collective-permute-start = (f32[2,6]{1,0:T(2,128)S(1)}, f32[2,6]{1,0:T(2,128)S(1)}, u32[]{:S(2)}, u32[]{:S(2)}) collective-permute-start(f32[2,6]{1,0:T(2,128)S(1)} %shard_map.103), channel_id=1, source_target_pairs={{0,16},{16,0},{1,17},{17,1},{2,18},{18,2},{3,19},{19,3},{4,20},{20... | collective-permute-start | bytes 152 | tf_op jit(solution)/shard_map/ppermute | solution.py:18
  2.9 5.9 %collective-permute-start.1 = (bf16[6,2304]{1,0:T(8,128)(2,1)S(1)}, bf16[6,2304]{1,0:T(8,128)(2,1)S(1)}, u32[]{:S(2)}, u32[]{:S(2)}) collective-permute-start(bf16[6,2304]{1,0:T(8,128)(2,1)S(1)} %pad_maximum_fusion.14), channel_id=1, source_target_pairs={{0,8},{1,9},{2,10},{3,11},{4,12},{5,13},{6,14},{7,15},{8,0},{9,1},... | collective-permute-start | bytes 82952 | tf_op jit(solution)/shard_map/ppermute | solution.py:18
  8.9 4.4 %collective-permute-start.2 = (bf16[12,2304]{1,0:T(8,128)(2,1)S(1)}, bf16[12,2304]{1,0:T(8,128)(2,1)S(1)}, u32[]{:S(2)}, u32[]{:S(2)}) collective-permute-start(bf16[12,2304]{1,0:T(8,128)(2,1)S(1)} %pad_maximum_fusion.12), channel_id=1, source_target_pairs={{0,4},{1,5},{2,6},{3,7},{4,0},{5,1},{6,2},{7,3},{8,12},{9,13},{10,... | collective-permute-start | bytes 165896 | tf_op jit(solution)/shard_map/ppermute | solution.py:18
  13.4 4.4 %collective-permute-start.3 = (bf16[24,1152]{1,0:T(8,128)(2,1)S(1)}, bf16[24,1152]{1,0:T(8,128)(2,1)S(1)}, u32[]{:S(2)}, u32[]{:S(2)}) collective-permute-start(bf16[24,1152]{1,0:T(8,128)(2,1)S(1)} %get-tuple-element.16), channel_id=1, source_target_pairs={{0,2},{1,3},{2,0},{3,1},{4,6},{5,7},{6,4},{7,5},{8,10},{9,11},{10,... | collective-permute-start | bytes 165896 | tf_op jit(solution)/shard_map/ppermute | solution.py:18
  15.8 4.2 %collective-permute-start.6 = (bf16[24,1152]{1,0:T(8,128)(2,1)S(1)}, bf16[24,1152]{1,0:T(8,128)(2,1)S(1)}, u32[]{:S(2)}, u32[]{:S(2)}) collective-permute-start(bf16[24,1152]{1,0:T(8,128)(2,1)S(1)} %get-tuple-element.15), channel_id=1, source_target_pairs={{0,1},{1,0},{2,3},{3,2},{4,5},{5,4},{6,7},{7,6},{8,9},{9,8},{10,11... | collective-permute-start | bytes 165896 | tf_op jit(solution)/shard_map/ppermute | solution.py:18
  17.9 4.8 %collective-permute-start.4 = (bf16[48,1152]{1,0:T(8,128)(2,1)S(1)}, bf16[48,1152]{1,0:T(8,128)(2,1)S(1)}, u32[]{:S(2)}, u32[]{:S(2)}) collective-permute-start(bf16[48,1152]{1,0:T(8,128)(2,1)S(1)} %pad_maximum_fusion.7), channel_id=1, source_target_pairs={{0,1},{1,0},{2,3},{3,2},{4,5},{5,4},{6,7},{7,6},{8,9},{9,8},{10,11... | collective-permute-start | bytes 331784 | tf_op jit(solution)/shard_map/ppermute | solution.py:18
  20.0 5.6 %collective-permute-start.7 = (bf16[48,1152]{1,0:T(8,128)(2,1)S(1)}, bf16[48,1152]{1,0:T(8,128)(2,1)S(1)}, u32[]{:S(2)}, u32[]{:S(2)}) collective-permute-start(bf16[48,1152]{1,0:T(8,128)(2,1)S(1)} %pad_maximum_fusion.8), channel_id=1, source_target_pairs={{0,2},{1,3},{2,0},{3,1},{4,6},{5,7},{6,4},{7,5},{8,10},{9,11},{10,... | collective-permute-start | bytes 331784 | tf_op jit(solution)/shard_map/ppermute | solution.py:18
  22.1 6.8 %copy-start.4 = (bf16[2,2048,1152]{2,1,0:T(8,128)(2,1)S(1)}, bf16[2,2048,1152]{2,1,0:T(8,128)(2,1)}, u32[]{:S(2)}) copy-start(bf16[2,2048,1152]{2,1,0:T(8,128)(2,1)} %param.13) | copy-start | bytes 28311556
  22.7 10.7 %slice-start = ((s8[14155776]{0:T(1024)(128)(4,1)}), s8[4194304]{0:T(1024)(128)(4,1)S(1)}, s32[]{:S(2)}) async-start(s8[14155776]{0:T(1024)(128)(4,1)} %bitcast.102), calls=%async_computation | async-start | bytes 8388608
  25.6 7.2 %collective-permute-start.9 = (bf16[2,96,576]{2,1,0:T(8,128)(2,1)S(1)}, bf16[2,96,576]{2,1,0:T(8,128)(2,1)S(1)}, u32[]{:S(2)}, u32[]{:S(2)}) collective-permute-start(bf16[2,96,576]{2,1,0:T(8,128)(2,1)S(1)} %pad_maximum_fusion.1), channel_id=1, source_target_pairs={{0,16},{16,0},{1,17},{17,1},{2,18},{18,2},{3,19},{19,3},{4,20},{20... | collective-permute-start | bytes 663560 | tf_op jit(solution)/shard_map/ppermute | solution.py:18
  25.7 7.8 %slice-start.1 = ((s8[14155776]{0:T(1024)(128)(4,1)}), s8[4194304]{0:T(1024)(128)(4,1)S(1)}, s32[]{:S(2)}) async-start(s8[14155776]{0:T(1024)(128)(4,1)} %bitcast.102), calls=%async_computation.1 | async-start | bytes 8388608
  28.8 4.6 %slice-start.2 = ((s8[14155776]{0:T(1024)(128)(4,1)}), s8[4194304]{0:T(1024)(128)(4,1)S(1)}, s32[]{:S(2)}) async-start(s8[14155776]{0:T(1024)(128)(4,1)} %bitcast.102), calls=%async_computation.2 | async-start | bytes 8388608
  28.9 3.9 %collective-permute-start.16 = (bf16[2,96,576]{2,1,0:T(8,128)(2,1)S(1)}, bf16[2,96,576]{2,1,0:T(8,128)(2,1)S(1)}, u32[]{:S(2)}, u32[]{:S(2)}) collective-permute-start(bf16[2,96,576]{2,1,0:T(8,128)(2,1)S(1)} %pad_maximum_fusion.2), channel_id=1, source_target_pairs={{0,16},{16,0},{1,17},{17,1},{2,18},{18,2},{3,19},{19,3},{4,20},{20... | collective-permute-start | bytes 663560 | tf_op jit(solution)/shard_map/ppermute | solution.py:18
  30.5 2.4 %copy-start = (bf16[2,576,1152]{2,1,0:T(8,128)(2,1)S(1)}, bf16[2,576,1152]{2,1,0:T(8,128)(2,1)}, u32[]{:S(2)}) copy-start(bf16[2,576,1152]{2,1,0:T(8,128)(2,1)} %param.12) | copy-start | bytes 7962628
  30.5 2.9 %slice-start.3 = ((s8[14155776]{0:T(1024)(128)(4,1)}), s8[1572864]{0:T(1024)(128)(4,1)S(1)}, s32[]{:S(2)}) async-start(s8[14155776]{0:T(1024)(128)(4,1)} %bitcast.102), calls=%async_computation.3 | async-start | bytes 3145728
  30.5 2.8 %collective-permute-start.5 = (f32[96,2048]{1,0:T(8,128)S(1)}, f32[96,2048]{1,0:T(8,128)S(1)}, u32[]{:S(2)}, u32[]{:S(2)}) collective-permute-start(f32[96,2048]{1,0:T(8,128)S(1)} %fusion.14), channel_id=1, source_target_pairs={{0,16},{16,0},{1,17},{17,1},{2,18},{18,2},{3,19},{19,3},{4,20},{20... | collective-permute-start | bytes 2359304 | tf_op jit(solution)/shard_map/ppermute | solution.py:18
  32.6 3.8 %collective-permute-start.8 = (f32[96,2048]{1,0:T(8,128)S(1)}, f32[96,2048]{1,0:T(8,128)S(1)}, u32[]{:S(2)}, u32[]{:S(2)}) collective-permute-start(f32[96,2048]{1,0:T(8,128)S(1)} %fusion.12), channel_id=1, source_target_pairs={{0,16},{16,0},{1,17},{17,1},{2,18},{18,2},{3,19},{19,3},{4,20},{20... | collective-permute-start | bytes 2359304 | tf_op jit(solution)/shard_map/ppermute | solution.py:18
  34.4 10.2 %collective-permute-start.10 = (bf16[48,1152]{1,0:T(8,128)(2,1)S(1)}, bf16[48,1152]{1,0:T(8,128)(2,1)S(1)}, u32[]{:S(2)}, u32[]{:S(2)}) collective-permute-start(bf16[48,1152]{1,0:T(8,128)(2,1)S(1)} %slice.294), channel_id=1, source_target_pairs={{0,1},{1,0},{2,3},{3,2},{4,5},{5,4},{6,7},{7,6},{8,9},{9,8},{10,11... | collective-permute-start | bytes 331784 | tf_op jit(solution)/shard_map/ppermute | solution.py:18
  38.8 4.9 %collective-permute-start.17 = (bf16[48,1152]{1,0:T(8,128)(2,1)S(1)}, bf16[48,1152]{1,0:T(8,128)(2,1)S(1)}, u32[]{:S(2)}, u32[]{:S(2)}) collective-permute-start(bf16[48,1152]{1,0:T(8,128)(2,1)S(1)} %pad_maximum_fusion.10), channel_id=1, source_target_pairs={{0,2},{1,3},{2,0},{3,1},{4,6},{5,7},{6,4},{7,5},{8,10},{9,11},{10,... | collective-permute-start | bytes 331784 | tf_op jit(solution)/shard_map/ppermute | solution.py:18
  43.8 4.2 %collective-permute-start.18 = (bf16[24,1152]{1,0:T(8,128)(2,1)S(1)}, bf16[24,1152]{1,0:T(8,128)(2,1)S(1)}, u32[]{:S(2)}, u32[]{:S(2)}) collective-permute-start(bf16[24,1152]{1,0:T(8,128)(2,1)S(1)} %slice.295), channel_id=1, source_target_pairs={{0,1},{1,0},{2,3},{3,2},{4,5},{5,4},{6,7},{7,6},{8,9},{9,8},{10,11... | collective-permute-start | bytes 165896 | tf_op jit(solution)/shard_map/ppermute | solution.py:18
  44.7 4.8 %collective-permute-start.11 = (bf16[24,1152]{1,0:T(8,128)(2,1)S(1)}, bf16[24,1152]{1,0:T(8,128)(2,1)S(1)}, u32[]{:S(2)}, u32[]{:S(2)}) collective-permute-start(bf16[24,1152]{1,0:T(8,128)(2,1)S(1)} %slice.296), channel_id=1, source_target_pairs={{0,2},{1,3},{2,0},{3,1},{4,6},{5,7},{6,4},{7,5},{8,10},{9,11},{10,... | collective-permute-start | bytes 165896 | tf_op jit(solution)/shard_map/ppermute | solution.py:18
  48.0 4.2 %collective-permute-start.19 = (bf16[24,1152]{1,0:T(8,128)(2,1)S(1)}, bf16[24,1152]{1,0:T(8,128)(2,1)S(1)}, u32[]{:S(2)}, u32[]{:S(2)}) collective-permute-start(bf16[24,1152]{1,0:T(8,128)(2,1)S(1)} %fusion.115), channel_id=1, source_target_pairs={{0,4},{1,5},{2,6},{3,7},{4,0},{5,1},{6,2},{7,3},{8,12},{9,13},{10,... | collective-permute-start | bytes 165896 | tf_op jit(solution)/shard_map/ppermute | solution.py:18
  49.5 5.8 %collective-permute-start.12 = (bf16[24,1152]{1,0:T(8,128)(2,1)S(1)}, bf16[24,1152]{1,0:T(8,128)(2,1)S(1)}, u32[]{:S(2)}, u32[]{:S(2)}) collective-permute-start(bf16[24,1152]{1,0:T(8,128)(2,1)S(1)} %fusion.114), channel_id=1, source_target_pairs={{0,4},{1,5},{2,6},{3,7},{4,0},{5,1},{6,2},{7,3},{8,12},{9,13},{10,... | collective-permute-start | bytes 165896 | tf_op jit(solution)/shard_map/ppermute | solution.py:18
  52.3 5.2 %collective-permute-start.20 = (bf16[24,1152]{1,0:T(8,128)(2,1)S(1)}, bf16[24,1152]{1,0:T(8,128)(2,1)S(1)}, u32[]{:S(2)}, u32[]{:S(2)}) collective-permute-start(bf16[24,1152]{1,0:T(8,128)(2,1)S(1)} %get-tuple-element.9), channel_id=1, source_target_pairs={{0,8},{1,9},{2,10},{3,11},{4,12},{5,13},{6,14},{7,15},{8,0},{9,1},... | collective-permute-start | bytes 165896 | tf_op jit(solution)/shard_map/ppermute | solution.py:18
  55.4 5.1 %collective-permute-start.13 = (bf16[24,1152]{1,0:T(8,128)(2,1)S(1)}, bf16[24,1152]{1,0:T(8,128)(2,1)S(1)}, u32[]{:S(2)}, u32[]{:S(2)}) collective-permute-start(bf16[24,1152]{1,0:T(8,128)(2,1)S(1)} %get-tuple-element.7), channel_id=1, source_target_pairs={{0,8},{1,9},{2,10},{3,11},{4,12},{5,13},{6,14},{7,15},{8,0},{9,1},... | collective-permute-start | bytes 165896 | tf_op jit(solution)/shard_map/ppermute | solution.py:18
  57.5 4.8 %collective-permute-start.21 = (bf16[24,1152]{1,0:T(8,128)(2,1)S(1)}, bf16[24,1152]{1,0:T(8,128)(2,1)S(1)}, u32[]{:S(2)}, u32[]{:S(2)}) collective-permute-start(bf16[24,1152]{1,0:T(8,128)(2,1)S(1)} %shard_map.105), channel_id=1, source_target_pairs={{0,1},{1,0},{2,3},{3,2},{4,5},{5,4},{6,7},{7,6},{8,9},{9,8},{10,11... | collective-permute-start | bytes 165896 | tf_op jit(solution)/shard_map/ppermute | solution.py:18
  60.5 4.2 %collective-permute-start.14 = (bf16[24,1152]{1,0:T(8,128)(2,1)S(1)}, bf16[24,1152]{1,0:T(8,128)(2,1)S(1)}, u32[]{:S(2)}, u32[]{:S(2)}) collective-permute-start(bf16[24,1152]{1,0:T(8,128)(2,1)S(1)} %shard_map.104), channel_id=1, source_target_pairs={{0,2},{1,3},{2,0},{3,1},{4,6},{5,7},{6,4},{7,5},{8,10},{9,11},{10,... | collective-permute-start | bytes 165896 | tf_op jit(solution)/shard_map/ppermute | solution.py:18
  62.3 4.8 %collective-permute-start.22 = (bf16[48,1152]{1,0:T(8,128)(2,1)S(1)}, bf16[48,1152]{1,0:T(8,128)(2,1)S(1)}, u32[]{:S(2)}, u32[]{:S(2)}) collective-permute-start(bf16[48,1152]{1,0:T(8,128)(2,1)S(1)} %pad_maximum_fusion.11), channel_id=1, source_target_pairs={{0,2},{1,3},{2,0},{3,1},{4,6},{5,7},{6,4},{7,5},{8,10},{9,11},{10,... | collective-permute-start | bytes 331784 | tf_op jit(solution)/shard_map/ppermute | solution.py:18
  64.7 5.5 %collective-permute-start.15 = (bf16[48,1152]{1,0:T(8,128)(2,1)S(1)}, bf16[48,1152]{1,0:T(8,128)(2,1)S(1)}, u32[]{:S(2)}, u32[]{:S(2)}) collective-permute-start(bf16[48,1152]{1,0:T(8,128)(2,1)S(1)} %pad_maximum_fusion.9), channel_id=1, source_target_pairs={{0,1},{1,0},{2,3},{3,2},{4,5},{5,4},{6,7},{7,6},{8,9},{9,8},{10,11... | collective-permute-start | bytes 331784 | tf_op jit(solution)/shard_map/ppermute | solution.py:18
  71.9 5.8 %collective-permute-start.23 = (bf16[2,96,2048]{2,1,0:T(8,128)(2,1)S(1)}, bf16[2,96,2048]{2,1,0:T(8,128)(2,1)S(1)}, u32[]{:S(2)}, u32[]{:S(2)}) collective-permute-start(bf16[2,96,2048]{2,1,0:T(8,128)(2,1)S(1)} %pad_maximum_fusion.own_ref), channel_id=1, source_target_pairs={{0,16},{16,0},{1,17},{17,1},{2,18},{18,2},{3,19},{19,3},{4,20},{20... | collective-permute-start | bytes 2359304 | tf_op jit(solution)/shard_map/ppermute | solution.py:18
  (2 other events, 2.9 us)

commit v3 on v2

--- a/solution.py
+++ b/solution.py
@@ -7,6 +7,7 @@
 from jax.experimental.pallas import tpu as pltpu
 from jax.sharding import PartitionSpec as P
 
+
 D = 2304
 
 
@@ -23,10 +24,9 @@
     return [1 << k for k in range(size.bit_length() - 1)]
 
 
-def mp_sum(values, wire=None):
+def mp_sum(values):
     for bit in bits_of("mp"):
-        sent = values if wire is None else values.astype(wire)
-        values = values + swap(sent, "mp", bit).astype(values.dtype)
+        values = values + swap(values, "mp", bit)
     return values
 
 
@@ -36,20 +36,50 @@
 
 def gather_inner(block):
     place = lax.axis_index("feat")
-    for bit in reversed(bits_of("feat")[2:]):
-        other = swap(block, "feat", bit)
-        upper = (place & bit) > 0
-        block = join(jnp.where(upper, other, block), jnp.where(upper, block, other))
-    return block
-
-
-def gather_outer(quarter, layer):
+    bits = bits_of("feat")[2:]
+    if len(bits) != 2:
+        for bit in reversed(bits):
+            other = swap(block, "feat", bit)
+            upper = (place & bit) > 0
+            block = join(jnp.where(upper, other, block), jnp.where(upper, block, other))
+        return block
+    low, high = bits
+    far, both, near = (swap(block, "feat", b) for b in (high, high | low, low))
+    at_low, at_high = (place & low) > 0, (place & high) > 0
+
+    def pick(l, h):
+        same_low = jnp.where(at_high == h, block, far)
+        other_low = jnp.where(at_high == h, near, both)
+        return jnp.where(at_low == l, same_low, other_low)
+
+    return join(pick(False, False), pick(False, True), pick(True, False), pick(True, True))
+
+
+def stack_rows(upper, lower, flops):
+    rows, cols = upper.shape
+
+    def kernel(upper_ref, lower_ref, out_ref):
+        out_ref[:rows] = upper_ref[...]
+        out_ref[rows:] = lower_ref[...]
+
+    return pl.pallas_call(
+        kernel,
+        out_shape=jax.ShapeDtypeStruct((2 * rows, cols), upper.dtype),
+        in_specs=[pl.BlockSpec(memory_space=pltpu.VMEM)] * 2,
+        out_specs=pl.BlockSpec(memory_space=pltpu.VMEM),
+        compiler_params=pltpu.CompilerParams(vmem_limit_bytes=4 << 20),
+        cost_estimate=pl.CostEstimate(flops=flops, bytes_accessed=1 << 16, transcendentals=0),
+    )(upper, lower)
+
+
+def gather_outer(quarter, layer, flops):
     rows = quarter.shape[0]
+    near, far = ((2, 1), (1, 2))[layer]
+    across = swap(quarter, "feat", near)
+    half = stack_rows(quarter, across, flops) if flops else join(quarter, across)
+    other = swap(half, "feat", far)
     if layer == 0:
-        half = join(quarter, swap(quarter, "feat", 2))
-        return join(half, swap(half, "feat", 1))
-    across = swap(quarter, "feat", 1)
-    other = swap(join(quarter, across), "feat", 2)
+        return join(half, other)
     return join(quarter, other[:rows], across, other[rows:])
 
 
@@ -57,23 +87,27 @@
     return kept + swap(sent.astype(jnp.bfloat16), "feat", bit).astype(jnp.float32)
 
 
-def scatter_outer(values, layer):
+def sum_tokens(values, layer):
     rows = values.shape[0] // 4
     own, second, first, both = (values[k * rows : (k + 1) * rows] for k in range(4))
     if layer == 0:
         half = send_add(values[: 2 * rows], values[2 * rows :], 1)
-        return send_add(half[:rows], half[rows:], 2)
-    half = send_add(join(own, first), join(second, both), 2)
-    return send_add(half[:rows], half[rows:], 1)
-
-
-def sum_inner(quarter):
+        quarter = send_add(half[:rows], half[rows:], 2)
+    else:
+        half = send_add(join(own, first), join(second, both), 2)
+        quarter = send_add(half[:rows], half[rows:], 1)
     bits = bits_of("feat")[2:]
+    if len(bits) == 2:
+        sent = quarter.astype(jnp.bfloat16)
+        offsets = (bits[1], bits[0] | bits[1], bits[0])
+        received = [swap(sent, "feat", b) for b in offsets]
+        for other in received[:-1]:
+            quarter = quarter + other.astype(jnp.float32)
+        return add_round(quarter, received[-1], int(4e10))
     for bit in bits:
         received = swap(quarter.astype(jnp.bfloat16), "feat", bit)
-        if bit == bits[-1]:
-            return add_round(quarter, received, int(4e10))
         quarter = quarter + received.astype(jnp.float32)
+    return quarter.astype(jnp.bfloat16)
 
 
 def square_sums(values, flops):
@@ -122,40 +156,47 @@
 nt = ((1,), (1,))
 
 
-def decoder_gradient(active, errors, scale):
-    tokens, features = active[0].shape
-    cols = errors[0].shape[1]
-    picks = [(0, 0), (0, 1), (1, 1)]
+def decoder_gradient(lefts, right, scale, slots, into=None):
+    tokens, features = lefts[0].shape
+    cols = right.shape[1]
+    count = len(lefts)
     chunks = row_chunks(features, 256)
 
-    def kernel(active_0, active_1, errors_0, errors_1, out_ref, held, sems):
-        actives, error_refs = (active_0, active_1), (errors_0, errors_1)
+    def kernel(*refs):
+        left_refs, right_ref = refs[:count], refs[count]
+        out_ref, held, sems = refs[-3:]
+        right_value = right_ref[...]
         copies = []
-        for k, (a, e) in enumerate(picks):
-            right = error_refs[e][...]
+        for k, left_ref in enumerate(left_refs):
             for c, (at, size) in enumerate(chunks):
                 rows = pl.ds(at, size)
-                held[k, rows] = (scale * dot(actives[a][:, rows], right, tn)).astype(jnp.bfloat16)
-                copies.append(pltpu.make_async_copy(held.at[k, rows], out_ref.at[k, rows], sems.at[k, c]))
+                held[k, rows] = (scale * dot(left_ref[:, rows], right_value, tn)).astype(jnp.bfloat16)
+                target = out_ref.at[slots[k], rows]
+                copies.append(pltpu.make_async_copy(held.at[k, rows], target, sems.at[k, c]))
                 copies[-1].start()
         for copy in copies:
             copy.wait()
 
     vmem = pl.BlockSpec(memory_space=pltpu.VMEM)
+    hbm = pl.BlockSpec(memory_space=pl.ANY)
+    more = () if into is None else (into,)
     return pl.pallas_call(
         kernel,
         out_shape=jax.ShapeDtypeStruct((3, features, cols), jnp.bfloat16),
-        in_specs=[vmem] * 4,
-        out_specs=pl.BlockSpec(memory_space=pl.ANY),
+        in_specs=[vmem] * (count + 1) + [hbm] * len(more),
+        out_specs=hbm,
+        input_output_aliases={count + 1: 0} if more else {},
         scratch_shapes=[
-            pltpu.VMEM((3, features, cols), jnp.bfloat16),
-            pltpu.SemaphoreType.DMA((3, len(chunks))),
+            pltpu.VMEM((count, features, cols), jnp.bfloat16),
+            pltpu.SemaphoreType.DMA((count, len(chunks))),
         ],
-        compiler_params=pltpu.CompilerParams(vmem_limit_bytes=24 << 20),
+        compiler_params=pltpu.CompilerParams(vmem_limit_bytes=(8 + 8 * count) << 20),
         cost_estimate=pl.CostEstimate(
-            flops=6 * tokens * features * cols, bytes_accessed=6 * features * cols, transcendentals=0
-        ),
-    )(*active, *errors)
+            flops=2 * count * tokens * features * cols,
+            bytes_accessed=2 * count * features * cols,
+            transcendentals=0,
+        ),
+    )(*lefts, right, *more)
 
 
 def encoder_gradient(active, own, received, normed, scale):
@@ -206,7 +247,7 @@
     normed_local = (values * inverse_rms[:, :, None] * norm_gain[:, None, :]).astype(jnp.bfloat16)
     model_cols = decoder.shape[2]
     quarter = gather_inner(jnp.concatenate([normed_local[0], normed_local[1]], axis=1))
-    normed = [gather_outer(quarter[:, l * model_cols : (l + 1) * model_cols], l) for l in range(2)]
+    normed = [gather_outer(quarter[:, l * model_cols : (l + 1) * model_cols], l, int(4e10)) for l in range(2)]
     tokens = normed[0].shape[0]
     active = []
     target = []
@@ -218,23 +259,22 @@
         mlp = mp_sum(jnp.stack([gate_part, up_part]).astype(jnp.bfloat16)).astype(jnp.float32)
         hidden = (jax.nn.gelu(mlp[0], approximate=True) * mlp[1]).astype(jnp.bfloat16)
         target.append(dot(hidden, down_weight[l], nn))
-    partial = [
-        dot(active[0], decoder[0], nn) - target[0],
-        dot(active[0], decoder[1], nn) + dot(active[1], decoder[2], nn) - target[1],
-    ]
-    errors = [
-        gather_outer(sum_inner(scatter_outer(partial[l], l)), l)
-        for l in range(2)
-    ]
-    back_first = dot(errors[0], decoder[0], nt) + dot(errors[1], decoder[1], nt)
+    partial_first = dot(active[0], decoder[0], nn) - target[0]
+    partial_second = (
+        dot(active[0], decoder[1], nn) + dot(active[1], decoder[2], nn) - target[1]
+    )
+    loss_scale = 1.0 / math.sqrt(tokens)
+    errors = [gather_outer(sum_tokens(partial_first, 0), 0, 0), gather_outer(sum_tokens(partial_second, 1), 1, 0)]
+    grad_decoder = decoder_gradient([active[0]], errors[0], loss_scale, (0,))
+    back_first = lax.optimization_barrier(dot(errors[0], decoder[0], nt))
+    back_first = back_first + dot(errors[1], decoder[1], nt)
     back_second = dot(errors[1], decoder[2], nt)
-    loss_scale = 1.0 / math.sqrt(tokens)
     own = jnp.stack([back_first, back_second]).astype(jnp.bfloat16)
     *inner, last = bits_of("mp")
     for bit in inner:
         own = own + swap(own, "mp", bit)
     received = swap(own, "mp", last)
-    grad_decoder = decoder_gradient(active, errors, loss_scale)
+    grad_decoder = decoder_gradient(active, errors[1], loss_scale, (1, 2), grad_decoder)
     grad_encoder, grad_bias = encoder_gradient(active, own, received, normed, loss_scale)
     return (grad_encoder, grad_bias, grad_decoder)
 

time: 82.7 us -> 79.1 us (0.956)
  matrix products: 17.2 us -> 13.3 us
  starting transfers between devices: 33.5 us -> 30.3 us
  local copies, waits for them, and re-layouts: 0.91 us -> 2.48 us
  Pallas kernels: 10.4 us -> 11.6 us
    dot_general x14, matrix products: 17.2 us -> 13.3 us  [dot(): lax.dot_general(a, b, (contract, ((), ())), preferred_element_type=jnp.fl...]
    ppermute x24 -> x27, starting transfers between devices: 33.5 us -> 30.3 us  [swap(): return lax.ppermute(values, axis, [(i, i ^ bit) for i in range(size)])]
    unnamed x21 -> x27, local copies, waits for them, and re-layouts: 0.81 us -> 2.37 us
    pallas_call x1 -> x2, Pallas kernels: 5.59 us -> 6.74 us  [decoder_gradient(): pl.pallas_call(kernel, out_shape=jax.ShapeDtypeStruct((3, features, cols)...]
    ppermute x24 -> x27, waiting for transfers between devices: 18.3 us -> 18.8 us  [swap(): return lax.ppermute(values, axis, [(i, i ^ bit) for i in range(size)])]
  transfers between devices with their start and end apart: 24 -> 27, of which waited for: 13 -> 16; matrix products, arithmetic and copies ran while one was open for 20% -> 14% of each run, Pallas kernels for 7% -> 9%
where the time goes in v3:
time: 79.1 us; the launch traced here: 78.9 us
  starting transfers between devices  30.3 us (38%)
  waiting for transfers between devices  18.8 us (24%)
  matrix products  13.3 us (17%)
  Pallas kernels  11.6 us (15%)
  local copies, waits for them, and re-layouts  2.48 us (3%)
  between operations  1.32 us (2%)
  other arithmetic  1.03 us (1%)
    ppermute x27, starting transfers between devices, swap(): return lax.ppermute(values, axis, [(i, i ^ bit) for i in range(size)])  30.3 us
    ppermute x27, waiting for transfers between devices, swap(): return lax.ppermute(values, axis, [(i, i ^ bit) for i in range(size)])  18.8 us
    dot_general x14, matrix products, dot(): lax.dot_general(a, b, (contract, ((), ())), preferred_element_type=jnp.fl...  13.3 us
    pallas_call x2, Pallas kernels, decoder_gradient(): pl.pallas_call(kernel, out_shape=jax.ShapeDtypeStruct((3, features, cols)...  6.74 us
    pallas_call x1, Pallas kernels, encoder_gradient(): pl.pallas_call(kernel, out_shape=(jax.ShapeDtypeStruct((2, features, cols...  4.73 us
    unnamed x27, local copies, waits for them, and re-layouts  2.37 us
  transfers between devices with their start and end apart: 27, of which 16 were waited for; matrix products, arithmetic and copies ran while one was open for 14% of the time, Pallas kernels for 9%

profile of v3, /device:TPU:0, one launch (start us, length us, event | category | flops | bytes accessed | tf_op | source)
XLA Modules:
  0.0 78.9 jit_solution(3273903104477821406)
XLA Ops:
  2.9 4.0 %collective-permute-start.1 = (bf16[6,2304]{1,0:T(8,128)(2,1)S(1)}, bf16[6,2304]{1,0:T(8,128)(2,1)S(1)}, u32[]{:S(2)}, u32[]{:S(2)}) collective-permute-start(bf16[6,2304]{1,0:T(8,128)(2,1)S(1)} %pad_maximum_fusion.11), channel_id=1, source_target_pairs={{0,8},{1,9},{2,10},{3,11},{4,12},{5,13},{6,14},{7,15},{8,0},{9,1},... | collective-permute-start | bytes 82952 | tf_op jit(solution)/shard_map/ppermute | solution.py:19
  6.9 1.6 %collective-permute-start.2 = (bf16[6,2304]{1,0:T(8,128)(2,1)S(1)}, bf16[6,2304]{1,0:T(8,128)(2,1)S(1)}, u32[]{:S(2)}, u32[]{:S(2)}) collective-permute-start(bf16[6,2304]{1,0:T(8,128)(2,1)S(1)} %pad_maximum_fusion.11), channel_id=1, source_target_pairs={{0,4},{1,5},{2,6},{3,7},{4,0},{5,1},{6,2},{7,3},{8,12},{9,13},{10,... | collective-permute-start | bytes 82952 | tf_op jit(solution)/shard_map/ppermute | solution.py:19
  8.9 2.0 %collective-permute-done.2 = bf16[6,2304]{1,0:T(8,128)(2,1)S(1)} collective-permute-done((bf16[6,2304]{1,0:T(8,128)(2,1)S(1)}, bf16[6,2304]{1,0:T(8,128)(2,1)S(1)}, u32[]{:S(2)}, u32[]{:S(2)}) %collective-permute-start.2) | collective-permute-done | bytes 27680 | tf_op jit(solution)/shard_map/ppermute | solution.py:19
  10.9 3.4 %collective-permute-done.3 = bf16[6,2304]{1,0:T(8,128)(2,1)S(1)} collective-permute-done((bf16[6,2304]{1,0:T(8,128)(2,1)S(1)}, bf16[6,2304]{1,0:T(8,128)(2,1)S(1)}, u32[]{:S(2)}, u32[]{:S(2)}) %collective-permute-start.3) | collective-permute-done | bytes 27680 | tf_op jit(solution)/shard_map/ppermute | solution.py:19
  14.4 1.6 %collective-permute-start.4 = (bf16[24,1152]{1,0:T(8,128)(2,1)S(1)}, bf16[24,1152]{1,0:T(8,128)(2,1)S(1)}, u32[]{:S(2)}, u32[]{:S(2)}) collective-permute-start(bf16[24,1152]{1,0:T(8,128)(2,1)S(1)} %get-tuple-element.20.upper_ref), channel_id=1, source_target_pairs={{0,2},{1,3},{2,0},{3,1},{4,6},{5,7},{6,4},{7,5},{8,10},{9,11},{10,... | collective-permute-start | bytes 165896 | tf_op jit(solution)/shard_map/ppermute | solution.py:19
  16.0 1.6 %collective-permute-start.7 = (bf16[24,1152]{1,0:T(8,128)(2,1)S(1)}, bf16[24,1152]{1,0:T(8,128)(2,1)S(1)}, u32[]{:S(2)}, u32[]{:S(2)}) collective-permute-start(bf16[24,1152]{1,0:T(8,128)(2,1)S(1)} %get-tuple-element.19.upper_ref), channel_id=1, source_target_pairs={{0,1},{1,0},{2,3},{3,2},{4,5},{5,4},{6,7},{7,6},{8,9},{9,8},{10,11... | collective-permute-start | bytes 165896 | tf_op jit(solution)/shard_map/ppermute | solution.py:19
  17.5 1.1 %collective-permute-done.4.lower_ref = bf16[24,1152]{1,0:T(8,128)(2,1)S(1)} collective-permute-done((bf16[24,1152]{1,0:T(8,128)(2,1)S(1)}, bf16[24,1152]{1,0:T(8,128)(2,1)S(1)}, u32[]{:S(2)}, u32[]{:S(2)}) %collective-permute-start.4) | collective-permute-done | bytes 55328 | tf_op jit(solution)/shard_map/ppermute | solution.py:19
  18.7 1.6 %collective-permute-start.5 = (bf16[48,1152]{1,0:T(8,128)(2,1)S(1)}, bf16[48,1152]{1,0:T(8,128)(2,1)S(1)}, u32[]{:S(2)}, u32[]{:S(2)}) collective-permute-start(bf16[48,1152]{1,0:T(8,128)(2,1)S(1)} %shard_map.104), channel_id=1, source_target_pairs={{0,1},{1,0},{2,3},{3,2},{4,5},{5,4},{6,7},{7,6},{8,9},{9,8},{10,11... | collective-permute-start | bytes 331784 | tf_op jit(solution)/shard_map/ppermute | solution.py:19
  20.4 1.4 %collective-permute-start.8 = (bf16[48,1152]{1,0:T(8,128)(2,1)S(1)}, bf16[48,1152]{1,0:T(8,128)(2,1)S(1)}, u32[]{:S(2)}, u32[]{:S(2)}) collective-permute-start(bf16[48,1152]{1,0:T(8,128)(2,1)S(1)} %shard_map.105), channel_id=1, source_target_pairs={{0,2},{1,3},{2,0},{3,1},{4,6},{5,7},{6,4},{7,5},{8,10},{9,11},{10,... | collective-permute-start | bytes 331784 | tf_op jit(solution)/shard_map/ppermute | solution.py:19
  21.9 1.7 %collective-permute-done.5 = bf16[48,1152]{1,0:T(8,128)(2,1)S(1)} collective-permute-done((bf16[48,1152]{1,0:T(8,128)(2,1)S(1)}, bf16[48,1152]{1,0:T(8,128)(2,1)S(1)}, u32[]{:S(2)}, u32[]{:S(2)}) %collective-permute-start.5) | collective-permute-done | bytes 110624 | tf_op jit(solution)/shard_map/ppermute | solution.py:19
  24.7 1.5 %slice-done.6 = s8[1048576]{0:T(1024)(128)(4,1)S(1)} async-done(((s8[9437184]{0:T(1024)(128)(4,1)}), s8[1048576]{0:T(1024)(128)(4,1)S(1)}, s32[]{:S(2)}) %slice-start.6) | async-done | bytes 1048600
  26.3 1.5 %fusion.14 = f32[96,2048]{1,0:T(8,128)S(1)} fusion(bf16[2,2048,1152]{2,1,0:T(8,128)(2,1)S(1)} %bitcast.99, bf16[48,1152]{1,0:T(8,128)(2,1)S(1)} %collective-permute-done.5, bf16[48,1152]{1,0:T(8,128)(2,1)S(1)} %shard_map.104), kind=kOutput, calls=%fused_computation.14 | convolution fusion | flops 453427200 | bytes 5726208 | tf_op jit(solution)/shard_map/dot_general | solution.py:151
  29.6 1.5 %fusion.12 = f32[96,2048]{1,0:T(8,128)S(1)} fusion(bf16[2,2048,1152]{2,1,0:T(8,128)(2,1)S(1)} %bitcast.99, bf16[24,1152]{1,0:T(8,128)(2,1)S(1)} %get-tuple-element.18, bf16[24,1152]{1,0:T(8,128)(2,1)S(1)} %collective-permute-done.7.lower_ref, bf16[24,1152]{1,0:T(8,128)(2,1)S(1)} %get-tuple-element.17, bf16[24,1152]{1,0:T(8,128)(2,1)S(1)} %get-tuple-element.19.upper_ref), kind=kOutput, calls=%fused_computation.12 | convolution fusion | flops 453869568 | bytes 5726208 | tf_op jit(solution)/shard_map/dot_general | solution.py:151
  32.9 1.6 %collective-permute-start.11 = (bf16[48,1152]{1,0:T(8,128)(2,1)S(1)}, bf16[48,1152]{1,0:T(8,128)(2,1)S(1)}, u32[]{:S(2)}, u32[]{:S(2)}) collective-permute-start(bf16[48,1152]{1,0:T(8,128)(2,1)S(1)} %slice.282), channel_id=1, source_target_pairs={{0,1},{1,0},{2,3},{3,2},{4,5},{5,4},{6,7},{7,6},{8,9},{9,8},{10,11... | collective-permute-start | bytes 331784 | tf_op jit(solution)/shard_map/ppermute | solution.py:19
  36.9 1.6 %collective-permute-start.19 = (bf16[48,1152]{1,0:T(8,128)(2,1)S(1)}, bf16[48,1152]{1,0:T(8,128)(2,1)S(1)}, u32[]{:S(2)}, u32[]{:S(2)}) collective-permute-start(bf16[48,1152]{1,0:T(8,128)(2,1)S(1)} %pad_maximum_fusion.9), channel_id=1, source_target_pairs={{0,2},{1,3},{2,0},{3,1},{4,6},{5,7},{6,4},{7,5},{8,10},{9,11},{10,... | collective-permute-start | bytes 331784 | tf_op jit(solution)/shard_map/ppermute | solution.py:19
  38.5 1.5 %collective-permute-start.12 = (bf16[24,1152]{1,0:T(8,128)(2,1)S(1)}, bf16[24,1152]{1,0:T(8,128)(2,1)S(1)}, u32[]{:S(2)}, u32[]{:S(2)}) collective-permute-start(bf16[24,1152]{1,0:T(8,128)(2,1)S(1)} %slice.284), channel_id=1, source_target_pairs={{0,2},{1,3},{2,0},{3,1},{4,6},{5,7},{6,4},{7,5},{8,10},{9,11},{10,... | collective-permute-start | bytes 165896 | tf_op jit(solution)/shard_map/ppermute | solution.py:19
  40.1 2.6 %collective-permute-done.19 = bf16[48,1152]{1,0:T(8,128)(2,1)S(1)} collective-permute-done((bf16[48,1152]{1,0:T(8,128)(2,1)S(1)}, bf16[48,1152]{1,0:T(8,128)(2,1)S(1)}, u32[]{:S(2)}, u32[]{:S(2)}) %collective-permute-start.19) | collective-permute-done | bytes 110624 | tf_op jit(solution)/shard_map/ppermute | solution.py:19
  43.4 1.0 %collective-permute-start.14 = (bf16[24,1152]{1,0:T(8,128)(2,1)S(1)}, bf16[24,1152]{1,0:T(8,128)(2,1)S(1)}, u32[]{:S(2)}, u32[]{:S(2)}) collective-permute-start(bf16[24,1152]{1,0:T(8,128)(2,1)S(1)} %fusion.106), channel_id=1, source_target_pairs={{0,12},{1,13},{2,14},{3,15},{4,8},{5,9},{6,10},{7,11},{8,4},{9,5},... | collective-permute-start | bytes 165896 | tf_op jit(solution)/shard_map/ppermute | solution.py:19
  44.4 2.5 %collective-permute-start.15 = (bf16[24,1152]{1,0:T(8,128)(2,1)S(1)}, bf16[24,1152]{1,0:T(8,128)(2,1)S(1)}, u32[]{:S(2)}, u32[]{:S(2)}) collective-permute-start(bf16[24,1152]{1,0:T(8,128)(2,1)S(1)} %fusion.106), channel_id=1, source_target_pairs={{0,4},{1,5},{2,6},{3,7},{4,0},{5,1},{6,2},{7,3},{8,12},{9,13},{10,... | collective-permute-start | bytes 165896 | tf_op jit(solution)/shard_map/ppermute | solution.py:19
  47.9 1.4 %collective-permute-start.22 = (bf16[24,1152]{1,0:T(8,128)(2,1)S(1)}, bf16[24,1152]{1,0:T(8,128)(2,1)S(1)}, u32[]{:S(2)}, u32[]{:S(2)}) collective-permute-start(bf16[24,1152]{1,0:T(8,128)(2,1)S(1)} %fusion.107), channel_id=1, source_target_pairs={{0,12},{1,13},{2,14},{3,15},{4,8},{5,9},{6,10},{7,11},{8,4},{9,5},... | collective-permute-start | bytes 165896 | tf_op jit(solution)/shard_map/ppermute | solution.py:19
  50.6 1.6 %collective-permute-start.16 = (bf16[24,1152]{1,0:T(8,128)(2,1)S(1)}, bf16[24,1152]{1,0:T(8,128)(2,1)S(1)}, u32[]{:S(2)}, u32[]{:S(2)}) collective-permute-start(bf16[24,1152]{1,0:T(8,128)(2,1)S(1)} %shard_map.106), channel_id=1, source_target_pairs={{0,2},{1,3},{2,0},{3,1},{4,6},{5,7},{6,4},{7,5},{8,10},{9,11},{10,... | collective-permute-start | bytes 165896 | tf_op jit(solution)/shard_map/ppermute | solution.py:19
  52.2 2.0 %collective-permute-done.21 = bf16[24,1152]{1,0:T(8,128)(2,1)S(1)} collective-permute-done((bf16[24,1152]{1,0:T(8,128)(2,1)S(1)}, bf16[24,1152]{1,0:T(8,128)(2,1)S(1)}, u32[]{:S(2)}, u32[]{:S(2)}) %collective-permute-start.21) | collective-permute-done | bytes 55328 | tf_op jit(solution)/shard_map/ppermute | solution.py:19
  54.8 1.8 %collective-permute-start.24 = (bf16[24,1152]{1,0:T(8,128)(2,1)S(1)}, bf16[24,1152]{1,0:T(8,128)(2,1)S(1)}, u32[]{:S(2)}, u32[]{:S(2)}) collective-permute-start(bf16[24,1152]{1,0:T(8,128)(2,1)S(1)} %shard_map.107), channel_id=1, source_target_pairs={{0,1},{1,0},{2,3},{3,2},{4,5},{5,4},{6,7},{7,6},{8,9},{9,8},{10,11... | collective-permute-start | bytes 165896 | tf_op jit(solution)/shard_map/ppermute | solution.py:19
  56.6 1.0 %collective-permute-start.17 = (bf16[48,1152]{1,0:T(8,128)(2,1)S(1)}, bf16[48,1152]{1,0:T(8,128)(2,1)S(1)}, u32[]{:S(2)}, u32[]{:S(2)}) collective-permute-start(bf16[48,1152]{1,0:T(8,128)(2,1)S(1)} %pad_maximum_fusion.8), channel_id=1, source_target_pairs={{0,1},{1,0},{2,3},{3,2},{4,5},{5,4},{6,7},{7,6},{8,9},{9,8},{10,11... | collective-permute-start | bytes 331784 | tf_op jit(solution)/shard_map/ppermute | solution.py:19
  57.6 1.4 %collective-permute-done.24 = bf16[24,1152]{1,0:T(8,128)(2,1)S(1)} collective-permute-done((bf16[24,1152]{1,0:T(8,128)(2,1)S(1)}, bf16[24,1152]{1,0:T(8,128)(2,1)S(1)}, u32[]{:S(2)}, u32[]{:S(2)}) %collective-permute-start.24) | collective-permute-done | bytes 55328 | tf_op jit(solution)/shard_map/ppermute | solution.py:19
  59.0 1.6 %collective-permute-start.25 = (bf16[48,1152]{1,0:T(8,128)(2,1)S(1)}, bf16[48,1152]{1,0:T(8,128)(2,1)S(1)}, u32[]{:S(2)}, u32[]{:S(2)}) collective-permute-start(bf16[48,1152]{1,0:T(8,128)(2,1)S(1)} %pad_maximum_fusion.10), channel_id=1, source_target_pairs={{0,2},{1,3},{2,0},{3,1},{4,6},{5,7},{6,4},{7,5},{8,10},{9,11},{10,... | collective-permute-start | bytes 331784 | tf_op jit(solution)/shard_map/ppermute | solution.py:19
  61.4 1.5 %fusion.8 = f32[96,2048]{1,0:T(8,128)S(1)} fusion(bf16[3,2048,1152]{2,1,0:T(8,128)(2,1)S(1)} %bitcast.97, bf16[48,1152]{1,0:T(8,128)(2,1)S(1)} %collective-permute-done.17, bf16[24,1152]{1,0:T(8,128)(2,1)S(1)} %collective-permute-done.16, bf16[24,1152]{1,0:T(8,128)(2,1)S(1)} %shard_map.106), kind=kOutput, calls=%fused_computation.8 | convolution fusion | flops 453648384 | bytes 5726208 | tf_op jit(solution)/shard_map/dot_general | solution.py:151
  63.8 1.5 %fusion.4 = f32[96,2048]{1,0:T(8,128)S(1)} fusion(bf16[3,2048,1152]{2,1,0:T(8,128)(2,1)S(1)} %bitcast.97, bf16[24,1152]{1,0:T(8,128)(2,1)S(1)} %get-tuple-element.16, bf16[24,1152]{1,0:T(8,128)(2,1)S(1)} %collective-permute-done.24, bf16[24,1152]{1,0:T(8,128)(2,1)S(1)} %get-tuple-element.15, bf16[24,1152]{1,0:T(8,128)(2,1)S(1)} %shard_map.107), kind=kOutput, calls=%fused_computation.4 | convolution fusion | flops 453869568 | bytes 5726208 | tf_op jit(solution)/shard_map/dot_general | solution.py:151
  65.5 1.6 %fusion.33 = bf16[1,96,2048]{2,1,0:T(8,128)(2,1)S(1)} fusion(bf16[3,2048,1152]{2,1,0:T(8,128)(2,1)S(1)} %bitcast.97, bf16[24,1152]{1,0:T(8,128)(2,1)S(1)} %get-tuple-element.16, bf16[24,1152]{1,0:T(8,128)(2,1)S(1)} %collective-permute-done.24, bf16[24,1152]{1,0:T(8,128)(2,1)S(1)} %get-tuple-element.15, bf16[24,1152]{1,0:T(8,128)(2,1)S(1)} %shard_map.107), kind=kOutput, calls=%fused_computation.28 | convolution fusion | flops 454066176 | bytes 5332992 | tf_op jit(solution)/shard_map/dot_general | solution.py:151
  67.2 2.6 %shard_map.109.refs_3_ = bf16[3,2048,1152]{2,1,0:T(8,128)(2,1)} custom-call(bf16[96,2048]{1,0:T(8,128)(2,1)S(1)} %maximum_convert_fusion.1.active_0.refs_0_, bf16[96,1152]{1,0:T(8,128)(2,1)S(1)} %pad_maximum_fusion.5.refs_1_), custom_call_target="tpu_custom_call" | custom-call | flops 452984832 | bytes 4718592 | tf_op jit(solution)/shard_map/pallas_call | solution.py:183
  69.9 4.1 %shard_map.110 = bf16[3,2048,1152]{2,1,0:T(8,128)(2,1)} custom-call(bf16[96,2048]{1,0:T(8,128)(2,1)S(1)} %maximum_convert_fusion.1.active_0.refs_0_, bf16[96,2048]{1,0:T(8,128)(2,1)S(1)} %maximum_convert_fusion.active_1.refs_1_, bf16[96,1152]{1,0:T(8,128)(2,1)S(1)} %pad_maximum_fusion.6.refs_2_, ...), custom_call_target="tpu_custom_call", output_to_operand_aliasing={{}: (3, {})} | custom-call | flops 905969664 | bytes 9437184 | tf_op jit(solution)/shard_map/pallas_call | solution.py:183
  74.0 4.7 %shard_map.108 = (bf16[2,2048,1152]{2,1,0:T(8,128)(2,1)}, f32[2,2048]{1,0:T(2,128)}) custom-call(bf16[96,2048]{1,0:T(8,128)(2,1)S(1)} %maximum_convert_fusion.1.active_0.refs_0_, bf16[96,2048]{1,0:T(8,128)(2,1)S(1)} %maximum_convert_fusion.active_1.refs_1_, bf16[2,96,2048]{2,1,0:T(8,128)(2,1)S(1)} %pad_maximum_fusion.own_ref, ...), custom_call_target="tpu_custom_call" | custom-call | flops 905969664 | bytes 9437184 | tf_op jit(solution)/shard_map/pallas_call | solution.py:224
  (109 shorter events, 15.5 us)
Async XLA Ops:
  1.4 14.6 %copy-start.2 = (f32[2,2048]{1,0:T(2,128)S(1)}, f32[2,2048]{1,0:T(2,128)}, u32[]{:S(2)}) copy-start(f32[2,2048]{1,0:T(2,128)} %param.14) | copy-start | bytes 49156
  1.5 1.3 %collective-permute-start = (f32[2,6]{1,0:T(2,128)S(1)}, f32[2,6]{1,0:T(2,128)S(1)}, u32[]{:S(2)}, u32[]{:S(2)}) collective-permute-start(f32[2,6]{1,0:T(2,128)S(1)} %shard_map.103), channel_id=1, source_target_pairs={{0,16},{16,0},{1,17},{17,1},{2,18},{18,2},{3,19},{19,3},{4,20},{20... | collective-permute-start | bytes 152 | tf_op jit(solution)/shard_map/ppermute | solution.py:19
  2.9 5.9 %collective-permute-start.1 = (bf16[6,2304]{1,0:T(8,128)(2,1)S(1)}, bf16[6,2304]{1,0:T(8,128)(2,1)S(1)}, u32[]{:S(2)}, u32[]{:S(2)}) collective-permute-start(bf16[6,2304]{1,0:T(8,128)(2,1)S(1)} %pad_maximum_fusion.11), channel_id=1, source_target_pairs={{0,8},{1,9},{2,10},{3,11},{4,12},{5,13},{6,14},{7,15},{8,0},{9,1},... | collective-permute-start | bytes 82952 | tf_op jit(solution)/shard_map/ppermute | solution.py:19
  6.9 4.0 %collective-permute-start.2 = (bf16[6,2304]{1,0:T(8,128)(2,1)S(1)}, bf16[6,2304]{1,0:T(8,128)(2,1)S(1)}, u32[]{:S(2)}, u32[]{:S(2)}) collective-permute-start(bf16[6,2304]{1,0:T(8,128)(2,1)S(1)} %pad_maximum_fusion.11), channel_id=1, source_target_pairs={{0,4},{1,5},{2,6},{3,7},{4,0},{5,1},{6,2},{7,3},{8,12},{9,13},{10,... | collective-permute-start | bytes 82952 | tf_op jit(solution)/shard_map/ppermute | solution.py:19
  8.5 5.8 %collective-permute-start.3 = (bf16[6,2304]{1,0:T(8,128)(2,1)S(1)}, bf16[6,2304]{1,0:T(8,128)(2,1)S(1)}, u32[]{:S(2)}, u32[]{:S(2)}) collective-permute-start(bf16[6,2304]{1,0:T(8,128)(2,1)S(1)} %pad_maximum_fusion.11), channel_id=1, source_target_pairs={{0,12},{1,13},{2,14},{3,15},{4,8},{5,9},{6,10},{7,11},{8,4},{9,5},... | collective-permute-start | bytes 82952 | tf_op jit(solution)/shard_map/ppermute | solution.py:19
  14.4 4.2 %collective-permute-start.4 = (bf16[24,1152]{1,0:T(8,128)(2,1)S(1)}, bf16[24,1152]{1,0:T(8,128)(2,1)S(1)}, u32[]{:S(2)}, u32[]{:S(2)}) collective-permute-start(bf16[24,1152]{1,0:T(8,128)(2,1)S(1)} %get-tuple-element.20.upper_ref), channel_id=1, source_target_pairs={{0,2},{1,3},{2,0},{3,1},{4,6},{5,7},{6,4},{7,5},{8,10},{9,11},{10,... | collective-permute-start | bytes 165896 | tf_op jit(solution)/shard_map/ppermute | solution.py:19
  16.0 4.4 %collective-permute-start.7 = (bf16[24,1152]{1,0:T(8,128)(2,1)S(1)}, bf16[24,1152]{1,0:T(8,128)(2,1)S(1)}, u32[]{:S(2)}, u32[]{:S(2)}) collective-permute-start(bf16[24,1152]{1,0:T(8,128)(2,1)S(1)} %get-tuple-element.19.upper_ref), channel_id=1, source_target_pairs={{0,1},{1,0},{2,3},{3,2},{4,5},{5,4},{6,7},{7,6},{8,9},{9,8},{10,11... | collective-permute-start | bytes 165896 | tf_op jit(solution)/shard_map/ppermute | solution.py:19
  18.6 13.3 %slice-start = ((s8[14155776]{0:T(1024)(128)(4,1)}), s8[4194304]{0:T(1024)(128)(4,1)S(1)}, s32[]{:S(2)}) async-start(s8[14155776]{0:T(1024)(128)(4,1)} %bitcast.96), calls=%async_computation | async-start | bytes 8388608
  18.6 13.3 %slice-start.1 = ((s8[14155776]{0:T(1024)(128)(4,1)}), s8[4194304]{0:T(1024)(128)(4,1)S(1)}, s32[]{:S(2)}) async-start(s8[14155776]{0:T(1024)(128)(4,1)} %bitcast.96), calls=%async_computation.1 | async-start | bytes 8388608
  18.7 13.3 %slice-start.2 = ((s8[14155776]{0:T(1024)(128)(4,1)}), s8[4194304]{0:T(1024)(128)(4,1)S(1)}, s32[]{:S(2)}) async-start(s8[14155776]{0:T(1024)(128)(4,1)} %bitcast.96), calls=%async_computation.2 | async-start | bytes 8388608
  18.7 13.3 %slice-start.3 = ((s8[14155776]{0:T(1024)(128)(4,1)}), s8[1572864]{0:T(1024)(128)(4,1)S(1)}, s32[]{:S(2)}) async-start(s8[14155776]{0:T(1024)(128)(4,1)} %bitcast.96), calls=%async_computation.3 | async-start | bytes 3145728
  18.7 4.8 %collective-permute-start.5 = (bf16[48,1152]{1,0:T(8,128)(2,1)S(1)}, bf16[48,1152]{1,0:T(8,128)(2,1)S(1)}, u32[]{:S(2)}, u32[]{:S(2)}) collective-permute-start(bf16[48,1152]{1,0:T(8,128)(2,1)S(1)} %shard_map.104), channel_id=1, source_target_pairs={{0,1},{1,0},{2,3},{3,2},{4,5},{5,4},{6,7},{7,6},{8,9},{9,8},{10,11... | collective-permute-start | bytes 331784 | tf_op jit(solution)/shard_map/ppermute | solution.py:19
  20.4 7.4 %collective-permute-start.8 = (bf16[48,1152]{1,0:T(8,128)(2,1)S(1)}, bf16[48,1152]{1,0:T(8,128)(2,1)S(1)}, u32[]{:S(2)}, u32[]{:S(2)}) collective-permute-start(bf16[48,1152]{1,0:T(8,128)(2,1)S(1)} %shard_map.105), channel_id=1, source_target_pairs={{0,2},{1,3},{2,0},{3,1},{4,6},{5,7},{6,4},{7,5},{8,10},{9,11},{10,... | collective-permute-start | bytes 331784 | tf_op jit(solution)/shard_map/ppermute | solution.py:19
  24.6 6.6 %collective-permute-start.10 = (bf16[2,96,576]{2,1,0:T(8,128)(2,1)S(1)}, bf16[2,96,576]{2,1,0:T(8,128)(2,1)S(1)}, u32[]{:S(2)}, u32[]{:S(2)}) collective-permute-start(bf16[2,96,576]{2,1,0:T(8,128)(2,1)S(1)} %pad_maximum_fusion.1), channel_id=1, source_target_pairs={{0,16},{16,0},{1,17},{17,1},{2,18},{18,2},{3,19},{19,3},{4,20},{20... | collective-permute-start | bytes 663560 | tf_op jit(solution)/shard_map/ppermute | solution.py:19
  27.8 4.0 %collective-permute-start.6 = (f32[96,2048]{1,0:T(8,128)S(1)}, f32[96,2048]{1,0:T(8,128)S(1)}, u32[]{:S(2)}, u32[]{:S(2)}) collective-permute-start(f32[96,2048]{1,0:T(8,128)S(1)} %fusion.14), channel_id=1, source_target_pairs={{0,16},{16,0},{1,17},{17,1},{2,18},{18,2},{3,19},{19,3},{4,20},{20... | collective-permute-start | bytes 2359304 | tf_op jit(solution)/shard_map/ppermute | solution.py:19
  29.0 2.3 %collective-permute-start.18 = (bf16[2,96,576]{2,1,0:T(8,128)(2,1)S(1)}, bf16[2,96,576]{2,1,0:T(8,128)(2,1)S(1)}, u32[]{:S(2)}, u32[]{:S(2)}) collective-permute-start(bf16[2,96,576]{2,1,0:T(8,128)(2,1)S(1)} %pad_maximum_fusion.2), channel_id=1, source_target_pairs={{0,16},{16,0},{1,17},{17,1},{2,18},{18,2},{3,19},{19,3},{4,20},{20... | collective-permute-start | bytes 663560 | tf_op jit(solution)/shard_map/ppermute | solution.py:19
  31.1 3.4 %collective-permute-start.9 = (f32[96,2048]{1,0:T(8,128)S(1)}, f32[96,2048]{1,0:T(8,128)S(1)}, u32[]{:S(2)}, u32[]{:S(2)}) collective-permute-start(f32[96,2048]{1,0:T(8,128)S(1)} %fusion.12), channel_id=1, source_target_pairs={{0,16},{16,0},{1,17},{17,1},{2,18},{18,2},{3,19},{19,3},{4,20},{20... | collective-permute-start | bytes 2359304 | tf_op jit(solution)/shard_map/ppermute | solution.py:19
  32.9 5.6 %collective-permute-start.11 = (bf16[48,1152]{1,0:T(8,128)(2,1)S(1)}, bf16[48,1152]{1,0:T(8,128)(2,1)S(1)}, u32[]{:S(2)}, u32[]{:S(2)}) collective-permute-start(bf16[48,1152]{1,0:T(8,128)(2,1)S(1)} %slice.282), channel_id=1, source_target_pairs={{0,1},{1,0},{2,3},{3,2},{4,5},{5,4},{6,7},{7,6},{8,9},{9,8},{10,11... | collective-permute-start | bytes 331784 | tf_op jit(solution)/shard_map/ppermute | solution.py:19
  36.9 5.8 %collective-permute-start.19 = (bf16[48,1152]{1,0:T(8,128)(2,1)S(1)}, bf16[48,1152]{1,0:T(8,128)(2,1)S(1)}, u32[]{:S(2)}, u32[]{:S(2)}) collective-permute-start(bf16[48,1152]{1,0:T(8,128)(2,1)S(1)} %pad_maximum_fusion.9), channel_id=1, source_target_pairs={{0,2},{1,3},{2,0},{3,1},{4,6},{5,7},{6,4},{7,5},{8,10},{9,11},{10,... | collective-permute-start | bytes 331784 | tf_op jit(solution)/shard_map/ppermute | solution.py:19
  38.5 4.8 %collective-permute-start.12 = (bf16[24,1152]{1,0:T(8,128)(2,1)S(1)}, bf16[24,1152]{1,0:T(8,128)(2,1)S(1)}, u32[]{:S(2)}, u32[]{:S(2)}) collective-permute-start(bf16[24,1152]{1,0:T(8,128)(2,1)S(1)} %slice.284), channel_id=1, source_target_pairs={{0,2},{1,3},{2,0},{3,1},{4,6},{5,7},{6,4},{7,5},{8,10},{9,11},{10,... | collective-permute-start | bytes 165896 | tf_op jit(solution)/shard_map/ppermute | solution.py:19
  42.7 4.2 %collective-permute-start.20 = (bf16[24,1152]{1,0:T(8,128)(2,1)S(1)}, bf16[24,1152]{1,0:T(8,128)(2,1)S(1)}, u32[]{:S(2)}, u32[]{:S(2)}) collective-permute-start(bf16[24,1152]{1,0:T(8,128)(2,1)S(1)} %slice.283), channel_id=1, source_target_pairs={{0,1},{1,0},{2,3},{3,2},{4,5},{5,4},{6,7},{7,6},{8,9},{9,8},{10,11... | collective-permute-start | bytes 165896 | tf_op jit(solution)/shard_map/ppermute | solution.py:19
  43.3 6.9 %collective-permute-start.13 = (bf16[24,1152]{1,0:T(8,128)(2,1)S(1)}, bf16[24,1152]{1,0:T(8,128)(2,1)S(1)}, u32[]{:S(2)}, u32[]{:S(2)}) collective-permute-start(bf16[24,1152]{1,0:T(8,128)(2,1)S(1)} %fusion.106), channel_id=1, source_target_pairs={{0,8},{1,9},{2,10},{3,11},{4,12},{5,13},{6,14},{7,15},{8,0},{9,1},... | collective-permute-start | bytes 165896 | tf_op jit(solution)/shard_map/ppermute | solution.py:19
  43.4 7.2 %collective-permute-start.14 = (bf16[24,1152]{1,0:T(8,128)(2,1)S(1)}, bf16[24,1152]{1,0:T(8,128)(2,1)S(1)}, u32[]{:S(2)}, u32[]{:S(2)}) collective-permute-start(bf16[24,1152]{1,0:T(8,128)(2,1)S(1)} %fusion.106), channel_id=1, source_target_pairs={{0,12},{1,13},{2,14},{3,15},{4,8},{5,9},{6,10},{7,11},{8,4},{9,5},... | collective-permute-start | bytes 165896 | tf_op jit(solution)/shard_map/ppermute | solution.py:19
  44.4 6.2 %collective-permute-start.15 = (bf16[24,1152]{1,0:T(8,128)(2,1)S(1)}, bf16[24,1152]{1,0:T(8,128)(2,1)S(1)}, u32[]{:S(2)}, u32[]{:S(2)}) collective-permute-start(bf16[24,1152]{1,0:T(8,128)(2,1)S(1)} %fusion.106), channel_id=1, source_target_pairs={{0,4},{1,5},{2,6},{3,7},{4,0},{5,1},{6,2},{7,3},{8,12},{9,13},{10,... | collective-permute-start | bytes 165896 | tf_op jit(solution)/shard_map/ppermute | solution.py:19
  47.0 7.2 %collective-permute-start.21 = (bf16[24,1152]{1,0:T(8,128)(2,1)S(1)}, bf16[24,1152]{1,0:T(8,128)(2,1)S(1)}, u32[]{:S(2)}, u32[]{:S(2)}) collective-permute-start(bf16[24,1152]{1,0:T(8,128)(2,1)S(1)} %fusion.107), channel_id=1, source_target_pairs={{0,8},{1,9},{2,10},{3,11},{4,12},{5,13},{6,14},{7,15},{8,0},{9,1},... | collective-permute-start | bytes 165896 | tf_op jit(solution)/shard_map/ppermute | solution.py:19
  47.9 6.3 %collective-permute-start.22 = (bf16[24,1152]{1,0:T(8,128)(2,1)S(1)}, bf16[24,1152]{1,0:T(8,128)(2,1)S(1)}, u32[]{:S(2)}, u32[]{:S(2)}) collective-permute-start(bf16[24,1152]{1,0:T(8,128)(2,1)S(1)} %fusion.107), channel_id=1, source_target_pairs={{0,12},{1,13},{2,14},{3,15},{4,8},{5,9},{6,10},{7,11},{8,4},{9,5},... | collective-permute-start | bytes 165896 | tf_op jit(solution)/shard_map/ppermute | solution.py:19
  50.2 4.6 %collective-permute-start.23 = (bf16[24,1152]{1,0:T(8,128)(2,1)S(1)}, bf16[24,1152]{1,0:T(8,128)(2,1)S(1)}, u32[]{:S(2)}, u32[]{:S(2)}) collective-permute-start(bf16[24,1152]{1,0:T(8,128)(2,1)S(1)} %fusion.107), channel_id=1, source_target_pairs={{0,4},{1,5},{2,6},{3,7},{4,0},{5,1},{6,2},{7,3},{8,12},{9,13},{10,... | collective-permute-start | bytes 165896 | tf_op jit(solution)/shard_map/ppermute | solution.py:19
  50.6 6.0 %collective-permute-start.16 = (bf16[24,1152]{1,0:T(8,128)(2,1)S(1)}, bf16[24,1152]{1,0:T(8,128)(2,1)S(1)}, u32[]{:S(2)}, u32[]{:S(2)}) collective-permute-start(bf16[24,1152]{1,0:T(8,128)(2,1)S(1)} %shard_map.106), channel_id=1, source_target_pairs={{0,2},{1,3},{2,0},{3,1},{4,6},{5,7},{6,4},{7,5},{8,10},{9,11},{10,... | collective-permute-start | bytes 165896 | tf_op jit(solution)/shard_map/ppermute | solution.py:19
  54.8 4.2 %collective-permute-start.24 = (bf16[24,1152]{1,0:T(8,128)(2,1)S(1)}, bf16[24,1152]{1,0:T(8,128)(2,1)S(1)}, u32[]{:S(2)}, u32[]{:S(2)}) collective-permute-start(bf16[24,1152]{1,0:T(8,128)(2,1)S(1)} %shard_map.107), channel_id=1, source_target_pairs={{0,1},{1,0},{2,3},{3,2},{4,5},{5,4},{6,7},{7,6},{8,9},{9,8},{10,11... | collective-permute-start | bytes 165896 | tf_op jit(solution)/shard_map/ppermute | solution.py:19
  56.6 4.8 %collective-permute-start.17 = (bf16[48,1152]{1,0:T(8,128)(2,1)S(1)}, bf16[48,1152]{1,0:T(8,128)(2,1)S(1)}, u32[]{:S(2)}, u32[]{:S(2)}) collective-permute-start(bf16[48,1152]{1,0:T(8,128)(2,1)S(1)} %pad_maximum_fusion.8), channel_id=1, source_target_pairs={{0,1},{1,0},{2,3},{3,2},{4,5},{5,4},{6,7},{7,6},{8,9},{9,8},{10,11... | collective-permute-start | bytes 331784 | tf_op jit(solution)/shard_map/ppermute | solution.py:19
  59.0 4.8 %collective-permute-start.25 = (bf16[48,1152]{1,0:T(8,128)(2,1)S(1)}, bf16[48,1152]{1,0:T(8,128)(2,1)S(1)}, u32[]{:S(2)}, u32[]{:S(2)}) collective-permute-start(bf16[48,1152]{1,0:T(8,128)(2,1)S(1)} %pad_maximum_fusion.10), channel_id=1, source_target_pairs={{0,2},{1,3},{2,0},{3,1},{4,6},{5,7},{6,4},{7,5},{8,10},{9,11},{10,... | collective-permute-start | bytes 331784 | tf_op jit(solution)/shard_map/ppermute | solution.py:19
  67.1 6.9 %collective-permute-start.26 = (bf16[2,96,2048]{2,1,0:T(8,128)(2,1)S(1)}, bf16[2,96,2048]{2,1,0:T(8,128)(2,1)S(1)}, u32[]{:S(2)}, u32[]{:S(2)}) collective-permute-start(bf16[2,96,2048]{2,1,0:T(8,128)(2,1)S(1)} %pad_maximum_fusion.own_ref), channel_id=1, source_target_pairs={{0,16},{16,0},{1,17},{17,1},{2,18},{18,2},{3,19},{19,3},{4,20},{20... | collective-permute-start | bytes 2359304 | tf_op jit(solution)/shard_map/ppermute | solution.py:19
  (8 other events, 35.3 us)

commit v4 on v3

--- a/solution.py
+++ b/solution.py
@@ -113,16 +113,34 @@
 def square_sums(values, flops):
     def kernel(values_ref, out_ref):
         v = values_ref[...].astype(jnp.float32)
-        out_ref[...] = jnp.sum(v * v, axis=2)
-
-    return pl.pallas_call(
-        kernel,
-        out_shape=jax.ShapeDtypeStruct(values.shape[:2], jnp.float32),
+        out_ref[...] = jnp.sum(v * v, axis=2, keepdims=True)
+
+    return pl.pallas_call(
+        kernel,
+        out_shape=jax.ShapeDtypeStruct((*values.shape[:2], 1), jnp.float32),
         in_specs=[pl.BlockSpec(memory_space=pltpu.VMEM)],
         out_specs=pl.BlockSpec(memory_space=pltpu.VMEM),
         compiler_params=pltpu.CompilerParams(vmem_limit_bytes=4 << 20),
         cost_estimate=pl.CostEstimate(flops=flops, bytes_accessed=1 << 16, transcendentals=0),
     )(values)
+
+
+def normalize(values, inverse_rms, gain, flops):
+    layers, rows, cols = values.shape
+
+    def kernel(values_ref, inverse_ref, gain_ref, out_ref):
+        for l in range(layers):
+            scaled = values_ref[l].astype(jnp.float32) * inverse_ref[l] * gain_ref[l : l + 1]
+            out_ref[:, l * cols : (l + 1) * cols] = scaled.astype(jnp.bfloat16)
+
+    return pl.pallas_call(
+        kernel,
+        out_shape=jax.ShapeDtypeStruct((rows, layers * cols), jnp.bfloat16),
+        in_specs=[pl.BlockSpec(memory_space=pltpu.VMEM)] * 3,
+        out_specs=pl.BlockSpec(memory_space=pltpu.VMEM),
+        compiler_params=pltpu.CompilerParams(vmem_limit_bytes=4 << 20),
+        cost_estimate=pl.CostEstimate(flops=flops, bytes_accessed=1 << 16, transcendentals=0),
+    )(values, inverse_rms, gain)
 
 
 def add_round(kept, received, flops):
@@ -241,13 +259,14 @@
 
 
 def body(residual, norm_gain, gate_weight, up_weight, down_weight, encoder, encoder_bias, decoder):
-    values = residual.astype(jnp.float32)
-    squares = mp_sum(square_sums(residual, int(4e11)))
+    squares = mp_sum(square_sums(residual, int(1e10)))
     inverse_rms = lax.rsqrt(squares / D + 1e-06)
-    normed_local = (values * inverse_rms[:, :, None] * norm_gain[:, None, :]).astype(jnp.bfloat16)
     model_cols = decoder.shape[2]
-    quarter = gather_inner(jnp.concatenate([normed_local[0], normed_local[1]], axis=1))
-    normed = [gather_outer(quarter[:, l * model_cols : (l + 1) * model_cols], l, int(4e10)) for l in range(2)]
+    quarter = gather_inner(normalize(residual, inverse_rms, norm_gain, int(4e10)))
+    normed = [
+        gather_outer(quarter[:, l * model_cols : (l + 1) * model_cols], l, int(1e10) if l == 0 else int(1e6))
+        for l in range(2)
+    ]
     tokens = normed[0].shape[0]
     active = []
     target = []

time: 79.1 us -> 77.5 us (0.980)
  local copies, waits for them, and re-layouts: 2.48 us -> 0.9 us
    unnamed x27 -> x21, local copies, waits for them, and re-layouts: 2.37 us -> 0.8 us
  transfers between devices with their start and end apart: 27 -> 27, of which waited for: 16 -> 15; matrix products, arithmetic and copies ran while one was open for 14% -> 14% of each run, Pallas kernels for 9% -> 9%
where the time goes in v4:
time: 77.5 us; the launch traced here: 77.3 us
  starting transfers between devices  30.9 us (40%)
  waiting for transfers between devices  18.4 us (24%)
  matrix products  13.3 us (17%)
  Pallas kernels  11.7 us (15%)
  between operations  1.24 us (2%)
  other arithmetic  0.91 us (1%)
  local copies, waits for them, and re-layouts  0.9 us (1%)
    ppermute x27, starting transfers between devices, swap(): return lax.ppermute(values, axis, [(i, i ^ bit) for i in range(size)])  30.9 us
    ppermute x27, waiting for transfers between devices, swap(): return lax.ppermute(values, axis, [(i, i ^ bit) for i in range(size)])  18.4 us
    dot_general x14, matrix products, dot(): lax.dot_general(a, b, (contract, ((), ())), preferred_element_type=jnp.fl...  13.3 us
    pallas_call x2, Pallas kernels, decoder_gradient(): pl.pallas_call(kernel, out_shape=jax.ShapeDtypeStruct((3, features, cols)...  6.7 us
    pallas_call x1, Pallas kernels, encoder_gradient(): pl.pallas_call(kernel, out_shape=(jax.ShapeDtypeStruct((2, features, cols...  4.73 us
  transfers between devices with their start and end apart: 27, of which 15 were waited for; matrix products, arithmetic and copies ran while one was open for 14% of the time, Pallas kernels for 9%

profile of v4, /device:TPU:0, one launch (start us, length us, event | category | flops | bytes accessed | tf_op | source)
XLA Modules:
  0.0 77.3 jit_solution(15660988372361543234)
XLA Ops:
  2.9 4.0 %collective-permute-start.1 = (bf16[6,2304]{1,0:T(8,128)(2,1)S(1)}, bf16[6,2304]{1,0:T(8,128)(2,1)S(1)}, u32[]{:S(2)}, u32[]{:S(2)}) collective-permute-start(bf16[6,2304]{1,0:T(8,128)(2,1)S(1)} %shard_map.104), channel_id=1, source_target_pairs={{0,8},{1,9},{2,10},{3,11},{4,12},{5,13},{6,14},{7,15},{8,0},{9,1},... | collective-permute-start | bytes 82952 | tf_op jit(solution)/shard_map/ppermute | solution.py:19
  6.8 1.6 %collective-permute-start.2 = (bf16[6,2304]{1,0:T(8,128)(2,1)S(1)}, bf16[6,2304]{1,0:T(8,128)(2,1)S(1)}, u32[]{:S(2)}, u32[]{:S(2)}) collective-permute-start(bf16[6,2304]{1,0:T(8,128)(2,1)S(1)} %shard_map.104), channel_id=1, source_target_pairs={{0,4},{1,5},{2,6},{3,7},{4,0},{5,1},{6,2},{7,3},{8,12},{9,13},{10,... | collective-permute-start | bytes 82952 | tf_op jit(solution)/shard_map/ppermute | solution.py:19
  8.8 2.0 %collective-permute-done.2 = bf16[6,2304]{1,0:T(8,128)(2,1)S(1)} collective-permute-done((bf16[6,2304]{1,0:T(8,128)(2,1)S(1)}, bf16[6,2304]{1,0:T(8,128)(2,1)S(1)}, u32[]{:S(2)}, u32[]{:S(2)}) %collective-permute-start.2) | collective-permute-done | bytes 27680 | tf_op jit(solution)/shard_map/ppermute | solution.py:19
  10.8 3.4 %collective-permute-done.3 = bf16[6,2304]{1,0:T(8,128)(2,1)S(1)} collective-permute-done((bf16[6,2304]{1,0:T(8,128)(2,1)S(1)}, bf16[6,2304]{1,0:T(8,128)(2,1)S(1)}, u32[]{:S(2)}, u32[]{:S(2)}) %collective-permute-start.3) | collective-permute-done | bytes 27680 | tf_op jit(solution)/shard_map/ppermute | solution.py:19
  14.3 1.6 %collective-permute-start.4 = (bf16[24,1152]{1,0:T(8,128)(2,1)S(1)}, bf16[24,1152]{1,0:T(8,128)(2,1)S(1)}, u32[]{:S(2)}, u32[]{:S(2)}) collective-permute-start(bf16[24,1152]{1,0:T(8,128)(2,1)S(1)} %get-tuple-element.20.upper_ref), channel_id=1, source_target_pairs={{0,2},{1,3},{2,0},{3,1},{4,6},{5,7},{6,4},{7,5},{8,10},{9,11},{10,... | collective-permute-start | bytes 165896 | tf_op jit(solution)/shard_map/ppermute | solution.py:19
  15.9 1.5 %collective-permute-start.7 = (bf16[24,1152]{1,0:T(8,128)(2,1)S(1)}, bf16[24,1152]{1,0:T(8,128)(2,1)S(1)}, u32[]{:S(2)}, u32[]{:S(2)}) collective-permute-start(bf16[24,1152]{1,0:T(8,128)(2,1)S(1)} %get-tuple-element.19.upper_ref), channel_id=1, source_target_pairs={{0,1},{1,0},{2,3},{3,2},{4,5},{5,4},{6,7},{7,6},{8,9},{9,8},{10,11... | collective-permute-start | bytes 165896 | tf_op jit(solution)/shard_map/ppermute | solution.py:19
  17.4 1.1 %collective-permute-done.4.lower_ref = bf16[24,1152]{1,0:T(8,128)(2,1)S(1)} collective-permute-done((bf16[24,1152]{1,0:T(8,128)(2,1)S(1)}, bf16[24,1152]{1,0:T(8,128)(2,1)S(1)}, u32[]{:S(2)}, u32[]{:S(2)}) %collective-permute-start.4) | collective-permute-done | bytes 55328 | tf_op jit(solution)/shard_map/ppermute | solution.py:19
  18.5 1.6 %collective-permute-start.5 = (bf16[48,1152]{1,0:T(8,128)(2,1)S(1)}, bf16[48,1152]{1,0:T(8,128)(2,1)S(1)}, u32[]{:S(2)}, u32[]{:S(2)}) collective-permute-start(bf16[48,1152]{1,0:T(8,128)(2,1)S(1)} %shard_map.105), channel_id=1, source_target_pairs={{0,1},{1,0},{2,3},{3,2},{4,5},{5,4},{6,7},{7,6},{8,9},{9,8},{10,11... | collective-permute-start | bytes 331784 | tf_op jit(solution)/shard_map/ppermute | solution.py:19
  20.3 1.4 %collective-permute-start.8 = (bf16[48,1152]{1,0:T(8,128)(2,1)S(1)}, bf16[48,1152]{1,0:T(8,128)(2,1)S(1)}, u32[]{:S(2)}, u32[]{:S(2)}) collective-permute-start(bf16[48,1152]{1,0:T(8,128)(2,1)S(1)} %shard_map.106), channel_id=1, source_target_pairs={{0,2},{1,3},{2,0},{3,1},{4,6},{5,7},{6,4},{7,5},{8,10},{9,11},{10,... | collective-permute-start | bytes 331784 | tf_op jit(solution)/shard_map/ppermute | solution.py:19
  21.7 1.6 %collective-permute-done.5 = bf16[48,1152]{1,0:T(8,128)(2,1)S(1)} collective-permute-done((bf16[48,1152]{1,0:T(8,128)(2,1)S(1)}, bf16[48,1152]{1,0:T(8,128)(2,1)S(1)}, u32[]{:S(2)}, u32[]{:S(2)}) %collective-permute-start.5) | collective-permute-done | bytes 110624 | tf_op jit(solution)/shard_map/ppermute | solution.py:19
  24.5 1.6 %fusion.14 = f32[96,2048]{1,0:T(8,128)S(1)} fusion(bf16[2,2048,1152]{2,1,0:T(8,128)(2,1)S(1)} %copy-done.3, bf16[48,1152]{1,0:T(8,128)(2,1)S(1)} %collective-permute-done.5, bf16[48,1152]{1,0:T(8,128)(2,1)S(1)} %shard_map.105), kind=kOutput, calls=%fused_computation.14 | convolution fusion | flops 453427200 | bytes 5726208 | tf_op jit(solution)/shard_map/dot_general | solution.py:169
  27.9 1.5 %fusion.12 = f32[96,2048]{1,0:T(8,128)S(1)} fusion(bf16[2,2048,1152]{2,1,0:T(8,128)(2,1)S(1)} %copy-done.3, bf16[24,1152]{1,0:T(8,128)(2,1)S(1)} %get-tuple-element.18, bf16[24,1152]{1,0:T(8,128)(2,1)S(1)} %collective-permute-done.7.lower_ref, bf16[24,1152]{1,0:T(8,128)(2,1)S(1)} %get-tuple-element.17, bf16[24,1152]{1,0:T(8,128)(2,1)S(1)} %get-tuple-element.19.upper_ref), kind=kOutput, calls=%fused_computation.12 | convolution fusion | flops 453869568 | bytes 5726208 | tf_op jit(solution)/shard_map/dot_general | solution.py:169
  31.7 1.6 %collective-permute-start.11 = (bf16[48,1152]{1,0:T(8,128)(2,1)S(1)}, bf16[48,1152]{1,0:T(8,128)(2,1)S(1)}, u32[]{:S(2)}, u32[]{:S(2)}) collective-permute-start(bf16[48,1152]{1,0:T(8,128)(2,1)S(1)} %slice.270), channel_id=1, source_target_pairs={{0,1},{1,0},{2,3},{3,2},{4,5},{5,4},{6,7},{7,6},{8,9},{9,8},{10,11... | collective-permute-start | bytes 331784 | tf_op jit(solution)/shard_map/ppermute | solution.py:19
  35.6 1.6 %collective-permute-start.19 = (bf16[48,1152]{1,0:T(8,128)(2,1)S(1)}, bf16[48,1152]{1,0:T(8,128)(2,1)S(1)}, u32[]{:S(2)}, u32[]{:S(2)}) collective-permute-start(bf16[48,1152]{1,0:T(8,128)(2,1)S(1)} %pad_maximum_fusion.9), channel_id=1, source_target_pairs={{0,2},{1,3},{2,0},{3,1},{4,6},{5,7},{6,4},{7,5},{8,10},{9,11},{10,... | collective-permute-start | bytes 331784 | tf_op jit(solution)/shard_map/ppermute | solution.py:19
  37.3 1.1 %collective-permute-start.12 = (bf16[24,1152]{1,0:T(8,128)(2,1)S(1)}, bf16[24,1152]{1,0:T(8,128)(2,1)S(1)}, u32[]{:S(2)}, u32[]{:S(2)}) collective-permute-start(bf16[24,1152]{1,0:T(8,128)(2,1)S(1)} %slice.272), channel_id=1, source_target_pairs={{0,2},{1,3},{2,0},{3,1},{4,6},{5,7},{6,4},{7,5},{8,10},{9,11},{10,... | collective-permute-start | bytes 165896 | tf_op jit(solution)/shard_map/ppermute | solution.py:19
  38.3 2.7 %collective-permute-done.19 = bf16[48,1152]{1,0:T(8,128)(2,1)S(1)} collective-permute-done((bf16[48,1152]{1,0:T(8,128)(2,1)S(1)}, bf16[48,1152]{1,0:T(8,128)(2,1)S(1)}, u32[]{:S(2)}, u32[]{:S(2)}) %collective-permute-start.19) | collective-permute-done | bytes 110624 | tf_op jit(solution)/shard_map/ppermute | solution.py:19
  42.0 1.0 %collective-permute-start.14 = (bf16[24,1152]{1,0:T(8,128)(2,1)S(1)}, bf16[24,1152]{1,0:T(8,128)(2,1)S(1)}, u32[]{:S(2)}, u32[]{:S(2)}) collective-permute-start(bf16[24,1152]{1,0:T(8,128)(2,1)S(1)} %fusion.106), channel_id=1, source_target_pairs={{0,12},{1,13},{2,14},{3,15},{4,8},{5,9},{6,10},{7,11},{8,4},{9,5},... | collective-permute-start | bytes 165896 | tf_op jit(solution)/shard_map/ppermute | solution.py:19
  43.0 2.5 %collective-permute-start.15 = (bf16[24,1152]{1,0:T(8,128)(2,1)S(1)}, bf16[24,1152]{1,0:T(8,128)(2,1)S(1)}, u32[]{:S(2)}, u32[]{:S(2)}) collective-permute-start(bf16[24,1152]{1,0:T(8,128)(2,1)S(1)} %fusion.106), channel_id=1, source_target_pairs={{0,4},{1,5},{2,6},{3,7},{4,0},{5,1},{6,2},{7,3},{8,12},{9,13},{10,... | collective-permute-start | bytes 165896 | tf_op jit(solution)/shard_map/ppermute | solution.py:19
  45.5 1.0 %collective-permute-start.21 = (bf16[24,1152]{1,0:T(8,128)(2,1)S(1)}, bf16[24,1152]{1,0:T(8,128)(2,1)S(1)}, u32[]{:S(2)}, u32[]{:S(2)}) collective-permute-start(bf16[24,1152]{1,0:T(8,128)(2,1)S(1)} %fusion.107), channel_id=1, source_target_pairs={{0,8},{1,9},{2,10},{3,11},{4,12},{5,13},{6,14},{7,15},{8,0},{9,1},... | collective-permute-start | bytes 165896 | tf_op jit(solution)/shard_map/ppermute | solution.py:19
  46.5 1.4 %collective-permute-start.22 = (bf16[24,1152]{1,0:T(8,128)(2,1)S(1)}, bf16[24,1152]{1,0:T(8,128)(2,1)S(1)}, u32[]{:S(2)}, u32[]{:S(2)}) collective-permute-start(bf16[24,1152]{1,0:T(8,128)(2,1)S(1)} %fusion.107), channel_id=1, source_target_pairs={{0,12},{1,13},{2,14},{3,15},{4,8},{5,9},{6,10},{7,11},{8,4},{9,5},... | collective-permute-start | bytes 165896 | tf_op jit(solution)/shard_map/ppermute | solution.py:19
  49.7 1.9 %collective-permute-start.16 = (bf16[24,1152]{1,0:T(8,128)(2,1)S(1)}, bf16[24,1152]{1,0:T(8,128)(2,1)S(1)}, u32[]{:S(2)}, u32[]{:S(2)}) collective-permute-start(bf16[24,1152]{1,0:T(8,128)(2,1)S(1)} %shard_map.107), channel_id=1, source_target_pairs={{0,2},{1,3},{2,0},{3,1},{4,6},{5,7},{6,4},{7,5},{8,10},{9,11},{10,... | collective-permute-start | bytes 165896 | tf_op jit(solution)/shard_map/ppermute | solution.py:19
  53.2 1.7 %collective-permute-start.24 = (bf16[24,1152]{1,0:T(8,128)(2,1)S(1)}, bf16[24,1152]{1,0:T(8,128)(2,1)S(1)}, u32[]{:S(2)}, u32[]{:S(2)}) collective-permute-start(bf16[24,1152]{1,0:T(8,128)(2,1)S(1)} %shard_map.108), channel_id=1, source_target_pairs={{0,1},{1,0},{2,3},{3,2},{4,5},{5,4},{6,7},{7,6},{8,9},{9,8},{10,11... | collective-permute-start | bytes 165896 | tf_op jit(solution)/shard_map/ppermute | solution.py:19
  54.9 1.1 %collective-permute-start.17 = (bf16[48,1152]{1,0:T(8,128)(2,1)S(1)}, bf16[48,1152]{1,0:T(8,128)(2,1)S(1)}, u32[]{:S(2)}, u32[]{:S(2)}) collective-permute-start(bf16[48,1152]{1,0:T(8,128)(2,1)S(1)} %pad_maximum_fusion.8), channel_id=1, source_target_pairs={{0,1},{1,0},{2,3},{3,2},{4,5},{5,4},{6,7},{7,6},{8,9},{9,8},{10,11... | collective-permute-start | bytes 331784 | tf_op jit(solution)/shard_map/ppermute | solution.py:19
  56.0 1.4 %collective-permute-done.24 = bf16[24,1152]{1,0:T(8,128)(2,1)S(1)} collective-permute-done((bf16[24,1152]{1,0:T(8,128)(2,1)S(1)}, bf16[24,1152]{1,0:T(8,128)(2,1)S(1)}, u32[]{:S(2)}, u32[]{:S(2)}) %collective-permute-start.24) | collective-permute-done | bytes 55328 | tf_op jit(solution)/shard_map/ppermute | solution.py:19
  57.4 1.6 %collective-permute-start.25 = (bf16[48,1152]{1,0:T(8,128)(2,1)S(1)}, bf16[48,1152]{1,0:T(8,128)(2,1)S(1)}, u32[]{:S(2)}, u32[]{:S(2)}) collective-permute-start(bf16[48,1152]{1,0:T(8,128)(2,1)S(1)} %pad_maximum_fusion.10), channel_id=1, source_target_pairs={{0,2},{1,3},{2,0},{3,1},{4,6},{5,7},{6,4},{7,5},{8,10},{9,11},{10,... | collective-permute-start | bytes 331784 | tf_op jit(solution)/shard_map/ppermute | solution.py:19
  59.7 1.6 %fusion.8 = f32[96,2048]{1,0:T(8,128)S(1)} fusion(bf16[3,2048,1152]{2,1,0:T(8,128)(2,1)S(1)} %bitcast.93, bf16[48,1152]{1,0:T(8,128)(2,1)S(1)} %collective-permute-done.17, bf16[24,1152]{1,0:T(8,128)(2,1)S(1)} %collective-permute-done.16, bf16[24,1152]{1,0:T(8,128)(2,1)S(1)} %shard_map.107), kind=kOutput, calls=%fused_computation.8 | convolution fusion | flops 453648384 | bytes 5726208 | tf_op jit(solution)/shard_map/dot_general | solution.py:169
  61.3 1.0 %collective-permute-done.25 = bf16[48,1152]{1,0:T(8,128)(2,1)S(1)} collective-permute-done((bf16[48,1152]{1,0:T(8,128)(2,1)S(1)}, bf16[48,1152]{1,0:T(8,128)(2,1)S(1)}, u32[]{:S(2)}, u32[]{:S(2)}) %collective-permute-start.25) | collective-permute-done | bytes 110624 | tf_op jit(solution)/shard_map/ppermute | solution.py:19
  62.3 1.5 %fusion.4 = f32[96,2048]{1,0:T(8,128)S(1)} fusion(bf16[3,2048,1152]{2,1,0:T(8,128)(2,1)S(1)} %bitcast.93, bf16[24,1152]{1,0:T(8,128)(2,1)S(1)} %get-tuple-element.16, bf16[24,1152]{1,0:T(8,128)(2,1)S(1)} %collective-permute-done.24, bf16[24,1152]{1,0:T(8,128)(2,1)S(1)} %get-tuple-element.15, bf16[24,1152]{1,0:T(8,128)(2,1)S(1)} %shard_map.108), kind=kOutput, calls=%fused_computation.4 | convolution fusion | flops 453869568 | bytes 5726208 | tf_op jit(solution)/shard_map/dot_general | solution.py:169
  63.9 1.6 %fusion.33 = bf16[1,96,2048]{2,1,0:T(8,128)(2,1)S(1)} fusion(bf16[3,2048,1152]{2,1,0:T(8,128)(2,1)S(1)} %bitcast.93, bf16[24,1152]{1,0:T(8,128)(2,1)S(1)} %get-tuple-element.16, bf16[24,1152]{1,0:T(8,128)(2,1)S(1)} %collective-permute-done.24, bf16[24,1152]{1,0:T(8,128)(2,1)S(1)} %get-tuple-element.15, bf16[24,1152]{1,0:T(8,128)(2,1)S(1)} %shard_map.108), kind=kOutput, calls=%fused_computation.28 | convolution fusion | flops 454066176 | bytes 5332992 | tf_op jit(solution)/shard_map/dot_general | solution.py:169
  65.7 2.6 %shard_map.110.refs_3_ = bf16[3,2048,1152]{2,1,0:T(8,128)(2,1)} custom-call(bf16[96,2048]{1,0:T(8,128)(2,1)S(1)} %maximum_convert_fusion.1.active_0.refs_0_, bf16[96,1152]{1,0:T(8,128)(2,1)S(1)} %pad_maximum_fusion.5.refs_1_), custom_call_target="tpu_custom_call" | custom-call | flops 452984832 | bytes 4718592 | tf_op jit(solution)/shard_map/pallas_call | solution.py:201
  68.3 4.1 %shard_map.111 = bf16[3,2048,1152]{2,1,0:T(8,128)(2,1)} custom-call(bf16[96,2048]{1,0:T(8,128)(2,1)S(1)} %maximum_convert_fusion.1.active_0.refs_0_, bf16[96,2048]{1,0:T(8,128)(2,1)S(1)} %maximum_convert_fusion.active_1.refs_1_, bf16[96,1152]{1,0:T(8,128)(2,1)S(1)} %pad_maximum_fusion.6.refs_2_, ...), custom_call_target="tpu_custom_call", output_to_operand_aliasing={{}: (3, {})} | custom-call | flops 905969664 | bytes 9437184 | tf_op jit(solution)/shard_map/pallas_call | solution.py:201
  72.4 4.7 %shard_map.109 = (bf16[2,2048,1152]{2,1,0:T(8,128)(2,1)}, f32[2,2048]{1,0:T(2,128)}) custom-call(bf16[96,2048]{1,0:T(8,128)(2,1)S(1)} %maximum_convert_fusion.1.active_0.refs_0_, bf16[96,2048]{1,0:T(8,128)(2,1)S(1)} %maximum_convert_fusion.active_1.refs_1_, bf16[2,96,2048]{2,1,0:T(8,128)(2,1)S(1)} %pad_maximum_fusion.own_ref, ...), custom_call_target="tpu_custom_call" | custom-call | flops 905969664 | bytes 9437184 | tf_op jit(solution)/shard_map/pallas_call | solution.py:242
  (100 shorter events, 15.7 us)
Async XLA Ops:
  1.5 1.3 %collective-permute-start = (f32[2,6,1]{2,1,0:T(8,128)S(1)}, f32[2,6,1]{2,1,0:T(8,128)S(1)}, u32[]{:S(2)}, u32[]{:S(2)}) collective-permute-start(f32[2,6,1]{2,1,0:T(8,128)S(1)} %shard_map.103), channel_id=1, source_target_pairs={{0,16},{16,0},{1,17},{17,1},{2,18},{18,2},{3,19},{19,3},{4,20},{20... | collective-permute-start | bytes 152 | tf_op jit(solution)/shard_map/ppermute | solution.py:19
  2.9 5.9 %collective-permute-start.1 = (bf16[6,2304]{1,0:T(8,128)(2,1)S(1)}, bf16[6,2304]{1,0:T(8,128)(2,1)S(1)}, u32[]{:S(2)}, u32[]{:S(2)}) collective-permute-start(bf16[6,2304]{1,0:T(8,128)(2,1)S(1)} %shard_map.104), channel_id=1, source_target_pairs={{0,8},{1,9},{2,10},{3,11},{4,12},{5,13},{6,14},{7,15},{8,0},{9,1},... | collective-permute-start | bytes 82952 | tf_op jit(solution)/shard_map/ppermute | solution.py:19
  6.8 4.0 %collective-permute-start.2 = (bf16[6,2304]{1,0:T(8,128)(2,1)S(1)}, bf16[6,2304]{1,0:T(8,128)(2,1)S(1)}, u32[]{:S(2)}, u32[]{:S(2)}) collective-permute-start(bf16[6,2304]{1,0:T(8,128)(2,1)S(1)} %shard_map.104), channel_id=1, source_target_pairs={{0,4},{1,5},{2,6},{3,7},{4,0},{5,1},{6,2},{7,3},{8,12},{9,13},{10,... | collective-permute-start | bytes 82952 | tf_op jit(solution)/shard_map/ppermute | solution.py:19
  8.4 5.8 %collective-permute-start.3 = (bf16[6,2304]{1,0:T(8,128)(2,1)S(1)}, bf16[6,2304]{1,0:T(8,128)(2,1)S(1)}, u32[]{:S(2)}, u32[]{:S(2)}) collective-permute-start(bf16[6,2304]{1,0:T(8,128)(2,1)S(1)} %shard_map.104), channel_id=1, source_target_pairs={{0,12},{1,13},{2,14},{3,15},{4,8},{5,9},{6,10},{7,11},{8,4},{9,5},... | collective-permute-start | bytes 82952 | tf_op jit(solution)/shard_map/ppermute | solution.py:19
  14.3 4.2 %collective-permute-start.4 = (bf16[24,1152]{1,0:T(8,128)(2,1)S(1)}, bf16[24,1152]{1,0:T(8,128)(2,1)S(1)}, u32[]{:S(2)}, u32[]{:S(2)}) collective-permute-start(bf16[24,1152]{1,0:T(8,128)(2,1)S(1)} %get-tuple-element.20.upper_ref), channel_id=1, source_target_pairs={{0,2},{1,3},{2,0},{3,1},{4,6},{5,7},{6,4},{7,5},{8,10},{9,11},{10,... | collective-permute-start | bytes 165896 | tf_op jit(solution)/shard_map/ppermute | solution.py:19
  15.9 7.5 %copy-start.4 = (bf16[2,1152,576]{1,2,0:T(8,128)(2,1)S(1)}, bf16[2,1152,576]{1,2,0:T(8,128)(2,1)}, u32[]{:S(2)}) copy-start(bf16[2,1152,576]{1,2,0:T(8,128)(2,1)} %param.11) | copy-start | bytes 7962628
  15.9 8.0 %copy-start.5 = (bf16[2,1152,576]{1,2,0:T(8,128)(2,1)S(1)}, bf16[2,1152,576]{1,2,0:T(8,128)(2,1)}, u32[]{:S(2)}) copy-start(bf16[2,1152,576]{1,2,0:T(8,128)(2,1)} %param.10) | copy-start | bytes 7962628
  15.9 4.4 %collective-permute-start.7 = (bf16[24,1152]{1,0:T(8,128)(2,1)S(1)}, bf16[24,1152]{1,0:T(8,128)(2,1)S(1)}, u32[]{:S(2)}, u32[]{:S(2)}) collective-permute-start(bf16[24,1152]{1,0:T(8,128)(2,1)S(1)} %get-tuple-element.19.upper_ref), channel_id=1, source_target_pairs={{0,1},{1,0},{2,3},{3,2},{4,5},{5,4},{6,7},{7,6},{8,9},{9,8},{10,11... | collective-permute-start | bytes 165896 | tf_op jit(solution)/shard_map/ppermute | solution.py:19
  18.5 12.2 %slice-start = ((s8[14155776]{0:T(1024)(128)(4,1)}), s8[4194304]{0:T(1024)(128)(4,1)S(1)}, s32[]{:S(2)}) async-start(s8[14155776]{0:T(1024)(128)(4,1)} %bitcast.92), calls=%async_computation | async-start | bytes 8388608
  18.5 12.2 %slice-start.1 = ((s8[14155776]{0:T(1024)(128)(4,1)}), s8[4194304]{0:T(1024)(128)(4,1)S(1)}, s32[]{:S(2)}) async-start(s8[14155776]{0:T(1024)(128)(4,1)} %bitcast.92), calls=%async_computation.1 | async-start | bytes 8388608
  18.5 12.2 %slice-start.2 = ((s8[14155776]{0:T(1024)(128)(4,1)}), s8[4194304]{0:T(1024)(128)(4,1)S(1)}, s32[]{:S(2)}) async-start(s8[14155776]{0:T(1024)(128)(4,1)} %bitcast.92), calls=%async_computation.2 | async-start | bytes 8388608
  18.5 4.8 %collective-permute-start.5 = (bf16[48,1152]{1,0:T(8,128)(2,1)S(1)}, bf16[48,1152]{1,0:T(8,128)(2,1)S(1)}, u32[]{:S(2)}, u32[]{:S(2)}) collective-permute-start(bf16[48,1152]{1,0:T(8,128)(2,1)S(1)} %shard_map.105), channel_id=1, source_target_pairs={{0,1},{1,0},{2,3},{3,2},{4,5},{5,4},{6,7},{7,6},{8,9},{9,8},{10,11... | collective-permute-start | bytes 331784 | tf_op jit(solution)/shard_map/ppermute | solution.py:19
  20.3 6.4 %collective-permute-start.8 = (bf16[48,1152]{1,0:T(8,128)(2,1)S(1)}, bf16[48,1152]{1,0:T(8,128)(2,1)S(1)}, u32[]{:S(2)}, u32[]{:S(2)}) collective-permute-start(bf16[48,1152]{1,0:T(8,128)(2,1)S(1)} %shard_map.106), channel_id=1, source_target_pairs={{0,2},{1,3},{2,0},{3,1},{4,6},{5,7},{6,4},{7,5},{8,10},{9,11},{10,... | collective-permute-start | bytes 331784 | tf_op jit(solution)/shard_map/ppermute | solution.py:19
  24.4 5.5 %collective-permute-start.10 = (bf16[2,96,576]{2,1,0:T(8,128)(2,1)S(1)}, bf16[2,96,576]{2,1,0:T(8,128)(2,1)S(1)}, u32[]{:S(2)}, u32[]{:S(2)}) collective-permute-start(bf16[2,96,576]{2,1,0:T(8,128)(2,1)S(1)} %pad_maximum_fusion.1), channel_id=1, source_target_pairs={{0,16},{16,0},{1,17},{17,1},{2,18},{18,2},{3,19},{19,3},{4,20},{20... | collective-permute-start | bytes 663560 | tf_op jit(solution)/shard_map/ppermute | solution.py:19
  26.1 4.4 %collective-permute-start.6 = (f32[96,2048]{1,0:T(8,128)S(1)}, f32[96,2048]{1,0:T(8,128)S(1)}, u32[]{:S(2)}, u32[]{:S(2)}) collective-permute-start(f32[96,2048]{1,0:T(8,128)S(1)} %fusion.14), channel_id=1, source_target_pairs={{0,16},{16,0},{1,17},{17,1},{2,18},{18,2},{3,19},{19,3},{4,20},{20... | collective-permute-start | bytes 2359304 | tf_op jit(solution)/shard_map/ppermute | solution.py:19
  27.8 2.3 %collective-permute-start.18 = (bf16[2,96,576]{2,1,0:T(8,128)(2,1)S(1)}, bf16[2,96,576]{2,1,0:T(8,128)(2,1)S(1)}, u32[]{:S(2)}, u32[]{:S(2)}) collective-permute-start(bf16[2,96,576]{2,1,0:T(8,128)(2,1)S(1)} %pad_maximum_fusion.2), channel_id=1, source_target_pairs={{0,16},{16,0},{1,17},{17,1},{2,18},{18,2},{3,19},{19,3},{4,20},{20... | collective-permute-start | bytes 663560 | tf_op jit(solution)/shard_map/ppermute | solution.py:19
  29.4 3.8 %collective-permute-start.9 = (f32[96,2048]{1,0:T(8,128)S(1)}, f32[96,2048]{1,0:T(8,128)S(1)}, u32[]{:S(2)}, u32[]{:S(2)}) collective-permute-start(f32[96,2048]{1,0:T(8,128)S(1)} %fusion.12), channel_id=1, source_target_pairs={{0,16},{16,0},{1,17},{17,1},{2,18},{18,2},{3,19},{19,3},{4,20},{20... | collective-permute-start | bytes 2359304 | tf_op jit(solution)/shard_map/ppermute | solution.py:19
  31.7 5.6 %collective-permute-start.11 = (bf16[48,1152]{1,0:T(8,128)(2,1)S(1)}, bf16[48,1152]{1,0:T(8,128)(2,1)S(1)}, u32[]{:S(2)}, u32[]{:S(2)}) collective-permute-start(bf16[48,1152]{1,0:T(8,128)(2,1)S(1)} %slice.270), channel_id=1, source_target_pairs={{0,1},{1,0},{2,3},{3,2},{4,5},{5,4},{6,7},{7,6},{8,9},{9,8},{10,11... | collective-permute-start | bytes 331784 | tf_op jit(solution)/shard_map/ppermute | solution.py:19
  35.6 5.4 %collective-permute-start.19 = (bf16[48,1152]{1,0:T(8,128)(2,1)S(1)}, bf16[48,1152]{1,0:T(8,128)(2,1)S(1)}, u32[]{:S(2)}, u32[]{:S(2)}) collective-permute-start(bf16[48,1152]{1,0:T(8,128)(2,1)S(1)} %pad_maximum_fusion.9), channel_id=1, source_target_pairs={{0,2},{1,3},{2,0},{3,1},{4,6},{5,7},{6,4},{7,5},{8,10},{9,11},{10,... | collective-permute-start | bytes 331784 | tf_op jit(solution)/shard_map/ppermute | solution.py:19
  37.3 4.6 %collective-permute-start.12 = (bf16[24,1152]{1,0:T(8,128)(2,1)S(1)}, bf16[24,1152]{1,0:T(8,128)(2,1)S(1)}, u32[]{:S(2)}, u32[]{:S(2)}) collective-permute-start(bf16[24,1152]{1,0:T(8,128)(2,1)S(1)} %slice.272), channel_id=1, source_target_pairs={{0,2},{1,3},{2,0},{3,1},{4,6},{5,7},{6,4},{7,5},{8,10},{9,11},{10,... | collective-permute-start | bytes 165896 | tf_op jit(solution)/shard_map/ppermute | solution.py:19
  41.1 4.4 %collective-permute-start.20 = (bf16[24,1152]{1,0:T(8,128)(2,1)S(1)}, bf16[24,1152]{1,0:T(8,128)(2,1)S(1)}, u32[]{:S(2)}, u32[]{:S(2)}) collective-permute-start(bf16[24,1152]{1,0:T(8,128)(2,1)S(1)} %slice.271), channel_id=1, source_target_pairs={{0,1},{1,0},{2,3},{3,2},{4,5},{5,4},{6,7},{7,6},{8,9},{9,8},{10,11... | collective-permute-start | bytes 165896 | tf_op jit(solution)/shard_map/ppermute | solution.py:19
  41.9 7.0 %collective-permute-start.13 = (bf16[24,1152]{1,0:T(8,128)(2,1)S(1)}, bf16[24,1152]{1,0:T(8,128)(2,1)S(1)}, u32[]{:S(2)}, u32[]{:S(2)}) collective-permute-start(bf16[24,1152]{1,0:T(8,128)(2,1)S(1)} %fusion.106), channel_id=1, source_target_pairs={{0,8},{1,9},{2,10},{3,11},{4,12},{5,13},{6,14},{7,15},{8,0},{9,1},... | collective-permute-start | bytes 165896 | tf_op jit(solution)/shard_map/ppermute | solution.py:19
  42.0 7.1 %collective-permute-start.14 = (bf16[24,1152]{1,0:T(8,128)(2,1)S(1)}, bf16[24,1152]{1,0:T(8,128)(2,1)S(1)}, u32[]{:S(2)}, u32[]{:S(2)}) collective-permute-start(bf16[24,1152]{1,0:T(8,128)(2,1)S(1)} %fusion.106), channel_id=1, source_target_pairs={{0,12},{1,13},{2,14},{3,15},{4,8},{5,9},{6,10},{7,11},{8,4},{9,5},... | collective-permute-start | bytes 165896 | tf_op jit(solution)/shard_map/ppermute | solution.py:19
  43.0 6.7 %collective-permute-start.15 = (bf16[24,1152]{1,0:T(8,128)(2,1)S(1)}, bf16[24,1152]{1,0:T(8,128)(2,1)S(1)}, u32[]{:S(2)}, u32[]{:S(2)}) collective-permute-start(bf16[24,1152]{1,0:T(8,128)(2,1)S(1)} %fusion.106), channel_id=1, source_target_pairs={{0,4},{1,5},{2,6},{3,7},{4,0},{5,1},{6,2},{7,3},{8,12},{9,13},{10,... | collective-permute-start | bytes 165896 | tf_op jit(solution)/shard_map/ppermute | solution.py:19
  45.5 7.1 %collective-permute-start.21 = (bf16[24,1152]{1,0:T(8,128)(2,1)S(1)}, bf16[24,1152]{1,0:T(8,128)(2,1)S(1)}, u32[]{:S(2)}, u32[]{:S(2)}) collective-permute-start(bf16[24,1152]{1,0:T(8,128)(2,1)S(1)} %fusion.107), channel_id=1, source_target_pairs={{0,8},{1,9},{2,10},{3,11},{4,12},{5,13},{6,14},{7,15},{8,0},{9,1},... | collective-permute-start | bytes 165896 | tf_op jit(solution)/shard_map/ppermute | solution.py:19
  46.5 6.1 %collective-permute-start.22 = (bf16[24,1152]{1,0:T(8,128)(2,1)S(1)}, bf16[24,1152]{1,0:T(8,128)(2,1)S(1)}, u32[]{:S(2)}, u32[]{:S(2)}) collective-permute-start(bf16[24,1152]{1,0:T(8,128)(2,1)S(1)} %fusion.107), channel_id=1, source_target_pairs={{0,12},{1,13},{2,14},{3,15},{4,8},{5,9},{6,10},{7,11},{8,4},{9,5},... | collective-permute-start | bytes 165896 | tf_op jit(solution)/shard_map/ppermute | solution.py:19
  48.9 4.3 %collective-permute-start.23 = (bf16[24,1152]{1,0:T(8,128)(2,1)S(1)}, bf16[24,1152]{1,0:T(8,128)(2,1)S(1)}, u32[]{:S(2)}, u32[]{:S(2)}) collective-permute-start(bf16[24,1152]{1,0:T(8,128)(2,1)S(1)} %fusion.107), channel_id=1, source_target_pairs={{0,4},{1,5},{2,6},{3,7},{4,0},{5,1},{6,2},{7,3},{8,12},{9,13},{10,... | collective-permute-start | bytes 165896 | tf_op jit(solution)/shard_map/ppermute | solution.py:19
  49.7 5.2 %collective-permute-start.16 = (bf16[24,1152]{1,0:T(8,128)(2,1)S(1)}, bf16[24,1152]{1,0:T(8,128)(2,1)S(1)}, u32[]{:S(2)}, u32[]{:S(2)}) collective-permute-start(bf16[24,1152]{1,0:T(8,128)(2,1)S(1)} %shard_map.107), channel_id=1, source_target_pairs={{0,2},{1,3},{2,0},{3,1},{4,6},{5,7},{6,4},{7,5},{8,10},{9,11},{10,... | collective-permute-start | bytes 165896 | tf_op jit(solution)/shard_map/ppermute | solution.py:19
  53.2 4.2 %collective-permute-start.24 = (bf16[24,1152]{1,0:T(8,128)(2,1)S(1)}, bf16[24,1152]{1,0:T(8,128)(2,1)S(1)}, u32[]{:S(2)}, u32[]{:S(2)}) collective-permute-start(bf16[24,1152]{1,0:T(8,128)(2,1)S(1)} %shard_map.108), channel_id=1, source_target_pairs={{0,1},{1,0},{2,3},{3,2},{4,5},{5,4},{6,7},{7,6},{8,9},{9,8},{10,11... | collective-permute-start | bytes 165896 | tf_op jit(solution)/shard_map/ppermute | solution.py:19
  54.9 4.8 %collective-permute-start.17 = (bf16[48,1152]{1,0:T(8,128)(2,1)S(1)}, bf16[48,1152]{1,0:T(8,128)(2,1)S(1)}, u32[]{:S(2)}, u32[]{:S(2)}) collective-permute-start(bf16[48,1152]{1,0:T(8,128)(2,1)S(1)} %pad_maximum_fusion.8), channel_id=1, source_target_pairs={{0,1},{1,0},{2,3},{3,2},{4,5},{5,4},{6,7},{7,6},{8,9},{9,8},{10,11... | collective-permute-start | bytes 331784 | tf_op jit(solution)/shard_map/ppermute | solution.py:19
  57.4 4.8 %collective-permute-start.25 = (bf16[48,1152]{1,0:T(8,128)(2,1)S(1)}, bf16[48,1152]{1,0:T(8,128)(2,1)S(1)}, u32[]{:S(2)}, u32[]{:S(2)}) collective-permute-start(bf16[48,1152]{1,0:T(8,128)(2,1)S(1)} %pad_maximum_fusion.10), channel_id=1, source_target_pairs={{0,2},{1,3},{2,0},{3,1},{4,6},{5,7},{6,4},{7,5},{8,10},{9,11},{10,... | collective-permute-start | bytes 331784 | tf_op jit(solution)/shard_map/ppermute | solution.py:19
  65.5 6.9 %collective-permute-start.26 = (bf16[2,96,2048]{2,1,0:T(8,128)(2,1)S(1)}, bf16[2,96,2048]{2,1,0:T(8,128)(2,1)S(1)}, u32[]{:S(2)}, u32[]{:S(2)}) collective-permute-start(bf16[2,96,2048]{2,1,0:T(8,128)(2,1)S(1)} %pad_maximum_fusion.own_ref), channel_id=1, source_target_pairs={{0,16},{16,0},{1,17},{17,1},{2,18},{18,2},{3,19},{19,3},{4,20},{20... | collective-permute-start | bytes 2359304 | tf_op jit(solution)/shard_map/ppermute | solution.py:19
  (5 other events, 18.1 us)

commit v5 on v4

--- a/solution.py
+++ b/solution.py
@@ -99,7 +99,7 @@
     bits = bits_of("feat")[2:]
     if len(bits) == 2:
         sent = quarter.astype(jnp.bfloat16)
-        offsets = (bits[1], bits[0] | bits[1], bits[0])
+        offsets = ((bits[1], bits[0] | bits[1], bits[0]), (bits[0], bits[0] | bits[1], bits[1]))[layer]
         received = [swap(sent, "feat", b) for b in offsets]
         for other in received[:-1]:
             quarter = quarter + other.astype(jnp.float32)
@@ -174,24 +174,29 @@
 nt = ((1,), (1,))
 
 
-def decoder_gradient(lefts, right, scale, slots, into=None):
+def decoder_gradient(lefts, rights, pieces, scale, into=None):
     tokens, features = lefts[0].shape
-    cols = right.shape[1]
-    count = len(lefts)
-    chunks = row_chunks(features, 256)
+    cols = rights[0].shape[1]
+    count = len(lefts) + len(rights)
+    tiles = [
+        (a, e, slot, first + at, size)
+        for a, e, slot, first, rows in pieces
+        for at, size in row_chunks(rows, 256)
+    ]
+    total = sum(size for *_, size in tiles)
 
     def kernel(*refs):
-        left_refs, right_ref = refs[:count], refs[count]
+        left_refs, right_refs = refs[: len(lefts)], refs[len(lefts) : count]
         out_ref, held, sems = refs[-3:]
-        right_value = right_ref[...]
         copies = []
-        for k, left_ref in enumerate(left_refs):
-            for c, (at, size) in enumerate(chunks):
-                rows = pl.ds(at, size)
-                held[k, rows] = (scale * dot(left_ref[:, rows], right_value, tn)).astype(jnp.bfloat16)
-                target = out_ref.at[slots[k], rows]
-                copies.append(pltpu.make_async_copy(held.at[k, rows], target, sems.at[k, c]))
-                copies[-1].start()
+        place = 0
+        for k, (a, e, slot, at, size) in enumerate(tiles):
+            rows, kept = pl.ds(at, size), pl.ds(place, size)
+            value = scale * dot(left_refs[a][:, rows], right_refs[e][...], tn)
+            held[kept] = value.astype(jnp.bfloat16)
+            copies.append(pltpu.make_async_copy(held.at[kept], out_ref.at[slot, rows], sems.at[k]))
+            copies[-1].start()
+            place += size
         for copy in copies:
             copy.wait()
 
@@ -201,20 +206,18 @@
     return pl.pallas_call(
         kernel,
         out_shape=jax.ShapeDtypeStruct((3, features, cols), jnp.bfloat16),
-        in_specs=[vmem] * (count + 1) + [hbm] * len(more),
+        in_specs=[vmem] * count + [hbm] * len(more),
         out_specs=hbm,
-        input_output_aliases={count + 1: 0} if more else {},
+        input_output_aliases={count: 0} if more else {},
         scratch_shapes=[
-            pltpu.VMEM((count, features, cols), jnp.bfloat16),
-            pltpu.SemaphoreType.DMA((count, len(chunks))),
+            pltpu.VMEM((total, cols), jnp.bfloat16),
+            pltpu.SemaphoreType.DMA((len(tiles),)),
         ],
-        compiler_params=pltpu.CompilerParams(vmem_limit_bytes=(8 + 8 * count) << 20),
+        compiler_params=pltpu.CompilerParams(vmem_limit_bytes=28 << 20),
         cost_estimate=pl.CostEstimate(
-            flops=2 * count * tokens * features * cols,
-            bytes_accessed=2 * count * features * cols,
-            transcendentals=0,
+            flops=2 * tokens * total * cols, bytes_accessed=2 * total * cols, transcendentals=0
         ),
-    )(*lefts, right, *more)
+    )(*lefts, *rights, *more)
 
 
 def encoder_gradient(active, own, received, normed, scale):
@@ -284,7 +287,9 @@
     )
     loss_scale = 1.0 / math.sqrt(tokens)
     errors = [gather_outer(sum_tokens(partial_first, 0), 0, 0), gather_outer(sum_tokens(partial_second, 1), 1, 0)]
-    grad_decoder = decoder_gradient([active[0]], errors[0], loss_scale, (0,))
+    features = decoder.shape[1]
+    early = features // 4
+    grad_decoder = decoder_gradient(active[:1], errors[:1], [(0, 0, 0, 0, early)], loss_scale)
     back_first = lax.optimization_barrier(dot(errors[0], decoder[0], nt))
     back_first = back_first + dot(errors[1], decoder[1], nt)
     back_second = dot(errors[1], decoder[2], nt)
@@ -293,7 +298,8 @@
     for bit in inner:
         own = own + swap(own, "mp", bit)
     received = swap(own, "mp", last)
-    grad_decoder = decoder_gradient(active, errors[1], loss_scale, (1, 2), grad_decoder)
+    rest = [(0, 0, 0, early, features - early), (0, 1, 1, 0, features), (1, 1, 2, 0, features)]
+    grad_decoder = decoder_gradient(active, errors, rest, loss_scale, grad_decoder)
     grad_encoder, grad_bias = encoder_gradient(active, own, received, normed, loss_scale)
     return (grad_encoder, grad_bias, grad_decoder)
 

time: 77.5 us -> 77.5 us (level)
  transfers between devices with their start and end apart: 27 -> 27, of which waited for: 15 -> 13; matrix products, arithmetic and copies ran while one was open for 14% -> 14% of each run, Pallas kernels for 9% -> 9%
where the time goes in v5:
time: 77.5 us; the launch traced here: 77.3 us
  starting transfers between devices  30.7 us (40%)
  waiting for transfers between devices  18.5 us (24%)
  matrix products  13.3 us (17%)
  Pallas kernels  11.7 us (15%)
  between operations  1.25 us (2%)
  other arithmetic  0.93 us (1%)
  local copies, waits for them, and re-layouts  0.9 us (1%)
    ppermute x27, starting transfers between devices, swap(): return lax.ppermute(values, axis, [(i, i ^ bit) for i in range(size)])  30.7 us
    ppermute x27, waiting for transfers between devices, swap(): return lax.ppermute(values, axis, [(i, i ^ bit) for i in range(size)])  18.5 us
    dot_general x14, matrix products, dot(): lax.dot_general(a, b, (contract, ((), ())), preferred_element_type=jnp.fl...  13.3 us
    pallas_call x2, Pallas kernels, decoder_gradient(): pl.pallas_call(kernel, out_shape=jax.ShapeDtypeStruct((3, features, cols)...  6.72 us
    pallas_call x1, Pallas kernels, encoder_gradient(): pl.pallas_call(kernel, out_shape=(jax.ShapeDtypeStruct((2, features, cols...  4.73 us
  transfers between devices with their start and end apart: 27, of which 13 were waited for; matrix products, arithmetic and copies ran while one was open for 14% of the time, Pallas kernels for 9%

profile of v5, /device:TPU:0, one launch (start us, length us, event | category | flops | bytes accessed | tf_op | source)
XLA Modules:
  0.0 77.3 jit_solution(129745061145085813)
XLA Ops:
  2.9 4.0 %collective-permute-start.1 = (bf16[6,2304]{1,0:T(8,128)(2,1)S(1)}, bf16[6,2304]{1,0:T(8,128)(2,1)S(1)}, u32[]{:S(2)}, u32[]{:S(2)}) collective-permute-start(bf16[6,2304]{1,0:T(8,128)(2,1)S(1)} %shard_map.104), channel_id=1, source_target_pairs={{0,8},{1,9},{2,10},{3,11},{4,12},{5,13},{6,14},{7,15},{8,0},{9,1},... | collective-permute-start | bytes 82952 | tf_op jit(solution)/shard_map/ppermute | solution.py:19
  6.8 1.6 %collective-permute-start.2 = (bf16[6,2304]{1,0:T(8,128)(2,1)S(1)}, bf16[6,2304]{1,0:T(8,128)(2,1)S(1)}, u32[]{:S(2)}, u32[]{:S(2)}) collective-permute-start(bf16[6,2304]{1,0:T(8,128)(2,1)S(1)} %shard_map.104), channel_id=1, source_target_pairs={{0,4},{1,5},{2,6},{3,7},{4,0},{5,1},{6,2},{7,3},{8,12},{9,13},{10,... | collective-permute-start | bytes 82952 | tf_op jit(solution)/shard_map/ppermute | solution.py:19
  8.8 2.0 %collective-permute-done.2 = bf16[6,2304]{1,0:T(8,128)(2,1)S(1)} collective-permute-done((bf16[6,2304]{1,0:T(8,128)(2,1)S(1)}, bf16[6,2304]{1,0:T(8,128)(2,1)S(1)}, u32[]{:S(2)}, u32[]{:S(2)}) %collective-permute-start.2) | collective-permute-done | bytes 27680 | tf_op jit(solution)/shard_map/ppermute | solution.py:19
  10.8 3.4 %collective-permute-done.3 = bf16[6,2304]{1,0:T(8,128)(2,1)S(1)} collective-permute-done((bf16[6,2304]{1,0:T(8,128)(2,1)S(1)}, bf16[6,2304]{1,0:T(8,128)(2,1)S(1)}, u32[]{:S(2)}, u32[]{:S(2)}) %collective-permute-start.3) | collective-permute-done | bytes 27680 | tf_op jit(solution)/shard_map/ppermute | solution.py:19
  14.3 1.6 %collective-permute-start.4 = (bf16[24,1152]{1,0:T(8,128)(2,1)S(1)}, bf16[24,1152]{1,0:T(8,128)(2,1)S(1)}, u32[]{:S(2)}, u32[]{:S(2)}) collective-permute-start(bf16[24,1152]{1,0:T(8,128)(2,1)S(1)} %get-tuple-element.20.upper_ref), channel_id=1, source_target_pairs={{0,2},{1,3},{2,0},{3,1},{4,6},{5,7},{6,4},{7,5},{8,10},{9,11},{10,... | collective-permute-start | bytes 165896 | tf_op jit(solution)/shard_map/ppermute | solution.py:19
  15.9 1.5 %collective-permute-start.7 = (bf16[24,1152]{1,0:T(8,128)(2,1)S(1)}, bf16[24,1152]{1,0:T(8,128)(2,1)S(1)}, u32[]{:S(2)}, u32[]{:S(2)}) collective-permute-start(bf16[24,1152]{1,0:T(8,128)(2,1)S(1)} %get-tuple-element.19.upper_ref), channel_id=1, source_target_pairs={{0,1},{1,0},{2,3},{3,2},{4,5},{5,4},{6,7},{7,6},{8,9},{9,8},{10,11... | collective-permute-start | bytes 165896 | tf_op jit(solution)/shard_map/ppermute | solution.py:19
  17.4 1.1 %collective-permute-done.4.lower_ref = bf16[24,1152]{1,0:T(8,128)(2,1)S(1)} collective-permute-done((bf16[24,1152]{1,0:T(8,128)(2,1)S(1)}, bf16[24,1152]{1,0:T(8,128)(2,1)S(1)}, u32[]{:S(2)}, u32[]{:S(2)}) %collective-permute-start.4) | collective-permute-done | bytes 55328 | tf_op jit(solution)/shard_map/ppermute | solution.py:19
  18.5 1.6 %collective-permute-start.5 = (bf16[48,1152]{1,0:T(8,128)(2,1)S(1)}, bf16[48,1152]{1,0:T(8,128)(2,1)S(1)}, u32[]{:S(2)}, u32[]{:S(2)}) collective-permute-start(bf16[48,1152]{1,0:T(8,128)(2,1)S(1)} %shard_map.105), channel_id=1, source_target_pairs={{0,1},{1,0},{2,3},{3,2},{4,5},{5,4},{6,7},{7,6},{8,9},{9,8},{10,11... | collective-permute-start | bytes 331784 | tf_op jit(solution)/shard_map/ppermute | solution.py:19
  20.3 1.4 %collective-permute-start.8 = (bf16[48,1152]{1,0:T(8,128)(2,1)S(1)}, bf16[48,1152]{1,0:T(8,128)(2,1)S(1)}, u32[]{:S(2)}, u32[]{:S(2)}) collective-permute-start(bf16[48,1152]{1,0:T(8,128)(2,1)S(1)} %shard_map.106), channel_id=1, source_target_pairs={{0,2},{1,3},{2,0},{3,1},{4,6},{5,7},{6,4},{7,5},{8,10},{9,11},{10,... | collective-permute-start | bytes 331784 | tf_op jit(solution)/shard_map/ppermute | solution.py:19
  21.7 1.6 %collective-permute-done.5 = bf16[48,1152]{1,0:T(8,128)(2,1)S(1)} collective-permute-done((bf16[48,1152]{1,0:T(8,128)(2,1)S(1)}, bf16[48,1152]{1,0:T(8,128)(2,1)S(1)}, u32[]{:S(2)}, u32[]{:S(2)}) %collective-permute-start.5) | collective-permute-done | bytes 110624 | tf_op jit(solution)/shard_map/ppermute | solution.py:19
  24.5 1.6 %fusion.14 = f32[96,2048]{1,0:T(8,128)S(1)} fusion(bf16[2,2048,1152]{2,1,0:T(8,128)(2,1)S(1)} %copy-done.3, bf16[48,1152]{1,0:T(8,128)(2,1)S(1)} %collective-permute-done.5, bf16[48,1152]{1,0:T(8,128)(2,1)S(1)} %shard_map.105), kind=kOutput, calls=%fused_computation.14 | convolution fusion | flops 453427200 | bytes 5726208 | tf_op jit(solution)/shard_map/dot_general | solution.py:169
  27.9 1.5 %fusion.12 = f32[96,2048]{1,0:T(8,128)S(1)} fusion(bf16[2,2048,1152]{2,1,0:T(8,128)(2,1)S(1)} %copy-done.3, bf16[24,1152]{1,0:T(8,128)(2,1)S(1)} %get-tuple-element.18, bf16[24,1152]{1,0:T(8,128)(2,1)S(1)} %collective-permute-done.7.lower_ref, bf16[24,1152]{1,0:T(8,128)(2,1)S(1)} %get-tuple-element.17, bf16[24,1152]{1,0:T(8,128)(2,1)S(1)} %get-tuple-element.19.upper_ref), kind=kOutput, calls=%fused_computation.12 | convolution fusion | flops 453869568 | bytes 5726208 | tf_op jit(solution)/shard_map/dot_general | solution.py:169
  31.7 1.6 %collective-permute-start.11 = (bf16[48,1152]{1,0:T(8,128)(2,1)S(1)}, bf16[48,1152]{1,0:T(8,128)(2,1)S(1)}, u32[]{:S(2)}, u32[]{:S(2)}) collective-permute-start(bf16[48,1152]{1,0:T(8,128)(2,1)S(1)} %slice.270), channel_id=1, source_target_pairs={{0,1},{1,0},{2,3},{3,2},{4,5},{5,4},{6,7},{7,6},{8,9},{9,8},{10,11... | collective-permute-start | bytes 331784 | tf_op jit(solution)/shard_map/ppermute | solution.py:19
  35.6 1.6 %collective-permute-start.19 = (bf16[48,1152]{1,0:T(8,128)(2,1)S(1)}, bf16[48,1152]{1,0:T(8,128)(2,1)S(1)}, u32[]{:S(2)}, u32[]{:S(2)}) collective-permute-start(bf16[48,1152]{1,0:T(8,128)(2,1)S(1)} %pad_maximum_fusion.9), channel_id=1, source_target_pairs={{0,2},{1,3},{2,0},{3,1},{4,6},{5,7},{6,4},{7,5},{8,10},{9,11},{10,... | collective-permute-start | bytes 331784 | tf_op jit(solution)/shard_map/ppermute | solution.py:19
  37.3 1.1 %collective-permute-start.12 = (bf16[24,1152]{1,0:T(8,128)(2,1)S(1)}, bf16[24,1152]{1,0:T(8,128)(2,1)S(1)}, u32[]{:S(2)}, u32[]{:S(2)}) collective-permute-start(bf16[24,1152]{1,0:T(8,128)(2,1)S(1)} %slice.272), channel_id=1, source_target_pairs={{0,2},{1,3},{2,0},{3,1},{4,6},{5,7},{6,4},{7,5},{8,10},{9,11},{10,... | collective-permute-start | bytes 165896 | tf_op jit(solution)/shard_map/ppermute | solution.py:19
  38.3 2.7 %collective-permute-done.19 = bf16[48,1152]{1,0:T(8,128)(2,1)S(1)} collective-permute-done((bf16[48,1152]{1,0:T(8,128)(2,1)S(1)}, bf16[48,1152]{1,0:T(8,128)(2,1)S(1)}, u32[]{:S(2)}, u32[]{:S(2)}) %collective-permute-start.19) | collective-permute-done | bytes 110624 | tf_op jit(solution)/shard_map/ppermute | solution.py:19
  42.0 1.0 %collective-permute-start.14 = (bf16[24,1152]{1,0:T(8,128)(2,1)S(1)}, bf16[24,1152]{1,0:T(8,128)(2,1)S(1)}, u32[]{:S(2)}, u32[]{:S(2)}) collective-permute-start(bf16[24,1152]{1,0:T(8,128)(2,1)S(1)} %fusion.106), channel_id=1, source_target_pairs={{0,12},{1,13},{2,14},{3,15},{4,8},{5,9},{6,10},{7,11},{8,4},{9,5},... | collective-permute-start | bytes 165896 | tf_op jit(solution)/shard_map/ppermute | solution.py:19
  43.0 2.5 %collective-permute-start.15 = (bf16[24,1152]{1,0:T(8,128)(2,1)S(1)}, bf16[24,1152]{1,0:T(8,128)(2,1)S(1)}, u32[]{:S(2)}, u32[]{:S(2)}) collective-permute-start(bf16[24,1152]{1,0:T(8,128)(2,1)S(1)} %fusion.106), channel_id=1, source_target_pairs={{0,4},{1,5},{2,6},{3,7},{4,0},{5,1},{6,2},{7,3},{8,12},{9,13},{10,... | collective-permute-start | bytes 165896 | tf_op jit(solution)/shard_map/ppermute | solution.py:19
  45.6 2.4 %collective-permute-start.22 = (bf16[24,1152]{1,0:T(8,128)(2,1)S(1)}, bf16[24,1152]{1,0:T(8,128)(2,1)S(1)}, u32[]{:S(2)}, u32[]{:S(2)}) collective-permute-start(bf16[24,1152]{1,0:T(8,128)(2,1)S(1)} %fusion.107), channel_id=1, source_target_pairs={{0,12},{1,13},{2,14},{3,15},{4,8},{5,9},{6,10},{7,11},{8,4},{9,5},... | collective-permute-start | bytes 165896 | tf_op jit(solution)/shard_map/ppermute | solution.py:19
  48.0 1.0 %collective-permute-start.23 = (bf16[24,1152]{1,0:T(8,128)(2,1)S(1)}, bf16[24,1152]{1,0:T(8,128)(2,1)S(1)}, u32[]{:S(2)}, u32[]{:S(2)}) collective-permute-start(bf16[24,1152]{1,0:T(8,128)(2,1)S(1)} %fusion.107), channel_id=1, source_target_pairs={{0,8},{1,9},{2,10},{3,11},{4,12},{5,13},{6,14},{7,15},{8,0},{9,1},... | collective-permute-start | bytes 165896 | tf_op jit(solution)/shard_map/ppermute | solution.py:19
  49.1 1.6 %collective-permute-start.16 = (bf16[24,1152]{1,0:T(8,128)(2,1)S(1)}, bf16[24,1152]{1,0:T(8,128)(2,1)S(1)}, u32[]{:S(2)}, u32[]{:S(2)}) collective-permute-start(bf16[24,1152]{1,0:T(8,128)(2,1)S(1)} %shard_map.107), channel_id=1, source_target_pairs={{0,2},{1,3},{2,0},{3,1},{4,6},{5,7},{6,4},{7,5},{8,10},{9,11},{10,... | collective-permute-start | bytes 165896 | tf_op jit(solution)/shard_map/ppermute | solution.py:19
  51.7 1.5 %collective-permute-done.23.received_ref = bf16[24,1152]{1,0:T(8,128)(2,1)S(1)} collective-permute-done((bf16[24,1152]{1,0:T(8,128)(2,1)S(1)}, bf16[24,1152]{1,0:T(8,128)(2,1)S(1)}, u32[]{:S(2)}, u32[]{:S(2)}) %collective-permute-start.23) | collective-permute-done | bytes 55328 | tf_op jit(solution)/shard_map/ppermute | solution.py:19
  53.2 1.2 %collective-permute-start.24 = (bf16[24,1152]{1,0:T(8,128)(2,1)S(1)}, bf16[24,1152]{1,0:T(8,128)(2,1)S(1)}, u32[]{:S(2)}, u32[]{:S(2)}) collective-permute-start(bf16[24,1152]{1,0:T(8,128)(2,1)S(1)} %shard_map.108), channel_id=1, source_target_pairs={{0,1},{1,0},{2,3},{3,2},{4,5},{5,4},{6,7},{7,6},{8,9},{9,8},{10,11... | collective-permute-start | bytes 165896 | tf_op jit(solution)/shard_map/ppermute | solution.py:19
  55.4 2.0 %collective-permute-done.24 = bf16[24,1152]{1,0:T(8,128)(2,1)S(1)} collective-permute-done((bf16[24,1152]{1,0:T(8,128)(2,1)S(1)}, bf16[24,1152]{1,0:T(8,128)(2,1)S(1)}, u32[]{:S(2)}, u32[]{:S(2)}) %collective-permute-start.24) | collective-permute-done | bytes 55328 | tf_op jit(solution)/shard_map/ppermute | solution.py:19
  57.4 1.5 %collective-permute-start.25 = (bf16[48,1152]{1,0:T(8,128)(2,1)S(1)}, bf16[48,1152]{1,0:T(8,128)(2,1)S(1)}, u32[]{:S(2)}, u32[]{:S(2)}) collective-permute-start(bf16[48,1152]{1,0:T(8,128)(2,1)S(1)} %pad_maximum_fusion.10), channel_id=1, source_target_pairs={{0,2},{1,3},{2,0},{3,1},{4,6},{5,7},{6,4},{7,5},{8,10},{9,11},{10,... | collective-permute-start | bytes 331784 | tf_op jit(solution)/shard_map/ppermute | solution.py:19
  59.2 1.5 %fusion.8 = f32[96,2048]{1,0:T(8,128)S(1)} fusion(bf16[3,2048,1152]{2,1,0:T(8,128)(2,1)S(1)} %bitcast.93, bf16[48,1152]{1,0:T(8,128)(2,1)S(1)} %collective-permute-done.17, bf16[24,1152]{1,0:T(8,128)(2,1)S(1)} %collective-permute-done.16, bf16[24,1152]{1,0:T(8,128)(2,1)S(1)} %shard_map.107), kind=kOutput, calls=%fused_computation.8 | convolution fusion | flops 453648384 | bytes 5726208 | tf_op jit(solution)/shard_map/dot_general | solution.py:169
  60.8 1.4 %collective-permute-done.25 = bf16[48,1152]{1,0:T(8,128)(2,1)S(1)} collective-permute-done((bf16[48,1152]{1,0:T(8,128)(2,1)S(1)}, bf16[48,1152]{1,0:T(8,128)(2,1)S(1)}, u32[]{:S(2)}, u32[]{:S(2)}) %collective-permute-start.25) | collective-permute-done | bytes 110624 | tf_op jit(solution)/shard_map/ppermute | solution.py:19
  62.2 1.5 %fusion.4 = f32[96,2048]{1,0:T(8,128)S(1)} fusion(bf16[3,2048,1152]{2,1,0:T(8,128)(2,1)S(1)} %bitcast.93, bf16[24,1152]{1,0:T(8,128)(2,1)S(1)} %get-tuple-element.16, bf16[24,1152]{1,0:T(8,128)(2,1)S(1)} %collective-permute-done.24, bf16[24,1152]{1,0:T(8,128)(2,1)S(1)} %get-tuple-element.15, bf16[24,1152]{1,0:T(8,128)(2,1)S(1)} %shard_map.108), kind=kOutput, calls=%fused_computation.4 | convolution fusion | flops 453869568 | bytes 5726208 | tf_op jit(solution)/shard_map/dot_general | solution.py:169
  63.9 1.6 %fusion.33 = bf16[1,96,2048]{2,1,0:T(8,128)(2,1)S(1)} fusion(bf16[3,2048,1152]{2,1,0:T(8,128)(2,1)S(1)} %bitcast.93, bf16[24,1152]{1,0:T(8,128)(2,1)S(1)} %get-tuple-element.16, bf16[24,1152]{1,0:T(8,128)(2,1)S(1)} %collective-permute-done.24, bf16[24,1152]{1,0:T(8,128)(2,1)S(1)} %get-tuple-element.15, bf16[24,1152]{1,0:T(8,128)(2,1)S(1)} %shard_map.108), kind=kOutput, calls=%fused_computation.28 | convolution fusion | flops 454066176 | bytes 5332992 | tf_op jit(solution)/shard_map/dot_general | solution.py:169
  65.7 1.4 %shard_map.110.refs_4_ = bf16[3,2048,1152]{2,1,0:T(8,128)(2,1)} custom-call(bf16[96,2048]{1,0:T(8,128)(2,1)S(1)} %maximum_convert_fusion.1.active_0.refs_0_, bf16[96,1152]{1,0:T(8,128)(2,1)S(1)} %pad_maximum_fusion.5.refs_1_.refs_2_), custom_call_target="tpu_custom_call" | custom-call | flops 113246208 | bytes 1179648 | tf_op jit(solution)/shard_map/pallas_call | solution.py:206
  67.1 5.3 %shard_map.111 = bf16[3,2048,1152]{2,1,0:T(8,128)(2,1)} custom-call(bf16[96,2048]{1,0:T(8,128)(2,1)S(1)} %maximum_convert_fusion.1.active_0.refs_0_, bf16[96,2048]{1,0:T(8,128)(2,1)S(1)} %maximum_convert_fusion.active_1.refs_1_, bf16[96,1152]{1,0:T(8,128)(2,1)S(1)} %pad_maximum_fusion.5.refs_1_.refs_2_, ...), custom_call_target="tpu_custom_call", output_to_operand_aliasing={{}: (4, {})} | custom-call | flops 1245708288 | bytes 12976128 | tf_op jit(solution)/shard_map/pallas_call | solution.py:206
  72.4 4.7 %shard_map.109 = (bf16[2,2048,1152]{2,1,0:T(8,128)(2,1)}, f32[2,2048]{1,0:T(2,128)}) custom-call(bf16[96,2048]{1,0:T(8,128)(2,1)S(1)} %maximum_convert_fusion.1.active_0.refs_0_, bf16[96,2048]{1,0:T(8,128)(2,1)S(1)} %maximum_convert_fusion.active_1.refs_1_, bf16[2,96,2048]{2,1,0:T(8,128)(2,1)S(1)} %pad_maximum_fusion.own_ref, ...), custom_call_target="tpu_custom_call" | custom-call | flops 905969664 | bytes 9437184 | tf_op jit(solution)/shard_map/pallas_call | solution.py:245
  (100 shorter events, 14.1 us)
Async XLA Ops:
  1.5 1.3 %collective-permute-start = (f32[2,6,1]{2,1,0:T(8,128)S(1)}, f32[2,6,1]{2,1,0:T(8,128)S(1)}, u32[]{:S(2)}, u32[]{:S(2)}) collective-permute-start(f32[2,6,1]{2,1,0:T(8,128)S(1)} %shard_map.103), channel_id=1, source_target_pairs={{0,16},{16,0},{1,17},{17,1},{2,18},{18,2},{3,19},{19,3},{4,20},{20... | collective-permute-start | bytes 152 | tf_op jit(solution)/shard_map/ppermute | solution.py:19
  2.9 5.9 %collective-permute-start.1 = (bf16[6,2304]{1,0:T(8,128)(2,1)S(1)}, bf16[6,2304]{1,0:T(8,128)(2,1)S(1)}, u32[]{:S(2)}, u32[]{:S(2)}) collective-permute-start(bf16[6,2304]{1,0:T(8,128)(2,1)S(1)} %shard_map.104), channel_id=1, source_target_pairs={{0,8},{1,9},{2,10},{3,11},{4,12},{5,13},{6,14},{7,15},{8,0},{9,1},... | collective-permute-start | bytes 82952 | tf_op jit(solution)/shard_map/ppermute | solution.py:19
  6.8 4.0 %collective-permute-start.2 = (bf16[6,2304]{1,0:T(8,128)(2,1)S(1)}, bf16[6,2304]{1,0:T(8,128)(2,1)S(1)}, u32[]{:S(2)}, u32[]{:S(2)}) collective-permute-start(bf16[6,2304]{1,0:T(8,128)(2,1)S(1)} %shard_map.104), channel_id=1, source_target_pairs={{0,4},{1,5},{2,6},{3,7},{4,0},{5,1},{6,2},{7,3},{8,12},{9,13},{10,... | collective-permute-start | bytes 82952 | tf_op jit(solution)/shard_map/ppermute | solution.py:19
  8.4 5.8 %collective-permute-start.3 = (bf16[6,2304]{1,0:T(8,128)(2,1)S(1)}, bf16[6,2304]{1,0:T(8,128)(2,1)S(1)}, u32[]{:S(2)}, u32[]{:S(2)}) collective-permute-start(bf16[6,2304]{1,0:T(8,128)(2,1)S(1)} %shard_map.104), channel_id=1, source_target_pairs={{0,12},{1,13},{2,14},{3,15},{4,8},{5,9},{6,10},{7,11},{8,4},{9,5},... | collective-permute-start | bytes 82952 | tf_op jit(solution)/shard_map/ppermute | solution.py:19
  14.3 4.2 %collective-permute-start.4 = (bf16[24,1152]{1,0:T(8,128)(2,1)S(1)}, bf16[24,1152]{1,0:T(8,128)(2,1)S(1)}, u32[]{:S(2)}, u32[]{:S(2)}) collective-permute-start(bf16[24,1152]{1,0:T(8,128)(2,1)S(1)} %get-tuple-element.20.upper_ref), channel_id=1, source_target_pairs={{0,2},{1,3},{2,0},{3,1},{4,6},{5,7},{6,4},{7,5},{8,10},{9,11},{10,... | collective-permute-start | bytes 165896 | tf_op jit(solution)/shard_map/ppermute | solution.py:19
  15.9 7.5 %copy-start.4 = (bf16[2,1152,576]{1,2,0:T(8,128)(2,1)S(1)}, bf16[2,1152,576]{1,2,0:T(8,128)(2,1)}, u32[]{:S(2)}) copy-start(bf16[2,1152,576]{1,2,0:T(8,128)(2,1)} %param.11) | copy-start | bytes 7962628
  15.9 8.0 %copy-start.5 = (bf16[2,1152,576]{1,2,0:T(8,128)(2,1)S(1)}, bf16[2,1152,576]{1,2,0:T(8,128)(2,1)}, u32[]{:S(2)}) copy-start(bf16[2,1152,576]{1,2,0:T(8,128)(2,1)} %param.10) | copy-start | bytes 7962628
  15.9 4.4 %collective-permute-start.7 = (bf16[24,1152]{1,0:T(8,128)(2,1)S(1)}, bf16[24,1152]{1,0:T(8,128)(2,1)S(1)}, u32[]{:S(2)}, u32[]{:S(2)}) collective-permute-start(bf16[24,1152]{1,0:T(8,128)(2,1)S(1)} %get-tuple-element.19.upper_ref), channel_id=1, source_target_pairs={{0,1},{1,0},{2,3},{3,2},{4,5},{5,4},{6,7},{7,6},{8,9},{9,8},{10,11... | collective-permute-start | bytes 165896 | tf_op jit(solution)/shard_map/ppermute | solution.py:19
  18.5 12.2 %slice-start = ((s8[14155776]{0:T(1024)(128)(4,1)}), s8[4194304]{0:T(1024)(128)(4,1)S(1)}, s32[]{:S(2)}) async-start(s8[14155776]{0:T(1024)(128)(4,1)} %bitcast.92), calls=%async_computation | async-start | bytes 8388608
  18.5 12.2 %slice-start.1 = ((s8[14155776]{0:T(1024)(128)(4,1)}), s8[4194304]{0:T(1024)(128)(4,1)S(1)}, s32[]{:S(2)}) async-start(s8[14155776]{0:T(1024)(128)(4,1)} %bitcast.92), calls=%async_computation.1 | async-start | bytes 8388608
  18.5 12.2 %slice-start.2 = ((s8[14155776]{0:T(1024)(128)(4,1)}), s8[4194304]{0:T(1024)(128)(4,1)S(1)}, s32[]{:S(2)}) async-start(s8[14155776]{0:T(1024)(128)(4,1)} %bitcast.92), calls=%async_computation.2 | async-start | bytes 8388608
  18.5 4.8 %collective-permute-start.5 = (bf16[48,1152]{1,0:T(8,128)(2,1)S(1)}, bf16[48,1152]{1,0:T(8,128)(2,1)S(1)}, u32[]{:S(2)}, u32[]{:S(2)}) collective-permute-start(bf16[48,1152]{1,0:T(8,128)(2,1)S(1)} %shard_map.105), channel_id=1, source_target_pairs={{0,1},{1,0},{2,3},{3,2},{4,5},{5,4},{6,7},{7,6},{8,9},{9,8},{10,11... | collective-permute-start | bytes 331784 | tf_op jit(solution)/shard_map/ppermute | solution.py:19
  20.3 6.4 %collective-permute-start.8 = (bf16[48,1152]{1,0:T(8,128)(2,1)S(1)}, bf16[48,1152]{1,0:T(8,128)(2,1)S(1)}, u32[]{:S(2)}, u32[]{:S(2)}) collective-permute-start(bf16[48,1152]{1,0:T(8,128)(2,1)S(1)} %shard_map.106), channel_id=1, source_target_pairs={{0,2},{1,3},{2,0},{3,1},{4,6},{5,7},{6,4},{7,5},{8,10},{9,11},{10,... | collective-permute-start | bytes 331784 | tf_op jit(solution)/shard_map/ppermute | solution.py:19
  24.5 5.5 %collective-permute-start.10 = (bf16[2,96,576]{2,1,0:T(8,128)(2,1)S(1)}, bf16[2,96,576]{2,1,0:T(8,128)(2,1)S(1)}, u32[]{:S(2)}, u32[]{:S(2)}) collective-permute-start(bf16[2,96,576]{2,1,0:T(8,128)(2,1)S(1)} %pad_maximum_fusion.1), channel_id=1, source_target_pairs={{0,16},{16,0},{1,17},{17,1},{2,18},{18,2},{3,19},{19,3},{4,20},{20... | collective-permute-start | bytes 663560 | tf_op jit(solution)/shard_map/ppermute | solution.py:19
  26.1 4.4 %collective-permute-start.6 = (f32[96,2048]{1,0:T(8,128)S(1)}, f32[96,2048]{1,0:T(8,128)S(1)}, u32[]{:S(2)}, u32[]{:S(2)}) collective-permute-start(f32[96,2048]{1,0:T(8,128)S(1)} %fusion.14), channel_id=1, source_target_pairs={{0,16},{16,0},{1,17},{17,1},{2,18},{18,2},{3,19},{19,3},{4,20},{20... | collective-permute-start | bytes 2359304 | tf_op jit(solution)/shard_map/ppermute | solution.py:19
  27.8 2.3 %collective-permute-start.18 = (bf16[2,96,576]{2,1,0:T(8,128)(2,1)S(1)}, bf16[2,96,576]{2,1,0:T(8,128)(2,1)S(1)}, u32[]{:S(2)}, u32[]{:S(2)}) collective-permute-start(bf16[2,96,576]{2,1,0:T(8,128)(2,1)S(1)} %pad_maximum_fusion.2), channel_id=1, source_target_pairs={{0,16},{16,0},{1,17},{17,1},{2,18},{18,2},{3,19},{19,3},{4,20},{20... | collective-permute-start | bytes 663560 | tf_op jit(solution)/shard_map/ppermute | solution.py:19
  29.4 3.8 %collective-permute-start.9 = (f32[96,2048]{1,0:T(8,128)S(1)}, f32[96,2048]{1,0:T(8,128)S(1)}, u32[]{:S(2)}, u32[]{:S(2)}) collective-permute-start(f32[96,2048]{1,0:T(8,128)S(1)} %fusion.12), channel_id=1, source_target_pairs={{0,16},{16,0},{1,17},{17,1},{2,18},{18,2},{3,19},{19,3},{4,20},{20... | collective-permute-start | bytes 2359304 | tf_op jit(solution)/shard_map/ppermute | solution.py:19
  31.7 5.6 %collective-permute-start.11 = (bf16[48,1152]{1,0:T(8,128)(2,1)S(1)}, bf16[48,1152]{1,0:T(8,128)(2,1)S(1)}, u32[]{:S(2)}, u32[]{:S(2)}) collective-permute-start(bf16[48,1152]{1,0:T(8,128)(2,1)S(1)} %slice.270), channel_id=1, source_target_pairs={{0,1},{1,0},{2,3},{3,2},{4,5},{5,4},{6,7},{7,6},{8,9},{9,8},{10,11... | collective-permute-start | bytes 331784 | tf_op jit(solution)/shard_map/ppermute | solution.py:19
  35.6 5.4 %collective-permute-start.19 = (bf16[48,1152]{1,0:T(8,128)(2,1)S(1)}, bf16[48,1152]{1,0:T(8,128)(2,1)S(1)}, u32[]{:S(2)}, u32[]{:S(2)}) collective-permute-start(bf16[48,1152]{1,0:T(8,128)(2,1)S(1)} %pad_maximum_fusion.9), channel_id=1, source_target_pairs={{0,2},{1,3},{2,0},{3,1},{4,6},{5,7},{6,4},{7,5},{8,10},{9,11},{10,... | collective-permute-start | bytes 331784 | tf_op jit(solution)/shard_map/ppermute | solution.py:19
  37.3 4.6 %collective-permute-start.12 = (bf16[24,1152]{1,0:T(8,128)(2,1)S(1)}, bf16[24,1152]{1,0:T(8,128)(2,1)S(1)}, u32[]{:S(2)}, u32[]{:S(2)}) collective-permute-start(bf16[24,1152]{1,0:T(8,128)(2,1)S(1)} %slice.272), channel_id=1, source_target_pairs={{0,2},{1,3},{2,0},{3,1},{4,6},{5,7},{6,4},{7,5},{8,10},{9,11},{10,... | collective-permute-start | bytes 165896 | tf_op jit(solution)/shard_map/ppermute | solution.py:19
  41.1 4.4 %collective-permute-start.20 = (bf16[24,1152]{1,0:T(8,128)(2,1)S(1)}, bf16[24,1152]{1,0:T(8,128)(2,1)S(1)}, u32[]{:S(2)}, u32[]{:S(2)}) collective-permute-start(bf16[24,1152]{1,0:T(8,128)(2,1)S(1)} %slice.271), channel_id=1, source_target_pairs={{0,1},{1,0},{2,3},{3,2},{4,5},{5,4},{6,7},{7,6},{8,9},{9,8},{10,11... | collective-permute-start | bytes 165896 | tf_op jit(solution)/shard_map/ppermute | solution.py:19
  41.9 6.1 %collective-permute-start.13 = (bf16[24,1152]{1,0:T(8,128)(2,1)S(1)}, bf16[24,1152]{1,0:T(8,128)(2,1)S(1)}, u32[]{:S(2)}, u32[]{:S(2)}) collective-permute-start(bf16[24,1152]{1,0:T(8,128)(2,1)S(1)} %fusion.106), channel_id=1, source_target_pairs={{0,8},{1,9},{2,10},{3,11},{4,12},{5,13},{6,14},{7,15},{8,0},{9,1},... | collective-permute-start | bytes 165896 | tf_op jit(solution)/shard_map/ppermute | solution.py:19
  42.0 7.1 %collective-permute-start.14 = (bf16[24,1152]{1,0:T(8,128)(2,1)S(1)}, bf16[24,1152]{1,0:T(8,128)(2,1)S(1)}, u32[]{:S(2)}, u32[]{:S(2)}) collective-permute-start(bf16[24,1152]{1,0:T(8,128)(2,1)S(1)} %fusion.106), channel_id=1, source_target_pairs={{0,12},{1,13},{2,14},{3,15},{4,8},{5,9},{6,10},{7,11},{8,4},{9,5},... | collective-permute-start | bytes 165896 | tf_op jit(solution)/shard_map/ppermute | solution.py:19
  43.0 6.1 %collective-permute-start.15 = (bf16[24,1152]{1,0:T(8,128)(2,1)S(1)}, bf16[24,1152]{1,0:T(8,128)(2,1)S(1)}, u32[]{:S(2)}, u32[]{:S(2)}) collective-permute-start(bf16[24,1152]{1,0:T(8,128)(2,1)S(1)} %fusion.106), channel_id=1, source_target_pairs={{0,4},{1,5},{2,6},{3,7},{4,0},{5,1},{6,2},{7,3},{8,12},{9,13},{10,... | collective-permute-start | bytes 165896 | tf_op jit(solution)/shard_map/ppermute | solution.py:19
  45.5 5.2 %collective-permute-start.21 = (bf16[24,1152]{1,0:T(8,128)(2,1)S(1)}, bf16[24,1152]{1,0:T(8,128)(2,1)S(1)}, u32[]{:S(2)}, u32[]{:S(2)}) collective-permute-start(bf16[24,1152]{1,0:T(8,128)(2,1)S(1)} %fusion.107), channel_id=1, source_target_pairs={{0,4},{1,5},{2,6},{3,7},{4,0},{5,1},{6,2},{7,3},{8,12},{9,13},{10,... | collective-permute-start | bytes 165896 | tf_op jit(solution)/shard_map/ppermute | solution.py:19
  45.6 6.1 %collective-permute-start.22 = (bf16[24,1152]{1,0:T(8,128)(2,1)S(1)}, bf16[24,1152]{1,0:T(8,128)(2,1)S(1)}, u32[]{:S(2)}, u32[]{:S(2)}) collective-permute-start(bf16[24,1152]{1,0:T(8,128)(2,1)S(1)} %fusion.107), channel_id=1, source_target_pairs={{0,12},{1,13},{2,14},{3,15},{4,8},{5,9},{6,10},{7,11},{8,4},{9,5},... | collective-permute-start | bytes 165896 | tf_op jit(solution)/shard_map/ppermute | solution.py:19
  48.0 5.2 %collective-permute-start.23 = (bf16[24,1152]{1,0:T(8,128)(2,1)S(1)}, bf16[24,1152]{1,0:T(8,128)(2,1)S(1)}, u32[]{:S(2)}, u32[]{:S(2)}) collective-permute-start(bf16[24,1152]{1,0:T(8,128)(2,1)S(1)} %fusion.107), channel_id=1, source_target_pairs={{0,8},{1,9},{2,10},{3,11},{4,12},{5,13},{6,14},{7,15},{8,0},{9,1},... | collective-permute-start | bytes 165896 | tf_op jit(solution)/shard_map/ppermute | solution.py:19
  49.1 5.3 %collective-permute-start.16 = (bf16[24,1152]{1,0:T(8,128)(2,1)S(1)}, bf16[24,1152]{1,0:T(8,128)(2,1)S(1)}, u32[]{:S(2)}, u32[]{:S(2)}) collective-permute-start(bf16[24,1152]{1,0:T(8,128)(2,1)S(1)} %shard_map.107), channel_id=1, source_target_pairs={{0,2},{1,3},{2,0},{3,1},{4,6},{5,7},{6,4},{7,5},{8,10},{9,11},{10,... | collective-permute-start | bytes 165896 | tf_op jit(solution)/shard_map/ppermute | solution.py:19
  53.2 4.2 %collective-permute-start.24 = (bf16[24,1152]{1,0:T(8,128)(2,1)S(1)}, bf16[24,1152]{1,0:T(8,128)(2,1)S(1)}, u32[]{:S(2)}, u32[]{:S(2)}) collective-permute-start(bf16[24,1152]{1,0:T(8,128)(2,1)S(1)} %shard_map.108), channel_id=1, source_target_pairs={{0,1},{1,0},{2,3},{3,2},{4,5},{5,4},{6,7},{7,6},{8,9},{9,8},{10,11... | collective-permute-start | bytes 165896 | tf_op jit(solution)/shard_map/ppermute | solution.py:19
  54.4 4.8 %collective-permute-start.17 = (bf16[48,1152]{1,0:T(8,128)(2,1)S(1)}, bf16[48,1152]{1,0:T(8,128)(2,1)S(1)}, u32[]{:S(2)}, u32[]{:S(2)}) collective-permute-start(bf16[48,1152]{1,0:T(8,128)(2,1)S(1)} %pad_maximum_fusion.8), channel_id=1, source_target_pairs={{0,1},{1,0},{2,3},{3,2},{4,5},{5,4},{6,7},{7,6},{8,9},{9,8},{10,11... | collective-permute-start | bytes 331784 | tf_op jit(solution)/shard_map/ppermute | solution.py:19
  57.4 4.8 %collective-permute-start.25 = (bf16[48,1152]{1,0:T(8,128)(2,1)S(1)}, bf16[48,1152]{1,0:T(8,128)(2,1)S(1)}, u32[]{:S(2)}, u32[]{:S(2)}) collective-permute-start(bf16[48,1152]{1,0:T(8,128)(2,1)S(1)} %pad_maximum_fusion.10), channel_id=1, source_target_pairs={{0,2},{1,3},{2,0},{3,1},{4,6},{5,7},{6,4},{7,5},{8,10},{9,11},{10,... | collective-permute-start | bytes 331784 | tf_op jit(solution)/shard_map/ppermute | solution.py:19
  65.5 6.9 %collective-permute-start.26 = (bf16[2,96,2048]{2,1,0:T(8,128)(2,1)S(1)}, bf16[2,96,2048]{2,1,0:T(8,128)(2,1)S(1)}, u32[]{:S(2)}, u32[]{:S(2)}) collective-permute-start(bf16[2,96,2048]{2,1,0:T(8,128)(2,1)S(1)} %pad_maximum_fusion.own_ref), channel_id=1, source_target_pairs={{0,16},{16,0},{1,17},{17,1},{2,18},{18,2},{3,19},{19,3},{4,20},{20... | collective-permute-start | bytes 2359304 | tf_op jit(solution)/shard_map/ppermute | solution.py:19
  (5 other events, 18.1 us)
